TPU v7x, 128 devices: a whole 4x4x4 slice. The times are simulated.
128 devices in a mesh: dp: 4 (over x), seq: 32 (over y, z, core).
Axes of the slice: x: 4, y: 4, z: 4, core: 2. Of those that a mesh axis runs over, the one named last changes fastest.
Arguments:
- queries: bfloat16 [4, 8192, 2048], P('dp', 'seq'), may hold values from -6 to 6
- key_states: bfloat16 [4, 8192, 2048], P('dp', 'seq'), may hold values from -6 to 6
- value_states: bfloat16 [4, 8192, 2048], P('dp', 'seq'), may hold values from -6 to 6
- out_weight: bfloat16 [2048, 2048], replicated, may hold values from -0.125 to 0.125
- cotangent: bfloat16 [4, 8192, 2048], P('dp', 'seq'), may hold values from -6 to 6
- block_offsets: int32 [4, 64, 4], P('dp', 'seq'), may hold values from 1 to 32, as said below
Outputs:
- grad_queries: bfloat16 [4, 8192, 2048], P('dp', 'seq')
- grad_keys: bfloat16 [4, 8192, 2048], P('dp', 'seq')
- grad_values: bfloat16 [4, 8192, 2048], P('dp', 'seq')
- grad_out_weight: float32 [2048, 2048], P(('dp', 'seq'))
Inputs may be any that keep to these rules, and one draw needn't show every extreme that they name: `block_offsets`: each query block lists 4 distinct offsets, each a power of two below 64; query block b always lists 2 ** (b mod log2(64)). Listed blocks before the document's start are skipped.
All inputs are finite; a program needn't handle non-finite values.
Results may differ from a plain program's by a relative error of at most 0.029.
Values may be sent and summed in bfloat16 or wider, within the bound.
No kernel may reach another device: no remote copies, remote signals or barrier semaphores. Data moves between devices by JAX's collectives and lax.ppermute only.
A program may use at most 256 MiB of HBM per device.

v0:
```python
import jax
import jax.numpy as jnp
from jax import lax
from jax.sharding import PartitionSpec as P

HEADS = 16
HEAD = 128
BLK = 128
SLOTS = 4


masked_score = -1e30


def passed_along(block, axis, distance):
    devices = range(lax.axis_size(axis))
    route = [(i - distance, i) for i in devices if i - distance in devices]
    return lax.ppermute(block, axis, route)


def level_of(ratio):
    powers = 2 ** jnp.arange(1, 24, dtype=jnp.int32)
    return jnp.sum((ratio[..., None] >= powers).astype(jnp.int32), axis=-1)


def attention_grads(query_rows, key_pool, value_pool, grad_attn, offsets, device, blocks):
    score_scale = HEAD ** (-0.5)
    model_width = query_rows.shape[1]
    local_block = jnp.arange(blocks, dtype=jnp.int32)
    global_block = device * blocks + local_block
    usable = global_block[:, None] - offsets >= 0
    nearby = offsets < blocks
    inside = local_block[:, None] >= offsets
    slot_index = jnp.where(nearby, jnp.where(inside, 0, 1), 1 + level_of(offsets // blocks))
    block_index = jnp.where(
        nearby,
        jnp.where(inside, local_block[:, None] - offsets, local_block[:, None] - offsets + blocks),
        local_block[:, None],
    )
    pool_index = jnp.where(usable, slot_index * blocks + block_index, 0)
    all_keys = jnp.concatenate(
        [key_pool[:blocks][:, None], jnp.take(key_pool, pool_index, axis=0)], axis=1
    )
    all_values = jnp.concatenate(
        [value_pool[:blocks][:, None], jnp.take(value_pool, pool_index, axis=0)], axis=1
    )
    all_keys = all_keys.reshape(blocks, -1, HEADS, HEAD)
    all_values = all_values.reshape(blocks, -1, HEADS, HEAD)
    query_heads = query_rows.reshape(blocks, BLK, HEADS, HEAD)
    key_width = all_keys.shape[1]
    scores = (
        jnp.einsum("pqhe,pkhe->phqk", query_heads, all_keys, preferred_element_type=jnp.float32)
        * score_scale
    )
    column = jnp.arange(key_width, dtype=jnp.int32)
    query_row = jnp.arange(BLK, dtype=jnp.int32)
    column_slot = column // BLK
    column_row = column % BLK
    slot_live = jnp.concatenate([jnp.ones((blocks, 1), dtype=bool), usable], axis=1)
    column_live = slot_live[:, column_slot]
    causal = (column_slot[None, :] > 0) | (column_row[None, :] <= query_row[:, None])
    allowed = column_live[:, None, None, :] & causal[None, None, :, :]
    scores = jnp.where(allowed, scores, masked_score)
    row_peak = jnp.max(scores, axis=-1, keepdims=True)
    weights = jnp.where(allowed, jnp.exp(scores - row_peak), 0.0)
    attn_prob = weights / jnp.sum(weights, axis=-1, keepdims=True)
    prob_low = attn_prob.astype(jnp.bfloat16)
    attended = jnp.einsum(
        "phqk,pkhe->pqhe", prob_low, all_values, preferred_element_type=jnp.float32
    )
    attn_out = attended.astype(jnp.bfloat16)
    grad_heads = grad_attn.reshape(blocks, BLK, HEADS, HEAD)
    row_dot = jnp.sum(grad_heads.astype(jnp.float32) * attn_out.astype(jnp.float32), axis=-1)
    grad_prob = jnp.einsum(
        "pqhe,pkhe->phqk", grad_heads, all_values, preferred_element_type=jnp.float32
    )
    grad_score = (
        attn_prob * (grad_prob - jnp.transpose(row_dot, (0, 2, 1))[..., None]) * score_scale
    ).astype(jnp.bfloat16)
    grad_query = jnp.einsum(
        "phqk,pkhe->pqhe", grad_score, all_keys, preferred_element_type=jnp.float32
    )
    key_terms = jnp.einsum(
        "phqk,pqhe->pkhe", grad_score, query_heads, preferred_element_type=jnp.float32
    ).reshape(blocks, 1 + SLOTS, BLK, model_width)
    value_terms = jnp.einsum(
        "phqk,pqhe->pkhe", prob_low, grad_heads, preferred_element_type=jnp.float32
    ).reshape(blocks, 1 + SLOTS, BLK, model_width)
    pool_size = key_pool.shape[0]
    key_acc = (
        jnp.zeros((pool_size, BLK, model_width), jnp.float32)
        .at[local_block]
        .add(key_terms[:, 0])
        .at[pool_index]
        .add(key_terms[:, 1:])
    )
    value_acc = (
        jnp.zeros((pool_size, BLK, model_width), jnp.float32)
        .at[local_block]
        .add(value_terms[:, 0])
        .at[pool_index]
        .add(value_terms[:, 1:])
    )
    return (
        attn_out.reshape(-1, model_width),
        grad_query.reshape(-1, model_width),
        key_acc,
        value_acc,
    )


def local(queries, key_states, value_states, out_weight, cotangent, block_offsets):
    query_rows = queries[0]
    upstream = cotangent[0]
    tokens = query_rows.shape[0]
    model_width = query_rows.shape[1]
    blocks = tokens // BLK
    hop_count = lax.axis_size("seq").bit_length() - 1
    device = lax.axis_index("seq")
    grad_attn = jnp.dot(upstream, out_weight.T, preferred_element_type=jnp.float32).astype(
        jnp.bfloat16
    )
    own_keys = key_states[0].reshape(blocks, BLK, model_width)
    own_values = value_states[0].reshape(blocks, BLK, model_width)
    key_parts = [own_keys]
    value_parts = [own_values]
    for hop_level in range(hop_count):
        fetched = passed_along((own_keys, own_values), "seq", 2**hop_level)
        key_parts.append(fetched[0])
        value_parts.append(fetched[1])
    key_pool = jnp.concatenate(key_parts, axis=0)
    value_pool = jnp.concatenate(value_parts, axis=0)
    attn_out, grad_query, key_acc, value_acc = attention_grads(
        query_rows, key_pool, value_pool, grad_attn, block_offsets[0], device, blocks
    )
    key_total = key_acc[:blocks]
    value_total = value_acc[:blocks]
    for hop_level in range(hop_count):
        lower = (1 + hop_level) * blocks
        outgoing = (
            key_acc[lower : lower + blocks].astype(jnp.bfloat16),
            value_acc[lower : lower + blocks].astype(jnp.bfloat16),
        )
        incoming = passed_along((outgoing[0], outgoing[1]), "seq", -(2**hop_level))
        key_total = key_total + incoming[0].astype(jnp.float32)
        value_total = value_total + incoming[1].astype(jnp.float32)
    weight_grad = lax.psum_scatter(
        lax.dot_general(
            attn_out, upstream, (((0,), (0,)), ((), ())), preferred_element_type=jnp.float32
        ),
        ("dp", "seq"),
        scatter_dimension=0,
        tiled=True,
    )
    return (
        grad_query.astype(jnp.bfloat16)[None],
        key_total.reshape(tokens, model_width).astype(jnp.bfloat16)[None],
        value_total.reshape(tokens, model_width).astype(jnp.bfloat16)[None],
        weight_grad,
    )


def solution(mesh):
    in_specs = (
        P("dp", "seq", None),
        P("dp", "seq", None),
        P("dp", "seq", None),
        P(),
        P("dp", "seq", None),
        P("dp", "seq", None),
    )
    out_specs = (
        P("dp", "seq", None),
        P("dp", "seq", None),
        P("dp", "seq", None),
        P(("dp", "seq"), None),
    )
    return jax.shard_map(local, mesh=mesh, in_specs=in_specs, out_specs=out_specs, check_vma=False)
```

profile of v0, /device:TPU:0, one launch (start us, length us, event | category | flops | bytes accessed | tf_op | source)
XLA Modules:
  0.0 1002.1 jit_solution(1021571506420258444)
XLA Ops:
  9.6 4.5 collective-permute-start.6
  14.2 5.5 collective-permute-start.7
  19.7 3.5 collective-permute-start.8
  23.2 4.8 collective-permute-start.9
  31.5 5.8 fusion.18
  53.8 5.8 collective-permute-done.7
  59.6 9.7 collective-permute-start.2
  71.7 7.0 collective-permute-start.3
  81.0 4.8 collective-permute-start.4
  88.2 5.5 gather_fusion.2
  98.3 6.3 collective-permute-done.2
  113.8 5.6 gather_fusion.1
  119.4 4.3 broadcast_select_fusion
  123.8 4.5 pad_maximum_fusion
  128.3 4.1 copy.115
  132.4 8.9 copy.99
  141.3 6.6 copy.118
  147.9 9.0 copy.96
  157.0 8.2 fusion.25
  165.2 16.0 %fusion.49 = (f32[2,16,128]{2,1,0:T(8,128)S(1)}, f32[2,16,128,640]{2,3,1,0:T(8,128)}) fusion(f32[2,16,640,128]{3,2,1,0:T(8,128)} %fusion.25, pred[2,128,640]{1,2,0:T(8,128)(4,1)S(1)} %broadcast_and_fusion), kind=kOutput, calls=%fused_computation.124 | output fusion | flops 18350720 | bytes 21151744 | tf_op jit(solution)/shard_map/sub | solution.py:65
  181.2 5.3 fusion.5
  191.8 9.4 fusion.19
  202.1 10.6 %multiply_convert_fusion = bf16[2,16,128,640]{2,3,1,0:T(8,128)(2,1)} fusion(f32[2,16,128]{2,1,0:T(8,128)S(1)} %bitcast.139, f32[2,16,128,640]{2,3,1,0:T(8,128)} %get-tuple-element.21, f32[2,16,128]{2,1,0:T(8,128)S(1)} %get-tuple-element.20, bf16[2,128,16,128]{1,3,2,0:T(8,128)(2,1)S(1)} %copy.95, bf16[2,640,16,128]{1,3,2,0:T(8,128)(2,1)} %copy.96), kind=kOutput, calls=%fused_computation.9 | convolution fusion | flops 684195840 | bytes 22052864 | tf_op jit(solution)/shard_map/pqhe,pkhe->phqk/dot_general | solution.py:74
  212.7 3.8 convolution_bitcast_fusion.1
  216.5 10.0 %copy.103 = f32[2,640,16,128]{3,2,1,0:T(8,128)} copy(f32[2,640,16,128]{3,1,2,0:T(8,128)S(1)} %convolution_bitcast_fusion.1) | data formatting | bytes 20971520 | tf_op jit(solution)/shard_map/phqk,pqhe->pkhe/transpose | solution.py:83
  226.6 11.5 %reshape.369 = f32[2,5,128,2048]{3,2,1,0:T(8,128)} reshape(f32[2,640,16,128]{3,2,1,0:T(8,128)} %copy.103) | data formatting | bytes 20971520 | tf_op jit(solution)/shard_map/reshape | solution.py:85
  238.1 7.9 slice.81
  247.7 6.1 broadcast.485.clone
  253.8 4.1 scatter_fusion
  257.9 16.1 %scatter_fusion.1 = f32[12,128,2048]{2,1,0:T(8,128)} fusion(f32[12,128,2048]{2,1,0:T(8,128)} %scatter_fusion, s32[8]{0:T(128)S(1)} %reshape.406, f32[8,128,2048]{2,1,0:T(8,128)} %bitcast.115), kind=kCustom, calls=%fused_computation.4 | custom fusion | flops 2097152 | bytes 25165856 | tf_op jit(solution)/shard_map/scatter-add | solution.py:95
  273.9 8.4 convert.14
  282.3 5.1 fusion.48
  294.1 5.8 convolution_bitcast_fusion
  299.9 11.3 %copy.108 = f32[2,640,16,128]{3,2,1,0:T(8,128)} copy(f32[2,640,16,128]{1,3,2,0:T(8,128)} %convolution_bitcast_fusion) | data formatting | bytes 20971520 | tf_op jit(solution)/shard_map/phqk,pqhe->pkhe/transpose | solution.py:86
  311.2 11.4 %reshape.370 = f32[2,5,128,2048]{3,2,1,0:T(8,128)} reshape(f32[2,640,16,128]{3,2,1,0:T(8,128)} %copy.108) | data formatting | bytes 20971520 | tf_op jit(solution)/shard_map/reshape | solution.py:88
  322.7 7.7 slice.89
  332.1 6.1 broadcast.485.clone.1
  338.2 4.1 scatter_fusion.2
  342.3 16.4 %scatter_fusion.3 = f32[12,128,2048]{2,1,0:T(8,128)} fusion(f32[12,128,2048]{2,1,0:T(8,128)} %scatter_fusion.2, s32[8]{0:T(128)S(1)} %reshape.406, f32[8,128,2048]{2,1,0:T(8,128)} %bitcast.114), kind=kCustom, calls=%fused_computation.6 | custom fusion | flops 2097152 | bytes 25165856 | tf_op jit(solution)/shard_map/scatter-add | solution.py:102
  358.7 8.5 convert.15
  367.1 4.9 fusion.47
  377.2 4.9 collective-permute-done.12
  386.0 5.1 fusion.17
  394.3 5.3 fusion.15
  399.6 132.5 %collective-permute-done.19 = bf16[2,128,2048]{2,1,0:T(8,128)(2,1)} collective-permute-done((bf16[2,128,2048]{2,1,0:T(8,128)(2,1)}, bf16[2,128,2048]{2,1,0:T(8,128)(2,1)}, u32[]{:S(2)}, u32[]{:S(2)}) %collective-permute-start.19) | collective-permute-done | bytes 1048608 | tf_op jit(solution)/shard_map/ppermute | solution.py:18
  532.1 3.4 collective-permute-done.18
  535.5 5.2 fusion.10
  540.7 454.3 %reduce-scatter.2.cloned.1.call-done = f32[16,2048]{1,0:T(8,128)} async-done(((f32[2048,2048]{1,0:T(8,128)}), f32[16,2048]{1,0:T(8,128)}) %reduce-scatter.2.cloned.1.call-update) | async-done | bytes 131088 | tf_op jit(solution)/shard_map/reduce_scatter | solution.py:147
  (109 shorter events, 71.6 us)
Async XLA Ops:
  7.2 24.3 %copy-start = (bf16[1,256,2048]{2,1,0:T(8,128)(2,1)S(1)}, bf16[1,256,2048]{2,1,0:T(8,128)(2,1)}, u32[]{:S(2)}) copy-start(bf16[1,256,2048]{2,1,0:T(8,128)(2,1)} %param.12) | copy-start | bytes 3145732
  7.2 987.9 %reduce-scatter.2.cloned.1.call-start = ((), (), s32[]{:S(2)}) async-start(), calls=%async_computation.1 | async-start | bytes 16908288 | tf_op jit(solution)/shard_map/reduce_scatter | solution.py:147
  7.2 37.2 %collective-permute-start.5 = (bf16[2,128,2048]{2,1,0:T(8,128)(2,1)}, bf16[2,128,2048]{2,1,0:T(8,128)(2,1)}, u32[]{:S(2)}, u32[]{:S(2)}) collective-permute-start(bf16[2,128,2048]{2,1,0:T(8,128)(2,1)} %bitcast.127), channel_id=1, source_target_pairs={{0,1},{1,2},{2,3},{3,4},{4,5},{5,6},{6,7},{7,8},{8,9},{9,10},{10,1... | collective-permute-start | bytes 3145736 | tf_op jit(solution)/shard_map/ppermute | solution.py:18
  9.6 39.5 %collective-permute-start.6 = (bf16[2,128,2048]{2,1,0:T(8,128)(2,1)}, bf16[2,128,2048]{2,1,0:T(8,128)(2,1)}, u32[]{:S(2)}, u32[]{:S(2)}) collective-permute-start(bf16[2,128,2048]{2,1,0:T(8,128)(2,1)} %bitcast.128), channel_id=1, source_target_pairs={{0,2},{1,3},{2,4},{3,5},{4,6},{5,7},{6,8},{7,9},{8,10},{9,11},{10,... | collective-permute-start | bytes 3145736 | tf_op jit(solution)/shard_map/ppermute | solution.py:18
  14.2 45.5 %collective-permute-start.7 = (bf16[2,128,2048]{2,1,0:T(8,128)(2,1)}, bf16[2,128,2048]{2,1,0:T(8,128)(2,1)}, u32[]{:S(2)}, u32[]{:S(2)}) collective-permute-start(bf16[2,128,2048]{2,1,0:T(8,128)(2,1)} %bitcast.129), channel_id=1, source_target_pairs={{0,4},{1,5},{2,6},{3,7},{4,8},{5,9},{6,10},{7,11},{8,12},{9,13},{1... | collective-permute-start | bytes 3145736 | tf_op jit(solution)/shard_map/ppermute | solution.py:18
  19.7 52.0 %collective-permute-start.8 = (bf16[2,128,2048]{2,1,0:T(8,128)(2,1)}, bf16[2,128,2048]{2,1,0:T(8,128)(2,1)}, u32[]{:S(2)}, u32[]{:S(2)}) collective-permute-start(bf16[2,128,2048]{2,1,0:T(8,128)(2,1)} %bitcast.130), channel_id=1, source_target_pairs={{0,8},{1,9},{2,10},{3,11},{4,12},{5,13},{6,14},{7,15},{8,16},{9,17... | collective-permute-start | bytes 3145736 | tf_op jit(solution)/shard_map/ppermute | solution.py:18
  23.2 57.8 %collective-permute-start.9 = (bf16[2,128,2048]{2,1,0:T(8,128)(2,1)}, bf16[2,128,2048]{2,1,0:T(8,128)(2,1)}, u32[]{:S(2)}, u32[]{:S(2)}) collective-permute-start(bf16[2,128,2048]{2,1,0:T(8,128)(2,1)} %bitcast.131), channel_id=1, source_target_pairs={{0,16},{1,17},{2,18},{3,19},{4,20},{5,21},{6,22},{7,23},{8,24},{9,... | collective-permute-start | bytes 3145736 | tf_op jit(solution)/shard_map/ppermute | solution.py:18
  31.5 5.9 copy-start.5
  42.6 159.4 %copy-start.3 = (bf16[2,128,16,128]{1,3,2,0:T(8,128)(2,1)}, bf16[2,128,16,128]{1,3,2,0:T(8,128)(2,1)S(1)}, u32[]{:S(2)}) copy-start(bf16[2,128,16,128]{1,3,2,0:T(8,128)(2,1)S(1)} %copy.95) | copy-start | bytes 3145732
  44.5 49.2 %collective-permute-start = (bf16[2,128,2048]{2,1,0:T(8,128)(2,1)}, bf16[2,128,2048]{2,1,0:T(8,128)(2,1)}, u32[]{:S(2)}, u32[]{:S(2)}) collective-permute-start(bf16[2,128,2048]{2,1,0:T(8,128)(2,1)} %bitcast.3), channel_id=1, source_target_pairs={{0,1},{1,2},{2,3},{3,4},{4,5},{5,6},{6,7},{7,8},{8,9},{9,10},{10,1... | collective-permute-start | bytes 3145736 | tf_op jit(solution)/shard_map/ppermute | solution.py:18
  49.1 46.9 %collective-permute-start.1 = (bf16[2,128,2048]{2,1,0:T(8,128)(2,1)}, bf16[2,128,2048]{2,1,0:T(8,128)(2,1)}, u32[]{:S(2)}, u32[]{:S(2)}) collective-permute-start(bf16[2,128,2048]{2,1,0:T(8,128)(2,1)} %bitcast.3), channel_id=1, source_target_pairs={{0,2},{1,3},{2,4},{3,5},{4,6},{5,7},{6,8},{7,9},{8,10},{9,11},{10,... | collective-permute-start | bytes 3145736 | tf_op jit(solution)/shard_map/ppermute | solution.py:18
  59.6 44.9 %collective-permute-start.2 = (bf16[2,128,2048]{2,1,0:T(8,128)(2,1)}, bf16[2,128,2048]{2,1,0:T(8,128)(2,1)}, u32[]{:S(2)}, u32[]{:S(2)}) collective-permute-start(bf16[2,128,2048]{2,1,0:T(8,128)(2,1)} %bitcast.3), channel_id=1, source_target_pairs={{0,4},{1,5},{2,6},{3,7},{4,8},{5,9},{6,10},{7,11},{8,12},{9,13},{1... | collective-permute-start | bytes 3145736 | tf_op jit(solution)/shard_map/ppermute | solution.py:18
  71.7 35.2 %collective-permute-start.3 = (bf16[2,128,2048]{2,1,0:T(8,128)(2,1)}, bf16[2,128,2048]{2,1,0:T(8,128)(2,1)}, u32[]{:S(2)}, u32[]{:S(2)}) collective-permute-start(bf16[2,128,2048]{2,1,0:T(8,128)(2,1)} %bitcast.3), channel_id=1, source_target_pairs={{0,8},{1,9},{2,10},{3,11},{4,12},{5,13},{6,14},{7,15},{8,16},{9,17... | collective-permute-start | bytes 3145736 | tf_op jit(solution)/shard_map/ppermute | solution.py:18
  81.0 30.4 %collective-permute-start.4 = (bf16[2,128,2048]{2,1,0:T(8,128)(2,1)}, bf16[2,128,2048]{2,1,0:T(8,128)(2,1)}, u32[]{:S(2)}, u32[]{:S(2)}) collective-permute-start(bf16[2,128,2048]{2,1,0:T(8,128)(2,1)} %bitcast.3), channel_id=1, source_target_pairs={{0,16},{1,17},{2,18},{3,19},{4,20},{5,21},{6,22},{7,23},{8,24},{9,... | collective-permute-start | bytes 3145736 | tf_op jit(solution)/shard_map/ppermute | solution.py:18
  119.4 4.4 copy-start.6
  156.9 29.5 %slice-start.4 = ((s8[5242880]{0:T(1024)(128)(4,1)}), s8[4194304]{0:T(1024)(128)(4,1)S(1)}, s32[]{:S(2)}) async-start(s8[5242880]{0:T(1024)(128)(4,1)} %bitcast.118), calls=%async_computation.6 | async-start | bytes 8388608
  165.2 21.3 %slice-start.5 = ((s8[5242880]{0:T(1024)(128)(4,1)}), s8[1048576]{0:T(1024)(128)(4,1)S(1)}, s32[]{:S(2)}) async-start(s8[5242880]{0:T(1024)(128)(4,1)} %bitcast.118), calls=%async_computation.7 | async-start | bytes 2097152
  186.5 2.7 copy-start.2
  201.2 0.7 copy-start.7
  257.9 36.2 %slice-start.2 = ((s8[5242880]{0:T(1024)(128)(4,1)}), s8[1048576]{0:T(1024)(128)(4,1)S(1)}, s32[]{:S(2)}) async-start(s8[5242880]{0:T(1024)(128)(4,1)} %bitcast.112), calls=%async_computation.4 | async-start | bytes 2097152
  273.9 20.2 %slice-start.3 = ((s8[5242880]{0:T(1024)(128)(4,1)}), s8[4194304]{0:T(1024)(128)(4,1)S(1)}, s32[]{:S(2)}) async-start(s8[5242880]{0:T(1024)(128)(4,1)} %bitcast.112), calls=%async_computation.5 | async-start | bytes 8388608
  282.3 11.8 %copy-start.4 = (bf16[2,128,16,128]{1,3,2,0:T(8,128)(2,1)S(1)}, bf16[2,128,16,128]{1,3,2,0:T(8,128)(2,1)}, u32[]{:S(2)}) copy-start(bf16[2,128,16,128]{1,3,2,0:T(8,128)(2,1)} %copy-done.3) | copy-start | bytes 3145732
  287.4 85.3 %collective-permute-start.14 = (bf16[2,128,2048]{2,1,0:T(8,128)(2,1)}, bf16[2,128,2048]{2,1,0:T(8,128)(2,1)}, u32[]{:S(2)}, u32[]{:S(2)}) collective-permute-start(bf16[2,128,2048]{2,1,0:T(8,128)(2,1)} %get-tuple-element.13), channel_id=1, source_target_pairs={{16,0},{17,1},{18,2},{19,3},{20,4},{21,5},{22,6},{23,7},{24,8},{25... | collective-permute-start | bytes 3145736 | tf_op jit(solution)/shard_map/ppermute | solution.py:18
  288.7 87.3 %collective-permute-start.13 = (bf16[2,128,2048]{2,1,0:T(8,128)(2,1)}, bf16[2,128,2048]{2,1,0:T(8,128)(2,1)}, u32[]{:S(2)}, u32[]{:S(2)}) collective-permute-start(bf16[2,128,2048]{2,1,0:T(8,128)(2,1)} %get-tuple-element.14), channel_id=1, source_target_pairs={{8,0},{9,1},{10,2},{11,3},{12,4},{13,5},{14,6},{15,7},{16,8},{17,9... | collective-permute-start | bytes 3145736 | tf_op jit(solution)/shard_map/ppermute | solution.py:18
  290.0 92.1 %collective-permute-start.12 = (bf16[2,128,2048]{2,1,0:T(8,128)(2,1)}, bf16[2,128,2048]{2,1,0:T(8,128)(2,1)}, u32[]{:S(2)}, u32[]{:S(2)}) collective-permute-start(bf16[2,128,2048]{2,1,0:T(8,128)(2,1)} %get-tuple-element.15), channel_id=1, source_target_pairs={{4,0},{5,1},{6,2},{7,3},{8,4},{9,5},{10,6},{11,7},{12,8},{13,9},{1... | collective-permute-start | bytes 3145736 | tf_op jit(solution)/shard_map/ppermute | solution.py:18
  291.3 92.1 %collective-permute-start.11 = (bf16[2,128,2048]{2,1,0:T(8,128)(2,1)}, bf16[2,128,2048]{2,1,0:T(8,128)(2,1)}, u32[]{:S(2)}, u32[]{:S(2)}) collective-permute-start(bf16[2,128,2048]{2,1,0:T(8,128)(2,1)} %get-tuple-element.16), channel_id=1, source_target_pairs={{2,0},{3,1},{4,2},{5,3},{6,4},{7,5},{8,6},{9,7},{10,8},{11,9},{12,... | collective-permute-start | bytes 3145736 | tf_op jit(solution)/shard_map/ppermute | solution.py:18
  292.6 92.1 %collective-permute-start.10 = (bf16[2,128,2048]{2,1,0:T(8,128)(2,1)}, bf16[2,128,2048]{2,1,0:T(8,128)(2,1)}, u32[]{:S(2)}, u32[]{:S(2)}) collective-permute-start(bf16[2,128,2048]{2,1,0:T(8,128)(2,1)} %get-tuple-element.12), channel_id=1, source_target_pairs={{1,0},{2,1},{3,2},{4,3},{5,4},{6,5},{7,6},{8,7},{9,8},{10,9},{11,1... | collective-permute-start | bytes 3145736 | tf_op jit(solution)/shard_map/ppermute | solution.py:18
  342.3 43.7 %slice-start = ((s8[5242880]{0:T(1024)(128)(4,1)}), s8[1048576]{0:T(1024)(128)(4,1)S(1)}, s32[]{:S(2)}) async-start(s8[5242880]{0:T(1024)(128)(4,1)} %bitcast.110), calls=%async_computation.2 | async-start | bytes 2097152
  358.7 27.3 %slice-start.1 = ((s8[5242880]{0:T(1024)(128)(4,1)}), s8[4194304]{0:T(1024)(128)(4,1)S(1)}, s32[]{:S(2)}) async-start(s8[5242880]{0:T(1024)(128)(4,1)} %bitcast.110), calls=%async_computation.3 | async-start | bytes 8388608
  372.7 159.4 %collective-permute-start.19 = (bf16[2,128,2048]{2,1,0:T(8,128)(2,1)}, bf16[2,128,2048]{2,1,0:T(8,128)(2,1)}, u32[]{:S(2)}, u32[]{:S(2)}) collective-permute-start(bf16[2,128,2048]{2,1,0:T(8,128)(2,1)} %get-tuple-element.8), channel_id=1, source_target_pairs={{16,0},{17,1},{18,2},{19,3},{20,4},{21,5},{22,6},{23,7},{24,8},{25... | collective-permute-start | bytes 3145736 | tf_op jit(solution)/shard_map/ppermute | solution.py:18
  376.0 159.6 %collective-permute-start.18 = (bf16[2,128,2048]{2,1,0:T(8,128)(2,1)}, bf16[2,128,2048]{2,1,0:T(8,128)(2,1)}, u32[]{:S(2)}, u32[]{:S(2)}) collective-permute-start(bf16[2,128,2048]{2,1,0:T(8,128)(2,1)} %get-tuple-element.9), channel_id=1, source_target_pairs={{8,0},{9,1},{10,2},{11,3},{12,4},{13,5},{14,6},{15,7},{16,8},{17,9... | collective-permute-start | bytes 3145736 | tf_op jit(solution)/shard_map/ppermute | solution.py:18
  382.1 153.4 %collective-permute-start.17 = (bf16[2,128,2048]{2,1,0:T(8,128)(2,1)}, bf16[2,128,2048]{2,1,0:T(8,128)(2,1)}, u32[]{:S(2)}, u32[]{:S(2)}) collective-permute-start(bf16[2,128,2048]{2,1,0:T(8,128)(2,1)} %get-tuple-element.10), channel_id=1, source_target_pairs={{4,0},{5,1},{6,2},{7,3},{8,4},{9,5},{10,6},{11,7},{12,8},{13,9},{1... | collective-permute-start | bytes 3145736 | tf_op jit(solution)/shard_map/ppermute | solution.py:18
  383.4 152.1 %collective-permute-start.16 = (bf16[2,128,2048]{2,1,0:T(8,128)(2,1)}, bf16[2,128,2048]{2,1,0:T(8,128)(2,1)}, u32[]{:S(2)}, u32[]{:S(2)}) collective-permute-start(bf16[2,128,2048]{2,1,0:T(8,128)(2,1)} %get-tuple-element.11), channel_id=1, source_target_pairs={{2,0},{3,1},{4,2},{5,3},{6,4},{7,5},{8,6},{9,7},{10,8},{11,9},{12,... | collective-permute-start | bytes 3145736 | tf_op jit(solution)/shard_map/ppermute | solution.py:18
  384.7 150.8 %collective-permute-start.15 = (bf16[2,128,2048]{2,1,0:T(8,128)(2,1)}, bf16[2,128,2048]{2,1,0:T(8,128)(2,1)}, u32[]{:S(2)}, u32[]{:S(2)}) collective-permute-start(bf16[2,128,2048]{2,1,0:T(8,128)(2,1)} %get-tuple-element.7), channel_id=1, source_target_pairs={{1,0},{2,1},{3,2},{4,3},{5,4},{6,5},{7,6},{8,7},{9,8},{10,9},{11,1... | collective-permute-start | bytes 3145736 | tf_op jit(solution)/shard_map/ppermute | solution.py:18
  394.3 600.7 %copy-start.1 = (bf16[1,256,2048]{2,1,0:T(8,128)(2,1)S(1)}, bf16[1,256,2048]{2,1,0:T(8,128)(2,1)}, u32[]{:S(2)}) copy-start(bf16[1,256,2048]{2,1,0:T(8,128)(2,1)} %param.12) | copy-start | bytes 3145732
Sparse Core Ops, SparseCore 0:
  201.4 793.6 reduce-scatter.1
where the time goes:
time: 1010 us; the launch traced here: 1000 us
  waiting for transfers between devices  612 us (61%)
  local copies, waits for them, and re-layouts  165 us (16%)
  other arithmetic  98.9 us (10%)
  starting transfers between devices  60 us (6%)
  matrix products  51.4 us (5%)
  between operations  14.7 us (1%)
    reduce_scatter x1, waiting for transfers between devices, local(): lax.psum_scatter(lax.dot_general(attn_out, upstream, (((0,), (0,)), ((),...  454 us
    ppermute x20, waiting for transfers between devices, passed_along(): return lax.ppermute(block, axis, route)  158 us
    ppermute x20, starting transfers between devices, passed_along(): return lax.ppermute(block, axis, route)  59.9 us
    unnamed x42, local copies, waits for them, and re-layouts  35.5 us
    scatter-add x2, other arithmetic, attention_grads(): value_acc = jnp.zeros((pool_size, BLK, model_width), jnp.float32).at[loca...  20.5 us
  transfers between devices with their start and end apart: 21, of which 9 were waited for; matrix products, arithmetic and copies ran while one was open for 22% of the time, Pallas kernels for 0%

commit v1 on v0

v1 whole, which is shorter than its diff:
```python
import math

import jax
import jax.numpy as jnp
from jax import lax
from jax.experimental import pallas as pl
from jax.experimental.pallas import tpu as pltpu
from jax.sharding import PartitionSpec as P

HEADS = 16
HEAD = 128
BLK = 128
SLOTS = 4
D = HEADS * HEAD
TOK = 256
CHIPS = 16
BLOCKS = 64
RIDER = 3 * TOK
ROWS = 3 * TOK + 8
SCALE = HEAD ** (-0.5)
SCALE2 = SCALE * math.log2(math.e)
NEG = -1e30
bf16 = jnp.bfloat16
f32 = jnp.float32

SAME_CORE = [[2 * c + k for c in range(CHIPS)] for k in range(2)]
CORE_SWAP = [(i, i ^ 1) for i in range(2 * CHIPS)]

VMEM_LIMIT = 56 * 1024 * 1024


def dot(a, b, ca, cb):
    return lax.dot_general(a, b, (((ca,), (cb,)), ((), ())), preferred_element_type=f32)


def exchange(x):
    return lax.all_to_all(x, "seq", 0, 0, axis_index_groups=SAME_CORE, tiled=True)


def pack_body(offs, k_ref, v_ref, q_ref, x_ref, rider, sems):
    lane = lax.broadcasted_iota(jnp.int32, (8, 128), 1)
    val = jnp.zeros((8, 128), jnp.int32)
    for j in range(2 * SLOTS):
        val = jnp.where(lane == j, offs[j // SLOTS, j % SLOTS], val)
    rider[...] = val.astype(f32).astype(bf16)
    copies = []
    for h in range(HEADS):
        for t, ref in enumerate((k_ref, v_ref, q_ref)):
            copies.append(
                pltpu.make_async_copy(
                    ref.at[:, pl.ds(h * HEAD, HEAD)],
                    x_ref.at[h, pl.ds(t * TOK, TOK), :],
                    sems.at[4 * h + t],
                )
            )
        copies.append(
            pltpu.make_async_copy(rider, x_ref.at[h, pl.ds(RIDER, 8), :], sems.at[4 * h + 3])
        )
    for copy in copies:
        copy.start()
    for copy in copies:
        copy.wait()


def pack(offs, k, v, q):
    return pl.pallas_call(
        pack_body,
        out_shape=jax.ShapeDtypeStruct((HEADS, ROWS, HEAD), bf16),
        in_specs=[pl.BlockSpec(memory_space=pltpu.SMEM)] + [pl.BlockSpec(memory_space=pl.ANY)] * 3,
        out_specs=pl.BlockSpec(memory_space=pl.ANY),
        scratch_shapes=[pltpu.VMEM((8, 128), bf16), pltpu.SemaphoreType.DMA((4 * HEADS,))],
        name="pack",
    )(offs, k, v, q)


def unpack_body(r_ref, gk_ref, gv_ref, gq_ref, sems):
    copies = []
    for h in range(HEADS):
        for t, ref in enumerate((gk_ref, gv_ref, gq_ref)):
            copies.append(
                pltpu.make_async_copy(
                    r_ref.at[h, pl.ds(t * TOK, TOK), :],
                    ref.at[:, pl.ds(h * HEAD, HEAD)],
                    sems.at[3 * h + t],
                )
            )
    for copy in copies:
        copy.start()
    for copy in copies:
        copy.wait()


def unpack(r):
    out = jax.ShapeDtypeStruct((TOK, D), bf16)
    return pl.pallas_call(
        unpack_body,
        out_shape=(out, out, out),
        in_specs=[pl.BlockSpec(memory_space=pl.ANY)],
        out_specs=[pl.BlockSpec(memory_space=pl.ANY)] * 3,
        scratch_shapes=[pltpu.SemaphoreType.DMA((3 * HEADS,))],
        name="unpack",
    )(r)


def grad_attn_body(c_ref, w_ref, o_ref):
    g = dot(c_ref[...], w_ref[...], 1, 1).astype(bf16)
    for j in range(2):
        o_ref[j] = g[:, j * HEAD : (j + 1) * HEAD]


def grad_attn_by_head(cot, weight):
    return pl.pallas_call(
        grad_attn_body,
        out_shape=jax.ShapeDtypeStruct((HEADS, TOK, HEAD), bf16),
        grid=(HEADS // 2,),
        in_specs=[
            pl.BlockSpec((TOK, D), lambda i: (0, 0)),
            pl.BlockSpec((2 * HEAD, D), lambda i: (i, 0)),
        ],
        out_specs=pl.BlockSpec((2, TOK, HEAD), lambda i: (i, 0, 0)),
        compiler_params=pltpu.CompilerParams(vmem_limit_bytes=VMEM_LIMIT),
        name="grad_attn",
    )(cot, weight)


def load_pool(x_ref, y_ref, kv, qs, sems):
    return [
        pltpu.make_async_copy(x_ref.at[:, pl.ds(0, 2 * TOK), :], kv.at[pl.ds(0, CHIPS)], sems.at[0]),
        pltpu.make_async_copy(y_ref.at[:, pl.ds(0, 2 * TOK), :], kv.at[pl.ds(CHIPS, CHIPS)], sems.at[1]),
        pltpu.make_async_copy(x_ref.at[:, pl.ds(2 * TOK, TOK), :], qs, sems.at[2]),
    ]


def listed(table, c, i):
    places = [(c, i * BLK, None)]
    for s in range(SLOTS):
        code = table[2 * c + i, s]
        f = jnp.maximum(code, 0)
        bias = jnp.where(code >= 0, 0.0, -NEG).astype(f32)
        places.append((f // 2, pl.multiple_of((f % 2) * BLK, BLK), bias))
    return places


def causal():
    u = lax.broadcasted_iota(jnp.int32, (BLK, BLK), 0)
    t = lax.broadcasted_iota(jnp.int32, (BLK, BLK), 1)
    return u <= t


def forward_body(table, x_ref, y_ref, o_ref, lse_ref, kv, qs, sems):
    copies = load_pool(x_ref, y_ref, kv, qs, sems)
    for copy in copies:
        copy.start()
    for copy in copies:
        copy.wait()

    def block(c, i):
        places = listed(table, c, i)
        q = qs[c, pl.ds(i * BLK, BLK), :]
        raw = [dot(kv[p, pl.ds(r, BLK), :], q, 1, 1) for p, r, _ in places]
        raw[0] = jnp.where(causal(), raw[0], NEG)
        peak = jnp.max(raw[0], axis=0, keepdims=True)
        for (_, _, bias), s in zip(places[1:], raw[1:]):
            peak = jnp.maximum(peak, jnp.max(s, axis=0, keepdims=True) - bias)
        peak = peak * SCALE2
        weights = []
        total = None
        for (_, _, bias), s in zip(places, raw):
            w = jnp.exp2(s * SCALE2 - (peak if bias is None else peak + bias))
            part = jnp.sum(w, axis=0, keepdims=True)
            total = part if total is None else total + part
            weights.append(w)
        inverse = 1.0 / total
        out = None
        for (p, r, _), w in zip(places, weights):
            v = kv[p, pl.ds(TOK + r, BLK), :]
            part = dot(v, (w * inverse).astype(bf16), 0, 0)
            out = part if out is None else out + part
        return out.astype(bf16), peak + jnp.log2(total)

    def step(c, carry):
        lses = []
        for i in range(2):
            out, lse = block(c, i)
            for g in range(8):
                row = (g % 2) * 64 + (g // 2) * 16
                o_ref[c, row : row + 16, i * BLK : (i + 1) * BLK] = out[g * 16 : g * 16 + 16, :]
            lses.append(lse)
        row = lax.broadcasted_iota(jnp.int32, (8, 128), 0)
        lse_ref[c] = jnp.where(row == 0, lses[0], lses[1])
        return carry

    lax.fori_loop(0, CHIPS, step, 0)


def attention_forward(table, x, y):
    return pl.pallas_call(
        forward_body,
        out_shape=(
            jax.ShapeDtypeStruct((CHIPS, HEAD, TOK), bf16),
            jax.ShapeDtypeStruct((CHIPS, 8, 128), f32),
        ),
        in_specs=[pl.BlockSpec(memory_space=pltpu.SMEM)] + [pl.BlockSpec(memory_space=pl.ANY)] * 2,
        out_specs=[pl.BlockSpec(memory_space=pltpu.VMEM)] * 2,
        scratch_shapes=[
            pltpu.VMEM((2 * CHIPS, 2 * TOK, HEAD), bf16),
            pltpu.VMEM((CHIPS, TOK, HEAD), bf16),
            pltpu.SemaphoreType.DMA((3,)),
        ],
        compiler_params=pltpu.CompilerParams(vmem_limit_bytes=VMEM_LIMIT),
        name="attn_fwd",
    )(table, x, y)


def backward_body(table, x_ref, y_ref, g_ref, lse_ref, own_ref, other_ref, gq_ref, kv, qs, acc, sems):
    copies = load_pool(x_ref, y_ref, kv, qs, sems)
    for copy in copies:
        copy.start()

    def clear(j, carry):
        acc[j] = jnp.zeros((2 * TOK, HEAD), f32)
        return carry

    lax.fori_loop(0, 2 * CHIPS, clear, 0)
    for copy in copies:
        copy.wait()

    def block(c, i):
        places = listed(table, c, i)
        q = qs[c, pl.ds(i * BLK, BLK), :]
        g = g_ref[c, pl.ds(i * BLK, BLK), :]
        lse = lse_ref[c, i : i + 1, :]
        probs, grads = [], []
        row_dot = None
        for p, r, bias in places:
            s = dot(kv[p, pl.ds(r, BLK), :], q, 1, 1)
            prob = jnp.exp2(s * SCALE2 - (lse if bias is None else lse + bias))
            if bias is None:
                prob = jnp.where(causal(), prob, 0.0)
            grad = dot(kv[p, pl.ds(TOK + r, BLK), :], g, 1, 1)
            part = jnp.sum(prob * grad, axis=0, keepdims=True)
            row_dot = part if row_dot is None else row_dot + part
            probs.append(prob)
            grads.append(grad)
        gq = None
        for (p, r, _), prob, grad in zip(places, probs, grads):
            score = (prob * (grad - row_dot) * SCALE).astype(bf16)
            acc[p, pl.ds(r, BLK), :] += dot(score, q, 1, 0)
            acc[p, pl.ds(TOK + r, BLK), :] += dot(prob.astype(bf16), g, 1, 0)
            part = dot(score, kv[p, pl.ds(r, BLK), :], 0, 0)
            gq = part if gq is None else gq + part
        gq_ref[c, pl.ds(i * BLK, BLK), :] = gq.astype(bf16)

    def step(c, carry):
        for i in range(2):
            block(c, i)
        return carry

    lax.fori_loop(0, CHIPS, step, 0)

    def flush(j, carry):
        own_ref[j] = acc[j]
        other_ref[j] = acc[CHIPS + j].astype(bf16)
        return carry

    lax.fori_loop(0, CHIPS, flush, 0)


def attention_backward(table, x, y, g, lse):
    return pl.pallas_call(
        backward_body,
        out_shape=(
            jax.ShapeDtypeStruct((CHIPS, 2 * TOK, HEAD), f32),
            jax.ShapeDtypeStruct((CHIPS, 2 * TOK, HEAD), bf16),
            jax.ShapeDtypeStruct((CHIPS, TOK, HEAD), bf16),
        ),
        in_specs=[pl.BlockSpec(memory_space=pltpu.SMEM)]
        + [pl.BlockSpec(memory_space=pl.ANY)] * 2
        + [pl.BlockSpec(memory_space=pltpu.VMEM)] * 2,
        out_specs=[pl.BlockSpec(memory_space=pltpu.VMEM)] * 3,
        scratch_shapes=[
            pltpu.VMEM((2 * CHIPS, 2 * TOK, HEAD), bf16),
            pltpu.VMEM((CHIPS, TOK, HEAD), bf16),
            pltpu.VMEM((2 * CHIPS, 2 * TOK, HEAD), f32),
            pltpu.SemaphoreType.DMA((3,)),
        ],
        compiler_params=pltpu.CompilerParams(vmem_limit_bytes=VMEM_LIMIT),
        name="attn_bwd",
    )(table, x, y, g, lse)


def combine_body(own_ref, got_ref, gq_ref, o_ref):
    o_ref[:, 0 : 2 * TOK, :] = (own_ref[...] + got_ref[...].astype(f32)).astype(bf16)
    o_ref[:, 2 * TOK : 3 * TOK, :] = gq_ref[...]


def combine(own, got, gq):
    n = 4
    return pl.pallas_call(
        combine_body,
        out_shape=jax.ShapeDtypeStruct((CHIPS, 3 * TOK, HEAD), bf16),
        grid=(CHIPS // n,),
        in_specs=[
            pl.BlockSpec((n, 2 * TOK, HEAD), lambda i: (i, 0, 0)),
            pl.BlockSpec((n, 2 * TOK, HEAD), lambda i: (i, 0, 0)),
            pl.BlockSpec((n, TOK, HEAD), lambda i: (i, 0, 0)),
        ],
        out_specs=pl.BlockSpec((n, 3 * TOK, HEAD), lambda i: (i, 0, 0)),
        compiler_params=pltpu.CompilerParams(vmem_limit_bytes=VMEM_LIMIT),
        name="combine",
    )(own, got, gq)


def weight_body(core, oa_ref, ob_ref, ca_ref, cb_ref, w_ref):
    a = oa_ref[...].reshape(4 * 64, TOK)
    b = ob_ref[...].reshape(4 * 64, TOK)
    w_ref[...] = (dot(a, ca_ref[...], 1, 0) + dot(b, cb_ref[...], 1, 0)).astype(bf16)


def weight_partial(core, oa, ob, ca, cb):
    return pl.pallas_call(
        weight_body,
        out_shape=jax.ShapeDtypeStruct((HEADS * 64, D), bf16),
        grid_spec=pltpu.PrefetchScalarGridSpec(
            num_scalar_prefetch=1,
            grid=(HEADS // 4,),
            in_specs=[
                pl.BlockSpec((4, 64, TOK), lambda i, core: (i, core[0], 0)),
                pl.BlockSpec((4, 64, TOK), lambda i, core: (i, core[0], 0)),
                pl.BlockSpec((TOK, D), lambda i, core: (0, 0)),
                pl.BlockSpec((TOK, D), lambda i, core: (0, 0)),
            ],
            out_specs=pl.BlockSpec((4 * 64, D), lambda i, core: (i, 0)),
        ),
        compiler_params=pltpu.CompilerParams(vmem_limit_bytes=VMEM_LIMIT),
        name="weight_partial",
    )(core, oa, ob, ca, cb)


def block_table(rider, core):
    offsets = rider.reshape(CHIPS, 2, SLOTS).astype(jnp.int32)
    c = jnp.arange(CHIPS, dtype=jnp.int32)[:, None, None]
    i = jnp.arange(2, dtype=jnp.int32)[None, :, None]
    target = 4 * c + 2 * core + i - offsets
    side = ((target >> 1) & 1) ^ core
    place = ((side * CHIPS + (target >> 2)) << 1) + (target & 1)
    return jnp.where(target >= 0, place, -1).reshape(2 * CHIPS, SLOTS)


def local(queries, key_states, value_states, out_weight, cotangent, block_offsets):
    core = lax.axis_index("seq") % 2
    cot = cotangent[0]
    x = exchange(pack(block_offsets[0], key_states[0], value_states[0], queries[0]))
    g = exchange(grad_attn_by_head(cot, out_weight))
    cot_other = lax.ppermute(cot, "seq", CORE_SWAP)
    y = lax.ppermute(x, "seq", CORE_SWAP)
    table = block_table(x[:, RIDER, 0 : 2 * SLOTS], core)
    out, lse = attention_forward(table, x, y)
    out_home = exchange(out)
    out_other = lax.ppermute(out_home, "seq", CORE_SWAP)
    own, other, gq = attention_backward(table, x, y, g, lse)
    got = lax.ppermute(other, "seq", CORE_SWAP)
    home = exchange(combine(own, got, gq))
    partial = weight_partial(core.reshape(1), out_home, out_other, cot, cot_other)
    by_doc = lax.psum_scatter(partial, "dp", scatter_dimension=0, tiled=True)
    pieces = exchange(by_doc.reshape(CHIPS, 16, D))
    weight_grad = jnp.sum(pieces.astype(f32), axis=0)
    gk, gv, gq = unpack(home)
    return gq[None], gk[None], gv[None], weight_grad


def solution(mesh):
    in_specs = (
        P("dp", "seq", None),
        P("dp", "seq", None),
        P("dp", "seq", None),
        P(),
        P("dp", "seq", None),
        P("dp", "seq", None),
    )
    out_specs = (
        P("dp", "seq", None),
        P("dp", "seq", None),
        P("dp", "seq", None),
        P(("dp", "seq"), None),
    )
    return jax.shard_map(local, mesh=mesh, in_specs=in_specs, out_specs=out_specs, check_vma=False)
```

time: 1010 us -> 433 us (0.43)
  waiting for transfers between devices: 612 us -> 29.7 us
  Pallas kernels: 0 us -> 261 us
  local copies, waits for them, and re-layouts: 165 us -> 2.58 us
  blocking collectives: 0 us -> 115 us
  other arithmetic: 98.9 us -> 1.86 us
  starting transfers between devices: 60 us -> 7.67 us
  matrix products: 51.4 us -> 0 us
    reduce_scatter x1, waiting for transfers between devices: 454 us -> 0.01 us  [local(): by_doc = lax.psum_scatter(partial, 'dp', scatter_dimension=0, tiled=True)]
    pallas_call x0 -> x7, Pallas kernels: none -> 261 us  [the longest x1 97.7 us: pack(): pl.pallas_call(pack_body, out_shape=jax.ShapeDtypeStruct((HEADS, ROWS, HE...]
    ppermute x20 -> x4, waiting for transfers between devices: 158 us -> 11.6 us  [the longest x1 4.61 us: local(): y = lax.ppermute(x, 'seq', CORE_SWAP)]
    all_to_all x0 -> x3, blocking collectives: none -> 115 us  [exchange(): lax.all_to_all(x, 'seq', 0, 0, axis_index_groups=SAME_CORE, tiled=True)]
    ppermute x20 -> x4, starting transfers between devices: 59.9 us -> 0.3 us  [the longest x1 0.21 us: local(): cot_other = lax.ppermute(cot, 'seq', CORE_SWAP)]
    dot_general x8 -> x0, matrix products: 51.4 us -> none  [the longest x1 10.6 us: attention_grads(): jnp.einsum('pqhe,pkhe->phqk', grad_heads, all_values, preferred_element_t...]
    reshape x5 -> x0, local copies, waits for them, and re-layouts: 41.9 us -> none  [the longest x1 11.5 us: attention_grads(): key_terms = jnp.einsum('phqk,pqhe->pkhe', grad_score, query_heads, prefer...]
    scatter-add x4 -> x0, other arithmetic: 40.6 us -> none  [the longest x2 20.5 us: attention_grads(): value_acc = jnp.zeros((pool_size, BLK, model_width), jnp.float32).at[loca...]
  transfers between devices with their start and end apart: 21 -> 7, of which waited for: 9 -> 4; matrix products, arithmetic and copies ran while one was open for 22% -> 0% of each run, Pallas kernels for 0% -> 32%
where the time goes in v1:
time: 433 us; the launch traced here: 432 us
  Pallas kernels  261 us (60%)
  blocking collectives  115 us (27%)
  waiting for transfers between devices  29.7 us (7%)
  between operations  14.1 us (3%)
  starting transfers between devices  7.67 us (2%)
    all_to_all x3, blocking collectives, exchange(): lax.all_to_all(x, 'seq', 0, 0, axis_index_groups=SAME_CORE, tiled=True)  115 us
    pallas_call x1, Pallas kernels, pack(): pl.pallas_call(pack_body, out_shape=jax.ShapeDtypeStruct((HEADS, ROWS, HE...  97.7 us
    pallas_call x1, Pallas kernels, unpack(): pl.pallas_call(unpack_body, out_shape=(out, out, out), in_specs=[pl.Block...  96.8 us
    pallas_call x1, Pallas kernels, attention_backward(): pl.pallas_call(backward_body, out_shape=(jax.ShapeDtypeStruct((CHIPS, 2 *...  27 us
    pallas_call x1, Pallas kernels, attention_forward(): pl.pallas_call(forward_body, out_shape=(jax.ShapeDtypeStruct((CHIPS, HEAD...  19.2 us
    all_to_all x2, waiting for transfers between devices, exchange(): lax.all_to_all(x, 'seq', 0, 0, axis_index_groups=SAME_CORE, tiled=True)  18.1 us
    pallas_call x1, Pallas kernels, grad_attn_by_head(): pl.pallas_call(grad_attn_body, out_shape=jax.ShapeDtypeStruct((HEADS, TOK...  9.07 us
  transfers between devices with their start and end apart: 7, of which 4 were waited for; matrix products, arithmetic and copies ran while one was open for 0% of the time, Pallas kernels for 32%

profile of v1, /device:TPU:0, one launch (start us, length us, event | category | flops | bytes accessed | tf_op | source)
XLA Modules:
  0.0 432.3 jit_solution(10955170011432211664)
XLA Ops:
  7.2 97.7 %pack.1 = bf16[16,776,128]{2,1,0:T(8,128)(2,1)} custom-call(s32[2,4]{1,0:T(2,128)} %bitcast.17, bf16[256,2048]{1,0:T(8,128)(2,1)} %bitcast.14, bf16[256,2048]{1,0:T(8,128)(2,1)} %bitcast.15, bf16[256,2048]{1,0:T(8,128)(2,1)} %bitcast.16), custom_call_target="tpu_custom_call" | custom-call | tf_op jit(solution)/shard_map/pack/pallas_call | solution.py:66
  104.8 48.7 %all_to_all.25.x_ref = bf16[16,776,128]{2,1,0:T(8,128)(2,1)S(1)} all-to-all(bf16[16,776,128]{2,1,0:T(8,128)(2,1)} %pack.1), channel_id=1, replica_groups={{0,2,4,6,8,10,12,14,16,18,20,22,24,26,28,30},{1,3,5,7,9,11,13,15,17,19,..., dimensions={0} | all-to-all | bytes 6356992 | tf_op jit(solution)/shard_map/all_to_all | solution.py:37
  153.5 0.0 copy-start
  153.5 0.0 collective-permute-start
  153.5 0.1 iota_add_fusion
  153.6 0.1 add.52
  153.7 0.1 reshape.51
  153.8 0.9 add_select_fusion.table
  154.7 4.6 %collective-permute-done.y_ref = bf16[16,776,128]{2,1,0:T(8,128)(2,1)} collective-permute-done((bf16[16,776,128]{2,1,0:T(8,128)(2,1)S(1)}, bf16[16,776,128]{2,1,0:T(8,128)(2,1)}, u32[]{:S(2)}, u32[]{:S(2)}) %collective-permute-start) | collective-permute-done | bytes 3178528 | tf_op jit(solution)/shard_map/ppermute | solution.py:356
  159.4 0.0 copy-done
  159.4 19.2 %attn_fwd.1 = (bf16[16,128,256]{2,1,0:T(8,128)(2,1)}, f32[16,8,128]{2,1,0:T(8,128)}) custom-call(s32[32,4]{1,0:T(8,128)} %add_select_fusion.table, bf16[16,776,128]{2,1,0:T(8,128)(2,1)} %copy-done, bf16[16,776,128]{2,1,0:T(8,128)(2,1)} %collective-permute-done.y_ref), custom_call_target="tpu_custom_call" | custom-call | tf_op jit(solution)/shard_map/attn_fwd/pallas_call | solution.py:197
  178.5 3.7 all-to-all-start.3
  182.2 0.0 reduce-scatter.2.cloned.1.call-start
  182.3 0.2 collective-permute-start.3
  182.5 18.1 %all-to-all-done.3.oa_ref = bf16[16,128,256]{2,1,0:T(8,128)(2,1)S(1)} async-done(((bf16[16,128,256]{2,1,0:T(8,128)(2,1)}), bf16[16,128,256]{2,1,0:T(8,128)(2,1)S(1)}, u32[]{:S(2)}, u32[]{:S(2)}) %all-to-all-start.3) | async-done | bytes 1048608 | tf_op jit(solution)/shard_map/all_to_all | solution.py:37
  200.6 0.0 copy-start.1
  200.6 0.0 collective-permute-start.2
  200.6 0.0 collective-permute-done.3.cb_ref
  200.6 0.0 copy-start.3
  200.6 2.6 collective-permute-done.2.ob_ref
  203.2 0.0 copy-start.4
  203.2 0.0 copy-done.1
  203.2 0.0 copy-done.3
  203.2 1.0 copy-done.4
  204.2 6.2 %weight_partial.1 = bf16[1024,2048]{1,0:T(8,128)(2,1)} custom-call(s32[1]{0:T(128)} %bitcast.8.core, bf16[16,128,256]{2,1,0:T(8,128)(2,1)} %copy-done.1, bf16[16,128,256]{2,1,0:T(8,128)(2,1)} %copy-done.4, bf16[256,2048]{1,0:T(8,128)(2,1)} %bitcast.11, bf16[256,2048]{1,0:T(8,128)(2,1)} %copy-done.3), custom_call_target="tpu_custom_call" | custom-call | tf_op jit(solution)/shard_map/weight_partial/pallas_call | solution.py:321
  210.4 0.0 reduce-scatter.2.cloned.1.call-update
  210.5 9.1 %grad_attn.1 = bf16[16,256,128]{2,1,0:T(8,128)(2,1)} custom-call(bf16[256,2048]{1,0:T(8,128)(2,1)} %bitcast.12, bf16[2048,2048]{1,0:T(8,128)(2,1)} %w_ref.1), custom_call_target="tpu_custom_call" | custom-call | tf_op jit(solution)/shard_map/grad_attn/pallas_call | solution.py:112
  219.5 22.0 %all_to_all.26.g_ref = bf16[16,256,128]{2,1,0:T(8,128)(2,1)} all-to-all(bf16[16,256,128]{2,1,0:T(8,128)(2,1)} %grad_attn.1), channel_id=1, replica_groups={{0,2,4,6,8,10,12,14,16,18,20,22,24,26,28,30},{1,3,5,7,9,11,13,15,17,19,..., dimensions={0} | all-to-all | bytes 2097152 | tf_op jit(solution)/shard_map/all_to_all | solution.py:37
  241.5 27.0 %attn_bwd.1 = (f32[16,512,128]{2,1,0:T(8,128)}, bf16[16,512,128]{2,1,0:T(8,128)(2,1)}, bf16[16,256,128]{2,1,0:T(8,128)(2,1)}) custom-call(s32[32,4]{1,0:T(8,128)} %add_select_fusion.table, bf16[16,776,128]{2,1,0:T(8,128)(2,1)} %copy-done, bf16[16,776,128]{2,1,0:T(8,128)(2,1)} %collective-permute-done.y_ref, bf16[16,256,128]{2,1,0:T(8,128)(2,1)} %all_to_all.26.g_ref, ...), custom_call_target="tpu_custom_call" | custom-call | tf_op jit(solution)/shard_map/attn_bwd/pallas_call | solution.py:270
  268.5 0.1 collective-permute-start.1
  268.6 4.4 %collective-permute-done.1.got_ref = bf16[16,512,128]{2,1,0:T(8,128)(2,1)S(1)} collective-permute-done((bf16[16,512,128]{2,1,0:T(8,128)(2,1)}, bf16[16,512,128]{2,1,0:T(8,128)(2,1)S(1)}, u32[]{:S(2)}, u32[]{:S(2)}) %collective-permute-start.1) | collective-permute-done | bytes 2097184 | tf_op jit(solution)/shard_map/ppermute | solution.py:362
  273.0 0.0 copy-start.2
  273.0 1.4 copy-done.2
  274.4 5.1 %combine.1 = bf16[16,768,128]{2,1,0:T(8,128)(2,1)} custom-call(f32[16,512,128]{2,1,0:T(8,128)} %get-tuple-element.13.own_ref, bf16[16,512,128]{2,1,0:T(8,128)(2,1)} %copy-done.2, bf16[16,256,128]{2,1,0:T(8,128)(2,1)} %get-tuple-element.15.gq_ref), custom_call_target="tpu_custom_call" | custom-call | tf_op jit(solution)/shard_map/combine/pallas_call | solution.py:299
  279.5 44.6 %all_to_all.27.r_ref = bf16[16,768,128]{2,1,0:T(8,128)(2,1)} all-to-all(bf16[16,768,128]{2,1,0:T(8,128)(2,1)} %combine.1), channel_id=1, replica_groups={{0,2,4,6,8,10,12,14,16,18,20,22,24,26,28,30},{1,3,5,7,9,11,13,15,17,19,..., dimensions={0} | all-to-all | bytes 6291456 | tf_op jit(solution)/shard_map/all_to_all | solution.py:37
  324.2 0.0 reduce-scatter.2.cloned.1.call-done
  324.2 3.7 all-to-all-start.4
  327.8 96.8 %unpack.1 = (bf16[256,2048]{1,0:T(8,128)(2,1)}, bf16[256,2048]{1,0:T(8,128)(2,1)}, bf16[256,2048]{1,0:T(8,128)(2,1)}) custom-call(bf16[16,768,128]{2,1,0:T(8,128)(2,1)} %all_to_all.27.r_ref), custom_call_target="tpu_custom_call" | custom-call | tf_op jit(solution)/shard_map/unpack/pallas_call | solution.py:95
  424.7 0.0 all-to-all-done.4
  424.7 0.8 convert_reduce_fusion
  (2 shorter events, 0.0 us)
Async XLA Ops:
  153.5 5.8 %copy-start = (bf16[16,776,128]{2,1,0:T(8,128)(2,1)}, bf16[16,776,128]{2,1,0:T(8,128)(2,1)S(1)}, u32[]{:S(2)}) copy-start(bf16[16,776,128]{2,1,0:T(8,128)(2,1)S(1)} %all_to_all.25.x_ref) | copy-start | bytes 9535492
  153.5 5.8 %collective-permute-start = (bf16[16,776,128]{2,1,0:T(8,128)(2,1)S(1)}, bf16[16,776,128]{2,1,0:T(8,128)(2,1)}, u32[]{:S(2)}, u32[]{:S(2)}) collective-permute-start(bf16[16,776,128]{2,1,0:T(8,128)(2,1)S(1)} %all_to_all.25.x_ref), channel_id=1, source_target_pairs={{0,1},{1,0},{2,3},{3,2},{4,5},{5,4},{6,7},{7,6},{8,9},{9,8},{10,11... | collective-permute-start | bytes 9535496 | tf_op jit(solution)/shard_map/ppermute | solution.py:356
  178.5 22.0 %all-to-all-start.3 = ((bf16[16,128,256]{2,1,0:T(8,128)(2,1)}), bf16[16,128,256]{2,1,0:T(8,128)(2,1)S(1)}, u32[]{:S(2)}, u32[]{:S(2)}) async-start(bf16[16,128,256]{2,1,0:T(8,128)(2,1)} %get-tuple-element.19), calls=%async_computation.3 | async-start | bytes 2097152 | tf_op jit(solution)/shard_map/all_to_all | solution.py:37
  182.2 142.0 %reduce-scatter.2.cloned.1.call-start = ((), (), s32[]{:S(2)}) async-start(), calls=%async_computation.6 | async-start | bytes 5242880 | tf_op jit(solution)/shard_map/reduce_scatter | solution.py:365
  182.3 18.3 %collective-permute-start.3 = (bf16[256,2048]{1,0:T(8,128)(2,1)}, bf16[256,2048]{1,0:T(8,128)(2,1)S(1)}, u32[]{:S(2)}, u32[]{:S(2)}) collective-permute-start(bf16[256,2048]{1,0:T(8,128)(2,1)} %bitcast.10), channel_id=1, source_target_pairs={{0,1},{1,0},{2,3},{3,2},{4,5},{5,4},{6,7},{7,6},{8,9},{9,8},{10,11... | collective-permute-start | bytes 3145736 | tf_op jit(solution)/shard_map/ppermute | solution.py:355
  200.6 2.7 copy-start.1
  200.6 2.7 collective-permute-start.2
  200.6 2.7 copy-start.3
  203.2 1.0 copy-start.4
  268.5 4.5 %collective-permute-start.1 = (bf16[16,512,128]{2,1,0:T(8,128)(2,1)}, bf16[16,512,128]{2,1,0:T(8,128)(2,1)S(1)}, u32[]{:S(2)}, u32[]{:S(2)}) collective-permute-start(bf16[16,512,128]{2,1,0:T(8,128)(2,1)} %get-tuple-element.14), channel_id=1, source_target_pairs={{0,1},{1,0},{2,3},{3,2},{4,5},{5,4},{6,7},{7,6},{8,9},{9,8},{10,11... | collective-permute-start | bytes 6291464 | tf_op jit(solution)/shard_map/ppermute | solution.py:362
  273.0 1.4 copy-start.2
  324.2 100.5 %all-to-all-start.4 = ((bf16[16,16,2048]{2,1,0:T(8,128)(2,1)}), bf16[16,16,2048]{2,1,0:T(8,128)(2,1)S(1)}, u32[]{:S(2)}, u32[]{:S(2)}) async-start(bf16[16,16,2048]{2,1,0:T(8,128)(2,1)} %bitcast.13), calls=%async_computation.5 | async-start | bytes 2097152 | tf_op jit(solution)/shard_map/all_to_all | solution.py:37
Sparse Core Ops, SparseCore 0:
  210.6 44.6 reduce-scatter.1

commit v2 on v1

--- a/solution.py
+++ b/solution.py
@@ -26,6 +26,7 @@
 SAME_CORE = [[2 * c + k for c in range(CHIPS)] for k in range(2)]
 CORE_SWAP = [(i, i ^ 1) for i in range(2 * CHIPS)]
 
+PACK = 4
 VMEM_LIMIT = 56 * 1024 * 1024
 
 
@@ -33,71 +34,67 @@
     return lax.dot_general(a, b, (((ca,), (cb,)), ((), ())), preferred_element_type=f32)
 
 
+def cost(flops, transcendentals=0, bytes_accessed=0):
+    return pl.CostEstimate(
+        flops=flops, transcendentals=transcendentals, bytes_accessed=bytes_accessed
+    )
+
+
+PAIRS = BLOCKS // 2 * BLK * (1 + SLOTS) * BLK
+PAIR_FLOPS = 2 * HEAD * PAIRS
+MIB = 1024 * 1024
+
+
 def exchange(x):
     return lax.all_to_all(x, "seq", 0, 0, axis_index_groups=SAME_CORE, tiled=True)
 
 
-def pack_body(offs, k_ref, v_ref, q_ref, x_ref, rider, sems):
+def after(*values):
+    return lax.optimization_barrier(values)
+
+
+def pack_body(offs, k_ref, v_ref, q_ref, x_ref):
     lane = lax.broadcasted_iota(jnp.int32, (8, 128), 1)
     val = jnp.zeros((8, 128), jnp.int32)
     for j in range(2 * SLOTS):
         val = jnp.where(lane == j, offs[j // SLOTS, j % SLOTS], val)
-    rider[...] = val.astype(f32).astype(bf16)
-    copies = []
-    for h in range(HEADS):
+    rider = val.astype(f32).astype(bf16)
+    for h in range(PACK):
         for t, ref in enumerate((k_ref, v_ref, q_ref)):
-            copies.append(
-                pltpu.make_async_copy(
-                    ref.at[:, pl.ds(h * HEAD, HEAD)],
-                    x_ref.at[h, pl.ds(t * TOK, TOK), :],
-                    sems.at[4 * h + t],
-                )
-            )
-        copies.append(
-            pltpu.make_async_copy(rider, x_ref.at[h, pl.ds(RIDER, 8), :], sems.at[4 * h + 3])
-        )
-    for copy in copies:
-        copy.start()
-    for copy in copies:
-        copy.wait()
+            x_ref[h, t * TOK : (t + 1) * TOK, :] = ref[:, h * HEAD : (h + 1) * HEAD]
+        x_ref[h, RIDER : RIDER + 8, :] = rider
 
 
 def pack(offs, k, v, q):
+    rows = pl.BlockSpec((TOK, PACK * HEAD), lambda i: (0, i))
     return pl.pallas_call(
         pack_body,
         out_shape=jax.ShapeDtypeStruct((HEADS, ROWS, HEAD), bf16),
-        in_specs=[pl.BlockSpec(memory_space=pltpu.SMEM)] + [pl.BlockSpec(memory_space=pl.ANY)] * 3,
-        out_specs=pl.BlockSpec(memory_space=pl.ANY),
-        scratch_shapes=[pltpu.VMEM((8, 128), bf16), pltpu.SemaphoreType.DMA((4 * HEADS,))],
+        grid=(HEADS // PACK,),
+        in_specs=[pl.BlockSpec(memory_space=pltpu.SMEM), rows, rows, rows],
+        out_specs=pl.BlockSpec((PACK, ROWS, HEAD), lambda i: (i, 0, 0)),
+        compiler_params=pltpu.CompilerParams(vmem_limit_bytes=VMEM_LIMIT),
         name="pack",
     )(offs, k, v, q)
 
 
-def unpack_body(r_ref, gk_ref, gv_ref, gq_ref, sems):
-    copies = []
-    for h in range(HEADS):
-        for t, ref in enumerate((gk_ref, gv_ref, gq_ref)):
-            copies.append(
-                pltpu.make_async_copy(
-                    r_ref.at[h, pl.ds(t * TOK, TOK), :],
-                    ref.at[:, pl.ds(h * HEAD, HEAD)],
-                    sems.at[3 * h + t],
-                )
-            )
-    for copy in copies:
-        copy.start()
-    for copy in copies:
-        copy.wait()
-
-
-def unpack(r):
+def unpack_body(r_ref, *refs):
+    for h in range(PACK):
+        for t, ref in enumerate(refs):
+            ref[:, h * HEAD : (h + 1) * HEAD] = r_ref[h, t * TOK : (t + 1) * TOK, :]
+
+
+def unpack(r, n):
     out = jax.ShapeDtypeStruct((TOK, D), bf16)
+    rows = pl.BlockSpec((TOK, PACK * HEAD), lambda i: (0, i))
     return pl.pallas_call(
         unpack_body,
-        out_shape=(out, out, out),
-        in_specs=[pl.BlockSpec(memory_space=pl.ANY)],
-        out_specs=[pl.BlockSpec(memory_space=pl.ANY)] * 3,
-        scratch_shapes=[pltpu.SemaphoreType.DMA((3 * HEADS,))],
+        out_shape=(out,) * n,
+        grid=(HEADS // PACK,),
+        in_specs=[pl.BlockSpec((PACK, n * TOK, HEAD), lambda i: (i, 0, 0))],
+        out_specs=[rows] * n,
+        compiler_params=pltpu.CompilerParams(vmem_limit_bytes=VMEM_LIMIT),
+        cost_estimate=cost(0, 0, 2 * n * MIB),
         name="unpack",
     )(r)
 
@@ -119,6 +116,7 @@
         ],
         out_specs=pl.BlockSpec((2, TOK, HEAD), lambda i: (i, 0, 0)),
         compiler_params=pltpu.CompilerParams(vmem_limit_bytes=VMEM_LIMIT),
+        cost_estimate=cost(2 * TOK * D * D, 0, 10 * MIB),
         name="grad_attn",
     )(cot, weight)
 
@@ -208,6 +206,7 @@
             pltpu.SemaphoreType.DMA((3,)),
         ],
         compiler_params=pltpu.CompilerParams(vmem_limit_bytes=VMEM_LIMIT),
+        cost_estimate=cost(2 * PAIR_FLOPS, PAIRS, 7 * MIB),
         name="attn_fwd",
     )(table, x, y)
 
@@ -285,30 +284,28 @@
             pltpu.SemaphoreType.DMA((3,)),
         ],
         compiler_params=pltpu.CompilerParams(vmem_limit_bytes=VMEM_LIMIT),
+        cost_estimate=cost(5 * PAIR_FLOPS, PAIRS, 14 * MIB),
         name="attn_bwd",
     )(table, x, y, g, lse)
 
 
-def combine_body(own_ref, got_ref, gq_ref, o_ref):
-    o_ref[:, 0 : 2 * TOK, :] = (own_ref[...] + got_ref[...].astype(f32)).astype(bf16)
-    o_ref[:, 2 * TOK : 3 * TOK, :] = gq_ref[...]
-
-
-def combine(own, got, gq):
+def combine_body(own_ref, got_ref, o_ref):
+    o_ref[...] = (own_ref[...] + got_ref[...].astype(f32)).astype(bf16)
+
+
+def combine(own, got):
     n = 4
+    rows = pl.BlockSpec((n, 2 * TOK, HEAD), lambda i: (i, 0, 0))
     return pl.pallas_call(
         combine_body,
-        out_shape=jax.ShapeDtypeStruct((CHIPS, 3 * TOK, HEAD), bf16),
+        out_shape=jax.ShapeDtypeStruct((CHIPS, 2 * TOK, HEAD), bf16),
         grid=(CHIPS // n,),
-        in_specs=[
-            pl.BlockSpec((n, 2 * TOK, HEAD), lambda i: (i, 0, 0)),
-            pl.BlockSpec((n, 2 * TOK, HEAD), lambda i: (i, 0, 0)),
-            pl.BlockSpec((n, TOK, HEAD), lambda i: (i, 0, 0)),
-        ],
-        out_specs=pl.BlockSpec((n, 3 * TOK, HEAD), lambda i: (i, 0, 0)),
-        compiler_params=pltpu.CompilerParams(vmem_limit_bytes=VMEM_LIMIT),
+        in_specs=[rows, rows],
+        out_specs=rows,
+        compiler_params=pltpu.CompilerParams(vmem_limit_bytes=VMEM_LIMIT),
+        cost_estimate=cost(CHIPS * 2 * TOK * HEAD, 0, 8 * MIB),
         name="combine",
-    )(own, got, gq)
+    )(own, got)
 
 
 def weight_body(core, oa_ref, ob_ref, ca_ref, cb_ref, w_ref):
@@ -333,6 +330,7 @@
             out_specs=pl.BlockSpec((4 * 64, D), lambda i, core: (i, 0)),
         ),
         compiler_params=pltpu.CompilerParams(vmem_limit_bytes=VMEM_LIMIT),
+        cost_estimate=cost(2 * TOK * D * D, 0, 8 * MIB),
         name="weight_partial",
     )(core, oa, ob, ca, cb)
 
@@ -350,22 +348,29 @@
 def local(queries, key_states, value_states, out_weight, cotangent, block_offsets):
     core = lax.axis_index("seq") % 2
     cot = cotangent[0]
+    cot_other = lax.ppermute(cot, "seq", CORE_SWAP)
     x = exchange(pack(block_offsets[0], key_states[0], value_states[0], queries[0]))
-    g = exchange(grad_attn_by_head(cot, out_weight))
-    cot_other = lax.ppermute(cot, "seq", CORE_SWAP)
+    x, g = after(x, grad_attn_by_head(cot, out_weight))
     y = lax.ppermute(x, "seq", CORE_SWAP)
+    g = exchange(g)
     table = block_table(x[:, RIDER, 0 : 2 * SLOTS], core)
     out, lse = attention_forward(table, x, y)
+    g, out = after(g, out)
     out_home = exchange(out)
+    own, other, gq = attention_backward(table, x, y, g, lse)
+    out_home, gq, other = after(out_home, gq, other)
+    gq_home = exchange(gq)
     out_other = lax.ppermute(out_home, "seq", CORE_SWAP)
-    own, other, gq = attention_backward(table, x, y, g, lse)
-    got = lax.ppermute(other, "seq", CORE_SWAP)
-    home = exchange(combine(own, got, gq))
     partial = weight_partial(core.reshape(1), out_home, out_other, cot, cot_other)
     by_doc = lax.psum_scatter(partial, "dp", scatter_dimension=0, tiled=True)
+    got = lax.ppermute(other, "seq", CORE_SWAP)
+    gq_home, gathered = after(gq_home, combine(own, got))
+    kv_home = exchange(gathered)
+    kv_home, by_doc = after(kv_home, by_doc)
     pieces = exchange(by_doc.reshape(CHIPS, 16, D))
     weight_grad = jnp.sum(pieces.astype(f32), axis=0)
-    gk, gv, gq = unpack(home)
+    (gq,) = unpack(gq_home, 1)
+    gk, gv = unpack(kv_home, 2)
     return gq[None], gk[None], gv[None], weight_grad
 
 

time: 433 us -> 218 us (0.50)
  Pallas kernels: 261 us -> 77.9 us
  blocking collectives: 115 us -> 30.8 us
  starting transfers between devices: 7.67 us -> 35.5 us
  waiting for transfers between devices: 29.7 us -> 54.6 us
    pallas_call x1, Pallas kernels: 97.7 us -> 4.37 us  [pack(): pl.pallas_call(pack_body, out_shape=jax.ShapeDtypeStruct((HEADS, ROWS, HE...]
    pallas_call x2 -> x3, Pallas kernels: 102 us -> 12.3 us  [the longest x2 7.3 us: unpack(): pl.pallas_call(unpack_body, out_shape=(out,) * n, grid=(HEADS // PACK,),...]
    all_to_all x3 -> x1, blocking collectives: 115 us -> 30.8 us  [exchange(): lax.all_to_all(x, 'seq', 0, 0, axis_index_groups=SAME_CORE, tiled=True)]
    all_to_all x2 -> x5, waiting for transfers between devices: 18.1 us -> 52.3 us  [exchange(): lax.all_to_all(x, 'seq', 0, 0, axis_index_groups=SAME_CORE, tiled=True)]
    all_to_all x2 -> x5, starting transfers between devices: 7.32 us -> 34.3 us  [exchange(): lax.all_to_all(x, 'seq', 0, 0, axis_index_groups=SAME_CORE, tiled=True)]
    ppermute x1, waiting for transfers between devices: 4.61 us -> 0.01 us  [local(): y = lax.ppermute(x, 'seq', CORE_SWAP)]
    ppermute x1, waiting for transfers between devices: 4.36 us -> 0.01 us  [local(): got = lax.ppermute(other, 'seq', CORE_SWAP)]
  transfers between devices with their start and end apart: 7 -> 10, of which waited for: 4 -> 4; matrix products, arithmetic and copies ran while one was open for 0% -> 0% of each run, Pallas kernels for 32% -> 31%
where the time goes in v2:
time: 218 us; the launch traced here: 217 us
  Pallas kernels  77.9 us (36%)
  waiting for transfers between devices  54.6 us (25%)
  starting transfers between devices  35.5 us (16%)
  blocking collectives  30.8 us (14%)
  between operations  14.2 us (7%)
  local copies, waits for them, and re-layouts  2.46 us (1%)
    all_to_all x5, waiting for transfers between devices, exchange(): lax.all_to_all(x, 'seq', 0, 0, axis_index_groups=SAME_CORE, tiled=True)  52.3 us
    all_to_all x5, starting transfers between devices, exchange(): lax.all_to_all(x, 'seq', 0, 0, axis_index_groups=SAME_CORE, tiled=True)  34.3 us
    all_to_all x1, blocking collectives, exchange(): lax.all_to_all(x, 'seq', 0, 0, axis_index_groups=SAME_CORE, tiled=True)  30.8 us
    pallas_call x1, Pallas kernels, attention_backward(): pl.pallas_call(backward_body, out_shape=(jax.ShapeDtypeStruct((CHIPS, 2 *...  27 us
    pallas_call x1, Pallas kernels, attention_forward(): pl.pallas_call(forward_body, out_shape=(jax.ShapeDtypeStruct((CHIPS, HEAD...  19.2 us
    pallas_call x1, Pallas kernels, grad_attn_by_head(): pl.pallas_call(grad_attn_body, out_shape=jax.ShapeDtypeStruct((HEADS, TOK...  8.78 us
    pallas_call x2, Pallas kernels, unpack(): pl.pallas_call(unpack_body, out_shape=(out,) * n, grid=(HEADS // PACK,),...  7.3 us
    pallas_call x1, Pallas kernels, weight_partial(): pl.pallas_call(weight_body, out_shape=jax.ShapeDtypeStruct((HEADS * 64, D...  6.28 us
  transfers between devices with their start and end apart: 10, of which 4 were waited for; matrix products, arithmetic and copies ran while one was open for 0% of the time, Pallas kernels for 31%

profile of v2, /device:TPU:0, one launch (start us, length us, event | category | flops | bytes accessed | tf_op | source)
XLA Modules:
  0.0 216.9 jit_solution(2510167548962602831)
XLA Ops:
  7.2 4.4 %pack.1 = bf16[16,776,128]{2,1,0:T(8,128)(2,1)} custom-call(s32[2,4]{1,0:T(2,128)} %bitcast.18, bf16[256,2048]{1,0:T(8,128)(2,1)} %bitcast.15, bf16[256,2048]{1,0:T(8,128)(2,1)} %bitcast.16, bf16[256,2048]{1,0:T(8,128)(2,1)} %bitcast.17), custom_call_target="tpu_custom_call" | custom-call | tf_op jit(solution)/shard_map/pack/pallas_call | solution.py:70
  11.5 8.1 %all-to-all-start = ((bf16[16,776,128]{2,1,0:T(8,128)(2,1)}), bf16[16,776,128]{2,1,0:T(8,128)(2,1)S(1)}, u32[]{:S(2)}, u32[]{:S(2)}) async-start(bf16[16,776,128]{2,1,0:T(8,128)(2,1)} %pack.1), calls=%async_computation | async-start | bytes 6356992 | tf_op jit(solution)/shard_map/all_to_all | solution.py:49
  19.7 8.8 %grad_attn.1 = bf16[16,256,128]{2,1,0:T(8,128)(2,1)} custom-call(bf16[256,2048]{1,0:T(8,128)(2,1)} %bitcast.10, bf16[2048,2048]{1,0:T(8,128)(2,1)} %w_ref.1), custom_call_target="tpu_custom_call" | custom-call | flops 2147483648 | bytes 10485760 | tf_op jit(solution)/shard_map/grad_attn/pallas_call | solution.py:109
  28.5 34.0 %all-to-all-done.x_ref = bf16[16,776,128]{2,1,0:T(8,128)(2,1)S(1)} async-done(((bf16[16,776,128]{2,1,0:T(8,128)(2,1)}), bf16[16,776,128]{2,1,0:T(8,128)(2,1)S(1)}, u32[]{:S(2)}, u32[]{:S(2)}) %all-to-all-start) | async-done | bytes 3178528 | tf_op jit(solution)/shard_map/all_to_all | solution.py:49
  62.5 0.0 copy-start
  62.5 0.0 collective-permute-start
  62.5 8.1 %all-to-all-start.1 = ((bf16[16,256,128]{2,1,0:T(8,128)(2,1)}), bf16[16,256,128]{2,1,0:T(8,128)(2,1)}, u32[]{:S(2)}, u32[]{:S(2)}) async-start(bf16[16,256,128]{2,1,0:T(8,128)(2,1)} %grad_attn.1), calls=%async_computation.1 | async-start | bytes 2097152 | tf_op jit(solution)/shard_map/all_to_all | solution.py:49
  70.7 0.1 iota_add_fusion
  70.7 0.1 add.52
  70.9 0.1 reshape.51
  70.9 0.7 add_select_fusion.table
  71.6 0.0 collective-permute-done.y_ref
  71.6 0.0 copy-done
  71.6 19.2 %attn_fwd.1 = (bf16[16,128,256]{2,1,0:T(8,128)(2,1)}, f32[16,8,128]{2,1,0:T(8,128)}) custom-call(s32[32,4]{1,0:T(8,128)} %add_select_fusion.table, bf16[16,776,128]{2,1,0:T(8,128)(2,1)} %copy-done, bf16[16,776,128]{2,1,0:T(8,128)(2,1)} %collective-permute-done.y_ref), custom_call_target="tpu_custom_call" | custom-call | flops 1342177280 | bytes 7340032 | tf_op jit(solution)/shard_map/attn_fwd/pallas_call | solution.py:195
  90.8 0.0 all-to-all-done.1.g_ref
  90.8 7.2 %all-to-all-start.2 = ((bf16[16,128,256]{2,1,0:T(8,128)(2,1)}), bf16[16,128,256]{2,1,0:T(8,128)(2,1)S(1)}, u32[]{:S(2)}, u32[]{:S(2)}) async-start(bf16[16,128,256]{2,1,0:T(8,128)(2,1)} %get-tuple-element.25), calls=%async_computation.2 | async-start | bytes 2097152 | tf_op jit(solution)/shard_map/all_to_all | solution.py:49
  98.0 0.0 reduce-scatter.2.cloned.1.call-start
  98.1 0.1 collective-permute-start.3
  98.2 27.0 %attn_bwd.1 = (f32[16,512,128]{2,1,0:T(8,128)}, bf16[16,512,128]{2,1,0:T(8,128)(2,1)}, bf16[16,256,128]{2,1,0:T(8,128)(2,1)}) custom-call(s32[32,4]{1,0:T(8,128)} %add_select_fusion.table, bf16[16,776,128]{2,1,0:T(8,128)(2,1)} %copy-done, bf16[16,776,128]{2,1,0:T(8,128)(2,1)} %collective-permute-done.y_ref, bf16[16,256,128]{2,1,0:T(8,128)(2,1)} %all-to-all-done.1.g_ref, ...), custom_call_target="tpu_custom_call" | custom-call | flops 3355443200 | bytes 14680064 | tf_op jit(solution)/shard_map/attn_bwd/pallas_call | solution.py:269
  125.1 0.0 all-to-all-done.2.oa_ref
  125.2 0.0 copy-start.1
  125.2 0.6 collective-permute-start.2
  125.7 0.0 collective-permute-done.3.cb_ref
  125.7 0.0 copy-start.4
  125.7 2.3 %collective-permute-done.2.ob_ref = bf16[16,128,256]{2,1,0:T(8,128)(2,1)S(1)} collective-permute-done((bf16[16,128,256]{2,1,0:T(8,128)(2,1)S(1)}, bf16[16,128,256]{2,1,0:T(8,128)(2,1)S(1)}, u32[]{:S(2)}, u32[]{:S(2)}) %collective-permute-start.2) | collective-permute-done | bytes 1048608 | tf_op jit(solution)/shard_map/ppermute | solution.py:363
  128.0 0.0 copy-start.5
  128.0 0.0 copy-done.1
  128.0 0.0 copy-done.4
  128.0 1.0 copy-done.5
  129.0 6.3 %weight_partial.1 = bf16[1024,2048]{1,0:T(8,128)(2,1)} custom-call(s32[1]{0:T(128)} %bitcast.6.core, bf16[16,128,256]{2,1,0:T(8,128)(2,1)} %copy-done.1, bf16[16,128,256]{2,1,0:T(8,128)(2,1)} %copy-done.5, bf16[256,2048]{1,0:T(8,128)(2,1)} %bitcast.12, bf16[256,2048]{1,0:T(8,128)(2,1)} %copy-done.4), custom_call_target="tpu_custom_call" | custom-call | flops 2147483648 | bytes 8388608 | tf_op jit(solution)/shard_map/weight_partial/pallas_call | solution.py:318
  135.3 0.0 reduce-scatter.2.cloned.1.call-update
  135.3 0.5 collective-permute-start.1
  135.8 7.2 %all-to-all-start.3 = ((bf16[16,256,128]{2,1,0:T(8,128)(2,1)}), bf16[16,256,128]{2,1,0:T(8,128)(2,1)S(1)}, u32[]{:S(2)}, u32[]{:S(2)}) async-start(bf16[16,256,128]{2,1,0:T(8,128)(2,1)} %get-tuple-element.30), calls=%async_computation.3 | async-start | bytes 2097152 | tf_op jit(solution)/shard_map/all_to_all | solution.py:49
  143.0 0.0 collective-permute-done.1.got_ref
  143.0 0.0 copy-start.3
  143.0 1.3 copy-done.3
  144.3 5.0 %combine.1 = bf16[16,512,128]{2,1,0:T(8,128)(2,1)} custom-call(f32[16,512,128]{2,1,0:T(8,128)} %get-tuple-element.31.own_ref, bf16[16,512,128]{2,1,0:T(8,128)(2,1)} %copy-done.3), custom_call_target="tpu_custom_call" | custom-call | flops 1048576 | bytes 8388608 | tf_op jit(solution)/shard_map/combine/pallas_call | solution.py:299
  149.3 11.8 %all-to-all-done.3.r_ref = bf16[16,256,128]{2,1,0:T(8,128)(2,1)S(1)} async-done(((bf16[16,256,128]{2,1,0:T(8,128)(2,1)}), bf16[16,256,128]{2,1,0:T(8,128)(2,1)S(1)}, u32[]{:S(2)}, u32[]{:S(2)}) %all-to-all-start.3) | async-done | bytes 1048608 | tf_op jit(solution)/shard_map/all_to_all | solution.py:49
  161.1 0.0 copy-start.2
  161.1 30.8 %all_to_all.30.r_ref = bf16[16,512,128]{2,1,0:T(8,128)(2,1)} all-to-all(bf16[16,512,128]{2,1,0:T(8,128)(2,1)} %combine.1), channel_id=1, replica_groups={{0,2,4,6,8,10,12,14,16,18,20,22,24,26,28,30},{1,3,5,7,9,11,13,15,17,19,..., dimensions={0} | all-to-all | bytes 4194304 | tf_op jit(solution)/shard_map/all_to_all | solution.py:49
  191.9 0.0 reduce-scatter.2.cloned.1.call-done
  191.9 3.7 %all-to-all-start.5 = ((bf16[16,16,2048]{2,1,0:T(8,128)(2,1)}), bf16[16,16,2048]{2,1,0:T(8,128)(2,1)S(1)}, u32[]{:S(2)}, u32[]{:S(2)}) async-start(bf16[16,16,2048]{2,1,0:T(8,128)(2,1)} %bitcast.13), calls=%async_computation.6 | async-start | bytes 2097152 | tf_op jit(solution)/shard_map/all_to_all | solution.py:49
  195.5 0.0 copy-done.2
  195.5 3.4 %unpack.2 = bf16[256,2048]{1,0:T(8,128)(2,1)} custom-call(bf16[16,256,128]{2,1,0:T(8,128)(2,1)} %copy-done.2), custom_call_target="tpu_custom_call" | custom-call | bytes 2097152 | tf_op jit(solution)/shard_map/unpack/pallas_call | solution.py:90
  199.0 3.9 %unpack.3 = (bf16[256,2048]{1,0:T(8,128)(2,1)}, bf16[256,2048]{1,0:T(8,128)(2,1)}) custom-call(bf16[16,512,128]{2,1,0:T(8,128)(2,1)} %all_to_all.30.r_ref), custom_call_target="tpu_custom_call" | custom-call | bytes 4194304 | tf_op jit(solution)/shard_map/unpack/pallas_call | solution.py:90
  202.8 6.4 %all-to-all-done.5 = bf16[16,16,2048]{2,1,0:T(8,128)(2,1)S(1)} async-done(((bf16[16,16,2048]{2,1,0:T(8,128)(2,1)}), bf16[16,16,2048]{2,1,0:T(8,128)(2,1)S(1)}, u32[]{:S(2)}, u32[]{:S(2)}) %all-to-all-start.5) | async-done | bytes 1048608 | tf_op jit(solution)/shard_map/all_to_all | solution.py:49
  209.3 0.8 convert_reduce_fusion
  (2 shorter events, 0.0 us)
Async XLA Ops:
  11.5 51.0 %all-to-all-start = ((bf16[16,776,128]{2,1,0:T(8,128)(2,1)}), bf16[16,776,128]{2,1,0:T(8,128)(2,1)S(1)}, u32[]{:S(2)}, u32[]{:S(2)}) async-start(bf16[16,776,128]{2,1,0:T(8,128)(2,1)} %pack.1), calls=%async_computation | async-start | bytes 6356992 | tf_op jit(solution)/shard_map/all_to_all | solution.py:49
  62.5 9.1 %copy-start = (bf16[16,776,128]{2,1,0:T(8,128)(2,1)}, bf16[16,776,128]{2,1,0:T(8,128)(2,1)S(1)}, u32[]{:S(2)}) copy-start(bf16[16,776,128]{2,1,0:T(8,128)(2,1)S(1)} %all-to-all-done.x_ref) | copy-start | bytes 9535492
  62.5 9.1 %collective-permute-start = (bf16[16,776,128]{2,1,0:T(8,128)(2,1)S(1)}, bf16[16,776,128]{2,1,0:T(8,128)(2,1)}, u32[]{:S(2)}, u32[]{:S(2)}) collective-permute-start(bf16[16,776,128]{2,1,0:T(8,128)(2,1)S(1)} %all-to-all-done.x_ref), channel_id=1, source_target_pairs={{0,1},{1,0},{2,3},{3,2},{4,5},{5,4},{6,7},{7,6},{8,9},{9,8},{10,11... | collective-permute-start | bytes 9535496 | tf_op jit(solution)/shard_map/ppermute | solution.py:354
  62.5 28.3 %all-to-all-start.1 = ((bf16[16,256,128]{2,1,0:T(8,128)(2,1)}), bf16[16,256,128]{2,1,0:T(8,128)(2,1)}, u32[]{:S(2)}, u32[]{:S(2)}) async-start(bf16[16,256,128]{2,1,0:T(8,128)(2,1)} %grad_attn.1), calls=%async_computation.1 | async-start | bytes 2097152 | tf_op jit(solution)/shard_map/all_to_all | solution.py:49
  90.8 34.3 %all-to-all-start.2 = ((bf16[16,128,256]{2,1,0:T(8,128)(2,1)}), bf16[16,128,256]{2,1,0:T(8,128)(2,1)S(1)}, u32[]{:S(2)}, u32[]{:S(2)}) async-start(bf16[16,128,256]{2,1,0:T(8,128)(2,1)} %get-tuple-element.25), calls=%async_computation.2 | async-start | bytes 2097152 | tf_op jit(solution)/shard_map/all_to_all | solution.py:49
  98.0 93.9 %reduce-scatter.2.cloned.1.call-start = ((), (), s32[]{:S(2)}) async-start(), calls=%async_computation.7 | async-start | bytes 5242880 | tf_op jit(solution)/shard_map/reduce_scatter | solution.py:365
  98.1 27.7 %collective-permute-start.3 = (bf16[256,2048]{1,0:T(8,128)(2,1)}, bf16[256,2048]{1,0:T(8,128)(2,1)S(1)}, u32[]{:S(2)}, u32[]{:S(2)}) collective-permute-start(bf16[256,2048]{1,0:T(8,128)(2,1)} %bitcast.11), channel_id=1, source_target_pairs={{0,1},{1,0},{2,3},{3,2},{4,5},{5,4},{6,7},{7,6},{8,9},{9,8},{10,11... | collective-permute-start | bytes 3145736 | tf_op jit(solution)/shard_map/ppermute | solution.py:351
  125.2 2.9 %copy-start.1 = (bf16[16,128,256]{2,1,0:T(8,128)(2,1)}, bf16[16,128,256]{2,1,0:T(8,128)(2,1)S(1)}, u32[]{:S(2)}) copy-start(bf16[16,128,256]{2,1,0:T(8,128)(2,1)S(1)} %all-to-all-done.2.oa_ref) | copy-start | bytes 3145732
  125.2 2.9 %collective-permute-start.2 = (bf16[16,128,256]{2,1,0:T(8,128)(2,1)S(1)}, bf16[16,128,256]{2,1,0:T(8,128)(2,1)S(1)}, u32[]{:S(2)}, u32[]{:S(2)}) collective-permute-start(bf16[16,128,256]{2,1,0:T(8,128)(2,1)S(1)} %all-to-all-done.2.oa_ref), channel_id=1, source_target_pairs={{0,1},{1,0},{2,3},{3,2},{4,5},{5,4},{6,7},{7,6},{8,9},{9,8},{10,11... | collective-permute-start | bytes 3145736 | tf_op jit(solution)/shard_map/ppermute | solution.py:363
  125.7 2.3 %copy-start.4 = (bf16[256,2048]{1,0:T(8,128)(2,1)}, bf16[256,2048]{1,0:T(8,128)(2,1)S(1)}, u32[]{:S(2)}) copy-start(bf16[256,2048]{1,0:T(8,128)(2,1)S(1)} %collective-permute-done.3.cb_ref) | copy-start | bytes 3145732
  128.0 1.0 copy-start.5
  135.3 7.7 %collective-permute-start.1 = (bf16[16,512,128]{2,1,0:T(8,128)(2,1)}, bf16[16,512,128]{2,1,0:T(8,128)(2,1)S(1)}, u32[]{:S(2)}, u32[]{:S(2)}) collective-permute-start(bf16[16,512,128]{2,1,0:T(8,128)(2,1)} %get-tuple-element.32), channel_id=1, source_target_pairs={{0,1},{1,0},{2,3},{3,2},{4,5},{5,4},{6,7},{7,6},{8,9},{9,8},{10,11... | collective-permute-start | bytes 6291464 | tf_op jit(solution)/shard_map/ppermute | solution.py:366
  135.8 25.3 %all-to-all-start.3 = ((bf16[16,256,128]{2,1,0:T(8,128)(2,1)}), bf16[16,256,128]{2,1,0:T(8,128)(2,1)S(1)}, u32[]{:S(2)}, u32[]{:S(2)}) async-start(bf16[16,256,128]{2,1,0:T(8,128)(2,1)} %get-tuple-element.30), calls=%async_computation.3 | async-start | bytes 2097152 | tf_op jit(solution)/shard_map/all_to_all | solution.py:49
  143.0 1.3 copy-start.3
  161.1 34.4 %copy-start.2 = (bf16[16,256,128]{2,1,0:T(8,128)(2,1)}, bf16[16,256,128]{2,1,0:T(8,128)(2,1)S(1)}, u32[]{:S(2)}) copy-start(bf16[16,256,128]{2,1,0:T(8,128)(2,1)S(1)} %all-to-all-done.3.r_ref) | copy-start | bytes 3145732
  191.9 17.4 %all-to-all-start.5 = ((bf16[16,16,2048]{2,1,0:T(8,128)(2,1)}), bf16[16,16,2048]{2,1,0:T(8,128)(2,1)S(1)}, u32[]{:S(2)}, u32[]{:S(2)}) async-start(bf16[16,16,2048]{2,1,0:T(8,128)(2,1)} %bitcast.13), calls=%async_computation.6 | async-start | bytes 2097152 | tf_op jit(solution)/shard_map/all_to_all | solution.py:49
Sparse Core Ops, SparseCore 0:
  135.4 48.3 reduce-scatter.1

commit v3 on v2

--- a/solution.py
+++ b/solution.py
@@ -26,6 +26,8 @@
 SAME_CORE = [[2 * c + k for c in range(CHIPS)] for k in range(2)]
 CORE_SWAP = [(i, i ^ 1) for i in range(2 * CHIPS)]
 
+UNROLL = 4
+GROUP = 4
 PACK = 4
 VMEM_LIMIT = 56 * 1024 * 1024
 
@@ -122,11 +124,25 @@
 
 
 def load_pool(x_ref, y_ref, kv, qs, sems):
-    return [
-        pltpu.make_async_copy(x_ref.at[:, pl.ds(0, 2 * TOK), :], kv.at[pl.ds(0, CHIPS)], sems.at[0]),
-        pltpu.make_async_copy(y_ref.at[:, pl.ds(0, 2 * TOK), :], kv.at[pl.ds(CHIPS, CHIPS)], sems.at[1]),
-        pltpu.make_async_copy(x_ref.at[:, pl.ds(2 * TOK, TOK), :], qs, sems.at[2]),
-    ]
+    groups = []
+    for j in range(CHIPS // GROUP):
+        at = pl.ds(j * GROUP, GROUP)
+        groups.append(
+            [
+                pltpu.make_async_copy(
+                    x_ref.at[at, pl.ds(0, 2 * TOK), :], kv.at[at], sems.at[3 * j]
+                ),
+                pltpu.make_async_copy(
+                    y_ref.at[at, pl.ds(0, 2 * TOK), :],
+                    kv.at[pl.ds(CHIPS + j * GROUP, GROUP)],
+                    sems.at[3 * j + 1],
+                ),
+                pltpu.make_async_copy(
+                    x_ref.at[at, pl.ds(2 * TOK, TOK), :], qs.at[at], sems.at[3 * j + 2]
+                ),
+            ]
+        )
+    return groups
 
 
 def listed(table, c, i):
@@ -146,16 +162,17 @@
 
 
 def forward_body(table, x_ref, y_ref, o_ref, lse_ref, kv, qs, sems):
-    copies = load_pool(x_ref, y_ref, kv, qs, sems)
-    for copy in copies:
-        copy.start()
-    for copy in copies:
-        copy.wait()
+    groups = load_pool(x_ref, y_ref, kv, qs, sems)
+    for copies in groups:
+        for copy in copies:
+            copy.start()
 
     def block(c, i):
         places = listed(table, c, i)
         q = qs[c, pl.ds(i * BLK, BLK), :]
-        raw = [dot(kv[p, pl.ds(r, BLK), :], q, 1, 1) for p, r, _ in places]
+        keys = jnp.concatenate([kv[p, pl.ds(r, BLK), :] for p, r, _ in places], axis=0)
+        every = dot(keys, q, 1, 1)
+        raw = [every[s * BLK : (s + 1) * BLK, :] for s in range(1 + SLOTS)]
         raw[0] = jnp.where(causal(), raw[0], NEG)
         peak = jnp.max(raw[0], axis=0, keepdims=True)
         for (_, _, bias), s in zip(places[1:], raw[1:]):
@@ -167,13 +184,9 @@
             w = jnp.exp2(s * SCALE2 - (peak if bias is None else peak + bias))
             part = jnp.sum(w, axis=0, keepdims=True)
             total = part if total is None else total + part
-            weights.append(w)
-        inverse = 1.0 / total
-        out = None
-        for (p, r, _), w in zip(places, weights):
-            v = kv[p, pl.ds(TOK + r, BLK), :]
-            part = dot(v, (w * inverse).astype(bf16), 0, 0)
-            out = part if out is None else out + part
+            weights.append(w.astype(bf16))
+        values = jnp.concatenate([kv[p, pl.ds(TOK + r, BLK), :] for p, r, _ in places], axis=0)
+        out = dot(values, jnp.concatenate(weights, axis=0), 0, 0) * (1.0 / total)
         return out.astype(bf16), peak + jnp.log2(total)
 
     def step(c, carry):
@@ -188,7 +201,10 @@
         lse_ref[c] = jnp.where(row == 0, lses[0], lses[1])
         return carry
 
-    lax.fori_loop(0, CHIPS, step, 0)
+    for j, copies in enumerate(groups):
+        for copy in copies:
+            copy.wait()
+        lax.fori_loop(j * GROUP, (j + 1) * GROUP, step, 0, unroll=UNROLL)
 
 
 def attention_forward(table, x, y):
@@ -203,7 +219,7 @@
         scratch_shapes=[
             pltpu.VMEM((2 * CHIPS, 2 * TOK, HEAD), bf16),
             pltpu.VMEM((CHIPS, TOK, HEAD), bf16),
-            pltpu.SemaphoreType.DMA((3,)),
+            pltpu.SemaphoreType.DMA((3 * (CHIPS // GROUP),)),
         ],
         compiler_params=pltpu.CompilerParams(vmem_limit_bytes=VMEM_LIMIT),
         cost_estimate=cost(2 * PAIR_FLOPS, PAIRS, 7 * MIB),
@@ -211,77 +227,116 @@
     )(table, x, y)
 
 
-def backward_body(table, x_ref, y_ref, g_ref, lse_ref, own_ref, other_ref, gq_ref, kv, qs, acc, sems):
-    copies = load_pool(x_ref, y_ref, kv, qs, sems)
-    for copy in copies:
-        copy.start()
+def backward_body(
+    table, x_ref, y_ref, g_ref, lse_ref, home_ref, other_ref, kv, qs, gs, acck, accv, own, other, gq, sems
+):
+    groups = load_pool(x_ref, y_ref, kv, qs, sems)
+    sends = []
+    n = CHIPS // GROUP
+    for j in range(n):
+        at = pl.ds(j * GROUP, GROUP)
+        groups[j].append(pltpu.make_async_copy(g_ref.at[at], gs.at[at], sems.at[3 * n + j]))
+        sends.append(
+            [
+                pltpu.make_async_copy(
+                    gq.at[at], home_ref.at[at, pl.ds(2 * TOK, TOK), :], sems.at[4 * n + j]
+                ),
+                pltpu.make_async_copy(
+                    own.at[at], home_ref.at[at, pl.ds(0, 2 * TOK), :], sems.at[5 * n + j]
+                ),
+                pltpu.make_async_copy(other.at[at], other_ref.at[at], sems.at[6 * n + j]),
+            ]
+        )
+    for copies in groups:
+        for copy in copies:
+            copy.start()
 
     def clear(j, carry):
-        acc[j] = jnp.zeros((2 * TOK, HEAD), f32)
+        acck[CHIPS + j] = jnp.zeros((TOK, HEAD), f32)
+        accv[CHIPS + j] = jnp.zeros((TOK, HEAD), f32)
         return carry
 
-    lax.fori_loop(0, 2 * CHIPS, clear, 0)
-    for copy in copies:
-        copy.wait()
+    lax.fori_loop(0, CHIPS, clear, 0)
 
     def block(c, i):
         places = listed(table, c, i)
         q = qs[c, pl.ds(i * BLK, BLK), :]
-        g = g_ref[c, pl.ds(i * BLK, BLK), :]
+        g = gs[c, pl.ds(i * BLK, BLK), :]
         lse = lse_ref[c, i : i + 1, :]
-        probs, grads = [], []
-        row_dot = None
-        for p, r, bias in places:
-            s = dot(kv[p, pl.ds(r, BLK), :], q, 1, 1)
+        keys = jnp.concatenate([kv[p, pl.ds(r, BLK), :] for p, r, _ in places], axis=0)
+        values = jnp.concatenate([kv[p, pl.ds(TOK + r, BLK), :] for p, r, _ in places], axis=0)
+        every = dot(keys, q, 1, 1)
+        grads = dot(values, g, 1, 1)
+        probs = []
+        for j, (_, _, bias) in enumerate(places):
+            s = every[j * BLK : (j + 1) * BLK, :]
             prob = jnp.exp2(s * SCALE2 - (lse if bias is None else lse + bias))
             if bias is None:
                 prob = jnp.where(causal(), prob, 0.0)
-            grad = dot(kv[p, pl.ds(TOK + r, BLK), :], g, 1, 1)
-            part = jnp.sum(prob * grad, axis=0, keepdims=True)
-            row_dot = part if row_dot is None else row_dot + part
             probs.append(prob)
-            grads.append(grad)
-        gq = None
-        for (p, r, _), prob, grad in zip(places, probs, grads):
-            score = (prob * (grad - row_dot) * SCALE).astype(bf16)
-            acc[p, pl.ds(r, BLK), :] += dot(score, q, 1, 0)
-            acc[p, pl.ds(TOK + r, BLK), :] += dot(prob.astype(bf16), g, 1, 0)
-            part = dot(score, kv[p, pl.ds(r, BLK), :], 0, 0)
-            gq = part if gq is None else gq + part
-        gq_ref[c, pl.ds(i * BLK, BLK), :] = gq.astype(bf16)
+        prob = jnp.concatenate(probs, axis=0)
+        row_dot = jnp.sum(prob * grads, axis=0, keepdims=True)
+        score = (prob * (grads - row_dot)).astype(bf16)
+        gk = dot(score, q, 1, 0)
+        gv = dot(prob.astype(bf16), g, 1, 0)
+        for j, (p, r, _) in enumerate(places):
+            at = pl.ds(r, BLK)
+            if j == 0:
+                acck[p, at, :] = gk[0:BLK, :]
+                accv[p, at, :] = gv[0:BLK, :]
+            else:
+                acck[p, at, :] += gk[j * BLK : (j + 1) * BLK, :]
+                accv[p, at, :] += gv[j * BLK : (j + 1) * BLK, :]
+        gq[c, pl.ds(i * BLK, BLK), :] = (dot(score, keys, 0, 0) * SCALE).astype(bf16)
 
     def step(c, carry):
         for i in range(2):
             block(c, i)
         return carry
 
-    lax.fori_loop(0, CHIPS, step, 0)
-
     def flush(j, carry):
-        own_ref[j] = acc[j]
-        other_ref[j] = acc[CHIPS + j].astype(bf16)
+        own[j, 0:TOK, :] = (acck[j] * SCALE).astype(bf16)
+        own[j, TOK : 2 * TOK, :] = accv[j].astype(bf16)
+        other[j, 0:TOK, :] = (acck[CHIPS + j] * SCALE).astype(bf16)
+        other[j, TOK : 2 * TOK, :] = accv[CHIPS + j].astype(bf16)
         return carry
 
-    lax.fori_loop(0, CHIPS, flush, 0)
+    for j in range(n + 2):
+        if j < n:
+            for copy in groups[j]:
+                copy.wait()
+            lax.fori_loop(j * GROUP, (j + 1) * GROUP, step, 0, unroll=UNROLL)
+            sends[j][0].start()
+        if j >= 2:
+            lax.fori_loop((j - 2) * GROUP, (j - 1) * GROUP, flush, 0)
+            sends[j - 2][1].start()
+            sends[j - 2][2].start()
+    for copies in sends:
+        for copy in copies:
+            copy.wait()
 
 
 def attention_backward(table, x, y, g, lse):
     return pl.pallas_call(
         backward_body,
         out_shape=(
-            jax.ShapeDtypeStruct((CHIPS, 2 * TOK, HEAD), f32),
+            jax.ShapeDtypeStruct((CHIPS, 3 * TOK, HEAD), bf16),
             jax.ShapeDtypeStruct((CHIPS, 2 * TOK, HEAD), bf16),
-            jax.ShapeDtypeStruct((CHIPS, TOK, HEAD), bf16),
         ),
         in_specs=[pl.BlockSpec(memory_space=pltpu.SMEM)]
-        + [pl.BlockSpec(memory_space=pl.ANY)] * 2
-        + [pl.BlockSpec(memory_space=pltpu.VMEM)] * 2,
-        out_specs=[pl.BlockSpec(memory_space=pltpu.VMEM)] * 3,
+        + [pl.BlockSpec(memory_space=pl.ANY)] * 3
+        + [pl.BlockSpec(memory_space=pltpu.VMEM)],
+        out_specs=[pl.BlockSpec(memory_space=pl.ANY)] * 2,
         scratch_shapes=[
             pltpu.VMEM((2 * CHIPS, 2 * TOK, HEAD), bf16),
             pltpu.VMEM((CHIPS, TOK, HEAD), bf16),
-            pltpu.VMEM((2 * CHIPS, 2 * TOK, HEAD), f32),
-            pltpu.SemaphoreType.DMA((3,)),
+            pltpu.VMEM((CHIPS, TOK, HEAD), bf16),
+            pltpu.VMEM((2 * CHIPS, TOK, HEAD), f32),
+            pltpu.VMEM((2 * CHIPS, TOK, HEAD), f32),
+            pltpu.VMEM((CHIPS, 2 * TOK, HEAD), bf16),
+            pltpu.VMEM((CHIPS, 2 * TOK, HEAD), bf16),
+            pltpu.VMEM((CHIPS, TOK, HEAD), bf16),
+            pltpu.SemaphoreType.DMA((7 * (CHIPS // GROUP),)),
         ],
         compiler_params=pltpu.CompilerParams(vmem_limit_bytes=VMEM_LIMIT),
         cost_estimate=cost(5 * PAIR_FLOPS, PAIRS, 14 * MIB),
@@ -290,44 +345,43 @@
 
 
 def combine_body(own_ref, got_ref, o_ref):
-    o_ref[...] = (own_ref[...] + got_ref[...].astype(f32)).astype(bf16)
-
-
-def combine(own, got):
+    o_ref[...] = (own_ref[...].astype(f32) + got_ref[...].astype(f32)).astype(bf16)
+
+
+def combine(home, got):
     n = 4
     rows = pl.BlockSpec((n, 2 * TOK, HEAD), lambda i: (i, 0, 0))
     return pl.pallas_call(
         combine_body,
-        out_shape=jax.ShapeDtypeStruct((CHIPS, 2 * TOK, HEAD), bf16),
+        out_shape=jax.ShapeDtypeStruct((CHIPS, 3 * TOK, HEAD), bf16),
         grid=(CHIPS // n,),
         in_specs=[rows, rows],
         out_specs=rows,
-        compiler_params=pltpu.CompilerParams(vmem_limit_bytes=VMEM_LIMIT),
-        cost_estimate=cost(CHIPS * 2 * TOK * HEAD, 0, 8 * MIB),
+        input_output_aliases={0: 0},
+        compiler_params=pltpu.CompilerParams(vmem_limit_bytes=VMEM_LIMIT),
+        cost_estimate=cost(CHIPS * 2 * TOK * HEAD, 0, 6 * MIB),
         name="combine",
-    )(own, got)
+    )(home, got)
 
 
 def weight_body(core, oa_ref, ob_ref, ca_ref, cb_ref, w_ref):
-    a = oa_ref[...].reshape(4 * 64, TOK)
-    b = ob_ref[...].reshape(4 * 64, TOK)
+    a = oa_ref[...].reshape(HEADS * 64, TOK)
+    b = ob_ref[...].reshape(HEADS * 64, TOK)
     w_ref[...] = (dot(a, ca_ref[...], 1, 0) + dot(b, cb_ref[...], 1, 0)).astype(bf16)
 
 
 def weight_partial(core, oa, ob, ca, cb):
+    n = 4
+    rows = pl.BlockSpec((HEADS, 64, TOK), lambda i, core: (0, core[0], 0))
+    columns = pl.BlockSpec((TOK, D // n), lambda i, core: (0, i))
     return pl.pallas_call(
         weight_body,
         out_shape=jax.ShapeDtypeStruct((HEADS * 64, D), bf16),
         grid_spec=pltpu.PrefetchScalarGridSpec(
             num_scalar_prefetch=1,
-            grid=(HEADS // 4,),
-            in_specs=[
-                pl.BlockSpec((4, 64, TOK), lambda i, core: (i, core[0], 0)),
-                pl.BlockSpec((4, 64, TOK), lambda i, core: (i, core[0], 0)),
-                pl.BlockSpec((TOK, D), lambda i, core: (0, 0)),
-                pl.BlockSpec((TOK, D), lambda i, core: (0, 0)),
-            ],
-            out_specs=pl.BlockSpec((4 * 64, D), lambda i, core: (i, 0)),
+            grid=(n,),
+            in_specs=[rows, rows, columns, columns],
+            out_specs=pl.BlockSpec((HEADS * 64, D // n), lambda i, core: (0, i)),
         ),
         compiler_params=pltpu.CompilerParams(vmem_limit_bytes=VMEM_LIMIT),
         cost_estimate=cost(2 * TOK * D * D, 0, 8 * MIB),
@@ -350,27 +404,26 @@
     cot = cotangent[0]
     cot_other = lax.ppermute(cot, "seq", CORE_SWAP)
     x = exchange(pack(block_offsets[0], key_states[0], value_states[0], queries[0]))
-    x, g = after(x, grad_attn_by_head(cot, out_weight))
+    x, g, cot_other = after(x, grad_attn_by_head(cot, out_weight), cot_other)
     y = lax.ppermute(x, "seq", CORE_SWAP)
     g = exchange(g)
     table = block_table(x[:, RIDER, 0 : 2 * SLOTS], core)
     out, lse = attention_forward(table, x, y)
     g, out = after(g, out)
     out_home = exchange(out)
-    own, other, gq = attention_backward(table, x, y, g, lse)
-    out_home, gq, other = after(out_home, gq, other)
-    gq_home = exchange(gq)
+    own, other = attention_backward(table, x, y, g, lse)
+    out_home, own, other = after(out_home, own, other)
     out_other = lax.ppermute(out_home, "seq", CORE_SWAP)
+    out_other, other = after(out_other, other)
+    got = lax.ppermute(other, "seq", CORE_SWAP)
     partial = weight_partial(core.reshape(1), out_home, out_other, cot, cot_other)
+    partial, got = after(partial, got)
     by_doc = lax.psum_scatter(partial, "dp", scatter_dimension=0, tiled=True)
-    got = lax.ppermute(other, "seq", CORE_SWAP)
-    gq_home, gathered = after(gq_home, combine(own, got))
-    kv_home = exchange(gathered)
-    kv_home, by_doc = after(kv_home, by_doc)
+    home = exchange(combine(own, got))
+    home, by_doc = after(home, by_doc)
     pieces = exchange(by_doc.reshape(CHIPS, 16, D))
     weight_grad = jnp.sum(pieces.astype(f32), axis=0)
-    (gq,) = unpack(gq_home, 1)
-    gk, gv = unpack(kv_home, 2)
+    gk, gv, gq = unpack(home, 3)
     return gq[None], gk[None], gv[None], weight_grad
 
 

time: 218 us -> 202 us (0.927)
  Pallas kernels: 77.9 us -> 53.6 us
  blocking collectives: 30.8 us -> 47.1 us
  starting transfers between devices: 35.5 us -> 24.1 us
  waiting for transfers between devices: 54.6 us -> 58 us
    all_to_all x1, blocking collectives: 30.8 us -> 47.1 us  [exchange(): lax.all_to_all(x, 'seq', 0, 0, axis_index_groups=SAME_CORE, tiled=True)]
    pallas_call x1, Pallas kernels: 19.2 us -> 7.87 us  [attention_forward(): pl.pallas_call(forward_body, out_shape=(jax.ShapeDtypeStruct((CHIPS, HEAD...]
    all_to_all x5 -> x4, starting transfers between devices: 34.3 us -> 23.6 us  [exchange(): lax.all_to_all(x, 'seq', 0, 0, axis_index_groups=SAME_CORE, tiled=True)]
    pallas_call x2, Pallas kernels: 31.9 us -> 22.2 us  [the longest x1 17.9 us: attention_backward(): pl.pallas_call(backward_body, out_shape=(jax.ShapeDtypeStruct((CHIPS, 3 *...]
    all_to_all x5 -> x4, waiting for transfers between devices: 52.3 us -> 55.3 us  [exchange(): lax.all_to_all(x, 'seq', 0, 0, axis_index_groups=SAME_CORE, tiled=True)]
    pallas_call x2 -> x1, Pallas kernels: 7.3 us -> 4.36 us  [unpack(): pl.pallas_call(unpack_body, out_shape=(out,) * n, grid=(HEADS // PACK,),...]
  transfers between devices with their start and end apart: 10 -> 9, of which waited for: 4 -> 4; matrix products, arithmetic and copies ran while one was open for 0% -> 0% of each run, Pallas kernels for 31% -> 25%
where the time goes in v3:
time: 202 us; the launch traced here: 201 us
  waiting for transfers between devices  58 us (29%)
  Pallas kernels  53.6 us (27%)
  blocking collectives  47.1 us (23%)
  starting transfers between devices  24.1 us (12%)
  between operations  14.2 us (7%)
  local copies, waits for them, and re-layouts  2.3 us (1%)
    all_to_all x4, waiting for transfers between devices, exchange(): lax.all_to_all(x, 'seq', 0, 0, axis_index_groups=SAME_CORE, tiled=True)  55.3 us
    all_to_all x1, blocking collectives, exchange(): lax.all_to_all(x, 'seq', 0, 0, axis_index_groups=SAME_CORE, tiled=True)  47.1 us
    all_to_all x4, starting transfers between devices, exchange(): lax.all_to_all(x, 'seq', 0, 0, axis_index_groups=SAME_CORE, tiled=True)  23.6 us
    pallas_call x1, Pallas kernels, attention_backward(): pl.pallas_call(backward_body, out_shape=(jax.ShapeDtypeStruct((CHIPS, 3 *...  17.9 us
    pallas_call x1, Pallas kernels, grad_attn_by_head(): pl.pallas_call(grad_attn_body, out_shape=jax.ShapeDtypeStruct((HEADS, TOK...  8.78 us
    pallas_call x1, Pallas kernels, attention_forward(): pl.pallas_call(forward_body, out_shape=(jax.ShapeDtypeStruct((CHIPS, HEAD...  7.87 us
    pallas_call x1, Pallas kernels, weight_partial(): pl.pallas_call(weight_body, out_shape=jax.ShapeDtypeStruct((HEADS * 64, D...  6.01 us
    pallas_call x1, Pallas kernels, combine(): pl.pallas_call(combine_body, out_shape=jax.ShapeDtypeStruct((CHIPS, 3 * T...  4.38 us
  transfers between devices with their start and end apart: 9, of which 4 were waited for; matrix products, arithmetic and copies ran while one was open for 0% of the time, Pallas kernels for 25%

profile of v3, /device:TPU:0, one launch (start us, length us, event | category | flops | bytes accessed | tf_op | source)
XLA Modules:
  0.0 200.9 jit_solution(2513564006507031310)
XLA Ops:
  7.2 4.4 %pack.1 = bf16[16,776,128]{2,1,0:T(8,128)(2,1)} custom-call(s32[2,4]{1,0:T(2,128)} %bitcast.17, bf16[256,2048]{1,0:T(8,128)(2,1)} %bitcast.14, bf16[256,2048]{1,0:T(8,128)(2,1)} %bitcast.15, bf16[256,2048]{1,0:T(8,128)(2,1)} %bitcast.16), custom_call_target="tpu_custom_call" | custom-call | tf_op jit(solution)/shard_map/pack/pallas_call | solution.py:72
  11.5 8.1 %all-to-all-start = ((bf16[16,776,128]{2,1,0:T(8,128)(2,1)}), bf16[16,776,128]{2,1,0:T(8,128)(2,1)S(1)}, u32[]{:S(2)}, u32[]{:S(2)}) async-start(bf16[16,776,128]{2,1,0:T(8,128)(2,1)} %pack.1), calls=%async_computation | async-start | bytes 6356992 | tf_op jit(solution)/shard_map/all_to_all | solution.py:51
  19.7 0.1 collective-permute-start
  19.8 8.8 %grad_attn.1 = bf16[16,256,128]{2,1,0:T(8,128)(2,1)} custom-call(bf16[256,2048]{1,0:T(8,128)(2,1)} %bitcast.11, bf16[2048,2048]{1,0:T(8,128)(2,1)} %w_ref.1), custom_call_target="tpu_custom_call" | custom-call | flops 2147483648 | bytes 10485760 | tf_op jit(solution)/shard_map/grad_attn/pallas_call | solution.py:111
  28.6 0.0 collective-permute-done.cb_ref
  28.6 33.9 %all-to-all-done.x_ref = bf16[16,776,128]{2,1,0:T(8,128)(2,1)S(1)} async-done(((bf16[16,776,128]{2,1,0:T(8,128)(2,1)}), bf16[16,776,128]{2,1,0:T(8,128)(2,1)S(1)}, u32[]{:S(2)}, u32[]{:S(2)}) %all-to-all-start) | async-done | bytes 3178528 | tf_op jit(solution)/shard_map/all_to_all | solution.py:51
  62.5 0.0 copy-start
  62.5 0.0 collective-permute-start.1
  62.5 8.1 %all-to-all-start.1 = ((bf16[16,256,128]{2,1,0:T(8,128)(2,1)}), bf16[16,256,128]{2,1,0:T(8,128)(2,1)}, u32[]{:S(2)}, u32[]{:S(2)}) async-start(bf16[16,256,128]{2,1,0:T(8,128)(2,1)} %grad_attn.1), calls=%async_computation.1 | async-start | bytes 2097152 | tf_op jit(solution)/shard_map/all_to_all | solution.py:51
  70.7 0.1 iota_add_fusion
  70.7 0.1 add.52
  70.9 0.1 reshape.51
  70.9 0.7 add_select_fusion.table
  71.6 0.0 collective-permute-done.1.y_ref
  71.6 0.0 copy-done
  71.6 7.9 %attn_fwd.1 = (bf16[16,128,256]{2,1,0:T(8,128)(2,1)}, f32[16,8,128]{2,1,0:T(8,128)}) custom-call(s32[32,4]{1,0:T(8,128)} %add_select_fusion.table, bf16[16,776,128]{2,1,0:T(8,128)(2,1)} %copy-done, bf16[16,776,128]{2,1,0:T(8,128)(2,1)} %collective-permute-done.1.y_ref), custom_call_target="tpu_custom_call" | custom-call | flops 1342177280 | bytes 7340032 | tf_op jit(solution)/shard_map/attn_fwd/pallas_call | solution.py:211
  79.5 9.7 %all-to-all-done.1.g_ref = bf16[16,256,128]{2,1,0:T(8,128)(2,1)} async-done(((bf16[16,256,128]{2,1,0:T(8,128)(2,1)}), bf16[16,256,128]{2,1,0:T(8,128)(2,1)}, u32[]{:S(2)}, u32[]{:S(2)}) %all-to-all-start.1) | async-done | bytes 1048608 | tf_op jit(solution)/shard_map/all_to_all | solution.py:51
  89.2 3.7 %all-to-all-start.2 = ((bf16[16,128,256]{2,1,0:T(8,128)(2,1)}), bf16[16,128,256]{2,1,0:T(8,128)(2,1)S(1)}, u32[]{:S(2)}, u32[]{:S(2)}) async-start(bf16[16,128,256]{2,1,0:T(8,128)(2,1)} %get-tuple-element.28), calls=%async_computation.2 | async-start | bytes 2097152 | tf_op jit(solution)/shard_map/all_to_all | solution.py:51
  92.8 0.2 reduce-scatter.2.cloned.1.call-start
  93.1 17.9 %attn_bwd.1 = (bf16[16,768,128]{2,1,0:T(8,128)(2,1)}, bf16[16,512,128]{2,1,0:T(8,128)(2,1)}) custom-call(s32[32,4]{1,0:T(8,128)} %add_select_fusion.table, bf16[16,776,128]{2,1,0:T(8,128)(2,1)} %copy-done, bf16[16,776,128]{2,1,0:T(8,128)(2,1)} %collective-permute-done.1.y_ref, bf16[16,256,128]{2,1,0:T(8,128)(2,1)} %all-to-all-done.1.g_ref, ...), custom_call_target="tpu_custom_call" | custom-call | flops 3355443200 | bytes 14680064 | tf_op jit(solution)/shard_map/attn_bwd/pallas_call | solution.py:320
  110.9 0.0 all-to-all-done.2.oa_ref
  110.9 0.0 copy-start.1
  111.0 0.1 collective-permute-start.2
  111.1 2.6 %collective-permute-done.2.ob_ref = bf16[16,128,256]{2,1,0:T(8,128)(2,1)S(1)} collective-permute-done((bf16[16,128,256]{2,1,0:T(8,128)(2,1)S(1)}, bf16[16,128,256]{2,1,0:T(8,128)(2,1)S(1)}, u32[]{:S(2)}, u32[]{:S(2)}) %collective-permute-start.2) | collective-permute-done | bytes 1048608 | tf_op jit(solution)/shard_map/ppermute | solution.py:416
  113.7 0.0 copy-start.3
  113.7 0.1 collective-permute-start.3
  113.8 0.0 copy-done.1
  113.8 0.8 copy-done.3
  114.7 6.0 %weight_partial.1 = bf16[1024,2048]{1,0:T(8,128)(2,1)} custom-call(s32[1]{0:T(128)} %bitcast.5.core, bf16[16,128,256]{2,1,0:T(8,128)(2,1)} %copy-done.1, bf16[16,128,256]{2,1,0:T(8,128)(2,1)} %copy-done.3, bf16[256,2048]{1,0:T(8,128)(2,1)} %bitcast.12, bf16[256,2048]{1,0:T(8,128)(2,1)} %collective-permute-done.cb_ref), custom_call_target="tpu_custom_call" | custom-call | flops 2147483648 | bytes 8388608 | tf_op jit(solution)/shard_map/weight_partial/pallas_call | solution.py:377
  120.7 0.0 collective-permute-done.3.got_ref
  120.7 0.0 copy-start.2
  120.7 0.0 reduce-scatter.2.cloned.1.call-update
  120.7 1.3 copy-done.2
  122.0 4.4 %combine.1 = bf16[16,768,128]{2,1,0:T(8,128)(2,1)} custom-call(bf16[16,768,128]{2,1,0:T(8,128)(2,1)} %get-tuple-element.33.own_ref, bf16[16,512,128]{2,1,0:T(8,128)(2,1)} %copy-done.2), custom_call_target="tpu_custom_call", output_to_operand_aliasing={{}: (0, {})} | custom-call | flops 1048576 | bytes 6291456 | tf_op jit(solution)/shard_map/combine/pallas_call | solution.py:354
  126.4 47.1 %all_to_all.25.r_ref = bf16[16,768,128]{2,1,0:T(8,128)(2,1)} all-to-all(bf16[16,768,128]{2,1,0:T(8,128)(2,1)} %combine.1), channel_id=1, replica_groups={{0,2,4,6,8,10,12,14,16,18,20,22,24,26,28,30},{1,3,5,7,9,11,13,15,17,19,..., dimensions={0} | all-to-all | bytes 6291456 | tf_op jit(solution)/shard_map/all_to_all | solution.py:51
  173.5 0.0 reduce-scatter.2.cloned.1.call-done
  173.5 3.7 %all-to-all-start.4 = ((bf16[16,16,2048]{2,1,0:T(8,128)(2,1)}), bf16[16,16,2048]{2,1,0:T(8,128)(2,1)S(1)}, u32[]{:S(2)}, u32[]{:S(2)}) async-start(bf16[16,16,2048]{2,1,0:T(8,128)(2,1)} %bitcast.13), calls=%async_computation.5 | async-start | bytes 2097152 | tf_op jit(solution)/shard_map/all_to_all | solution.py:51
  177.2 4.4 %unpack.1 = (bf16[256,2048]{1,0:T(8,128)(2,1)}, bf16[256,2048]{1,0:T(8,128)(2,1)}, bf16[256,2048]{1,0:T(8,128)(2,1)}) custom-call(bf16[16,768,128]{2,1,0:T(8,128)(2,1)} %all_to_all.25.r_ref), custom_call_target="tpu_custom_call" | custom-call | bytes 6291456 | tf_op jit(solution)/shard_map/unpack/pallas_call | solution.py:92
  181.5 11.7 %all-to-all-done.4 = bf16[16,16,2048]{2,1,0:T(8,128)(2,1)S(1)} async-done(((bf16[16,16,2048]{2,1,0:T(8,128)(2,1)}), bf16[16,16,2048]{2,1,0:T(8,128)(2,1)S(1)}, u32[]{:S(2)}, u32[]{:S(2)}) %all-to-all-start.4) | async-done | bytes 1048608 | tf_op jit(solution)/shard_map/all_to_all | solution.py:51
  193.3 0.8 convert_reduce_fusion
  (2 shorter events, 0.0 us)
Async XLA Ops:
  11.5 51.0 %all-to-all-start = ((bf16[16,776,128]{2,1,0:T(8,128)(2,1)}), bf16[16,776,128]{2,1,0:T(8,128)(2,1)S(1)}, u32[]{:S(2)}, u32[]{:S(2)}) async-start(bf16[16,776,128]{2,1,0:T(8,128)(2,1)} %pack.1), calls=%async_computation | async-start | bytes 6356992 | tf_op jit(solution)/shard_map/all_to_all | solution.py:51
  19.7 8.9 %collective-permute-start = (bf16[256,2048]{1,0:T(8,128)(2,1)}, bf16[256,2048]{1,0:T(8,128)(2,1)}, u32[]{:S(2)}, u32[]{:S(2)}) collective-permute-start(bf16[256,2048]{1,0:T(8,128)(2,1)} %bitcast.10), channel_id=1, source_target_pairs={{0,1},{1,0},{2,3},{3,2},{4,5},{5,4},{6,7},{7,6},{8,9},{9,8},{10,11... | collective-permute-start | bytes 3145736 | tf_op jit(solution)/shard_map/ppermute | solution.py:405
  62.5 9.1 %copy-start = (bf16[16,776,128]{2,1,0:T(8,128)(2,1)}, bf16[16,776,128]{2,1,0:T(8,128)(2,1)S(1)}, u32[]{:S(2)}) copy-start(bf16[16,776,128]{2,1,0:T(8,128)(2,1)S(1)} %all-to-all-done.x_ref) | copy-start | bytes 9535492
  62.5 9.1 %collective-permute-start.1 = (bf16[16,776,128]{2,1,0:T(8,128)(2,1)S(1)}, bf16[16,776,128]{2,1,0:T(8,128)(2,1)}, u32[]{:S(2)}, u32[]{:S(2)}) collective-permute-start(bf16[16,776,128]{2,1,0:T(8,128)(2,1)S(1)} %all-to-all-done.x_ref), channel_id=1, source_target_pairs={{0,1},{1,0},{2,3},{3,2},{4,5},{5,4},{6,7},{7,6},{8,9},{9,8},{10,11... | collective-permute-start | bytes 9535496 | tf_op jit(solution)/shard_map/ppermute | solution.py:408
  62.5 26.7 %all-to-all-start.1 = ((bf16[16,256,128]{2,1,0:T(8,128)(2,1)}), bf16[16,256,128]{2,1,0:T(8,128)(2,1)}, u32[]{:S(2)}, u32[]{:S(2)}) async-start(bf16[16,256,128]{2,1,0:T(8,128)(2,1)} %grad_attn.1), calls=%async_computation.1 | async-start | bytes 2097152 | tf_op jit(solution)/shard_map/all_to_all | solution.py:51
  89.2 21.8 %all-to-all-start.2 = ((bf16[16,128,256]{2,1,0:T(8,128)(2,1)}), bf16[16,128,256]{2,1,0:T(8,128)(2,1)S(1)}, u32[]{:S(2)}, u32[]{:S(2)}) async-start(bf16[16,128,256]{2,1,0:T(8,128)(2,1)} %get-tuple-element.28), calls=%async_computation.2 | async-start | bytes 2097152 | tf_op jit(solution)/shard_map/all_to_all | solution.py:51
  92.8 80.7 %reduce-scatter.2.cloned.1.call-start = ((), (), s32[]{:S(2)}) async-start(), calls=%async_computation.6 | async-start | bytes 5242880 | tf_op jit(solution)/shard_map/reduce_scatter | solution.py:421
  110.9 2.9 %copy-start.1 = (bf16[16,128,256]{2,1,0:T(8,128)(2,1)}, bf16[16,128,256]{2,1,0:T(8,128)(2,1)S(1)}, u32[]{:S(2)}) copy-start(bf16[16,128,256]{2,1,0:T(8,128)(2,1)S(1)} %all-to-all-done.2.oa_ref) | copy-start | bytes 3145732
  111.0 2.7 %collective-permute-start.2 = (bf16[16,128,256]{2,1,0:T(8,128)(2,1)S(1)}, bf16[16,128,256]{2,1,0:T(8,128)(2,1)S(1)}, u32[]{:S(2)}, u32[]{:S(2)}) collective-permute-start(bf16[16,128,256]{2,1,0:T(8,128)(2,1)S(1)} %all-to-all-done.2.oa_ref), channel_id=1, source_target_pairs={{0,1},{1,0},{2,3},{3,2},{4,5},{5,4},{6,7},{7,6},{8,9},{9,8},{10,11... | collective-permute-start | bytes 3145736 | tf_op jit(solution)/shard_map/ppermute | solution.py:416
  113.7 1.0 copy-start.3
  113.7 7.0 %collective-permute-start.3 = (bf16[16,512,128]{2,1,0:T(8,128)(2,1)}, bf16[16,512,128]{2,1,0:T(8,128)(2,1)S(1)}, u32[]{:S(2)}, u32[]{:S(2)}) collective-permute-start(bf16[16,512,128]{2,1,0:T(8,128)(2,1)} %get-tuple-element.38), channel_id=1, source_target_pairs={{0,1},{1,0},{2,3},{3,2},{4,5},{5,4},{6,7},{7,6},{8,9},{9,8},{10,11... | collective-permute-start | bytes 6291464 | tf_op jit(solution)/shard_map/ppermute | solution.py:418
  120.7 1.3 copy-start.2
  173.5 19.7 %all-to-all-start.4 = ((bf16[16,16,2048]{2,1,0:T(8,128)(2,1)}), bf16[16,16,2048]{2,1,0:T(8,128)(2,1)S(1)}, u32[]{:S(2)}, u32[]{:S(2)}) async-start(bf16[16,16,2048]{2,1,0:T(8,128)(2,1)} %bitcast.13), calls=%async_computation.5 | async-start | bytes 2097152 | tf_op jit(solution)/shard_map/all_to_all | solution.py:51
Sparse Core Ops, SparseCore 0:
  120.8 48.2 reduce-scatter.1

commit v4 on v3

--- a/solution.py
+++ b/solution.py
@@ -15,6 +15,8 @@
 TOK = 256
 CHIPS = 16
 BLOCKS = 64
+DOCS = 4
+CHUNK = D // 4 // DOCS
 RIDER = 3 * TOK
 ROWS = 3 * TOK + 8
 SCALE = HEAD ** (-0.5)
@@ -364,29 +366,61 @@
     )(home, got)
 
 
-def weight_body(core, oa_ref, ob_ref, ca_ref, cb_ref, w_ref):
-    a = oa_ref[...].reshape(HEADS * 64, TOK)
-    b = ob_ref[...].reshape(HEADS * 64, TOK)
-    w_ref[...] = (dot(a, ca_ref[...], 1, 0) + dot(b, cb_ref[...], 1, 0)).astype(bf16)
-
-
-def weight_partial(core, oa, ob, ca, cb):
-    n = 4
-    rows = pl.BlockSpec((HEADS, 64, TOK), lambda i, core: (0, core[0], 0))
-    columns = pl.BlockSpec((TOK, D // n), lambda i, core: (0, i))
-    return pl.pallas_call(
+def weight_body(place, oa_ref, ob_ref, ca_ref, cb_ref, *rest):
+    outs, buf, sems = rest[: 2 * DOCS], rest[2 * DOCS], rest[2 * DOCS + 1]
+    copies = []
+    for d in (3, 1, 2, 0):
+        heads = pl.ds(((place[1] + d) % DOCS) * (HEADS // DOCS), HEADS // DOCS)
+        a = oa_ref[heads].reshape(2 * CHUNK, TOK)
+        b = ob_ref[heads].reshape(2 * CHUNK, TOK)
+        buf[d] = (dot(a, ca_ref[...], 1, 0) + dot(b, cb_ref[...], 1, 0)).astype(bf16)
+        for half in range(2):
+            j = 2 * d + half
+            copies.append(
+                pltpu.make_async_copy(
+                    buf.at[d, pl.ds(half * CHUNK, CHUNK), :], outs[j], sems.at[j]
+                )
+            )
+            copies[-1].start()
+    for copy in copies:
+        copy.wait()
+
+
+def weight_partial(place, oa, ob, ca, cb):
+    rows = pl.BlockSpec((HEADS, 64, TOK), lambda i, place: (0, place[0], 0))
+    whole = pl.BlockSpec((TOK, D), lambda i, place: (0, 0))
+    outs = pl.pallas_call(
         weight_body,
-        out_shape=jax.ShapeDtypeStruct((HEADS * 64, D), bf16),
+        out_shape=(jax.ShapeDtypeStruct((CHUNK, D), bf16),) * (2 * DOCS),
         grid_spec=pltpu.PrefetchScalarGridSpec(
             num_scalar_prefetch=1,
-            grid=(n,),
-            in_specs=[rows, rows, columns, columns],
-            out_specs=pl.BlockSpec((HEADS * 64, D // n), lambda i, core: (0, i)),
+            grid=(1,),
+            in_specs=[rows, rows, whole, whole],
+            out_specs=[pl.BlockSpec(memory_space=pl.ANY)] * (2 * DOCS),
+            scratch_shapes=[
+                pltpu.VMEM((DOCS, 2 * CHUNK, D), bf16),
+                pltpu.SemaphoreType.DMA((2 * DOCS,)),
+            ],
         ),
         compiler_params=pltpu.CompilerParams(vmem_limit_bytes=VMEM_LIMIT),
         cost_estimate=cost(2 * TOK * D * D, 0, 8 * MIB),
         name="weight_partial",
-    )(core, oa, ob, ca, cb)
+    )(place, oa, ob, ca, cb)
+    return outs[0::2], outs[1::2]
+
+
+def plus(a, b):
+    return (a.astype(f32) + b.astype(f32)).astype(bf16)
+
+
+def sum_over_docs(up, down):
+    route_up = [(i, (i + 1) % DOCS) for i in range(DOCS)]
+    route_down = [(i, (i - 1) % DOCS) for i in range(DOCS)]
+    a, b = up[3], down[1]
+    for step in range(1, DOCS):
+        a = plus(lax.ppermute(a, "dp", route_up), up[3 - step])
+        b = plus(lax.ppermute(b, "dp", route_down), down[(1 + step) % DOCS])
+    return a, b
 
 
 def block_table(rider, core):
@@ -416,12 +450,15 @@
     out_other = lax.ppermute(out_home, "seq", CORE_SWAP)
     out_other, other = after(out_other, other)
     got = lax.ppermute(other, "seq", CORE_SWAP)
-    partial = weight_partial(core.reshape(1), out_home, out_other, cot, cot_other)
-    partial, got = after(partial, got)
-    by_doc = lax.psum_scatter(partial, "dp", scatter_dimension=0, tiled=True)
+    place = jnp.stack([core, lax.axis_index("dp")])
+    partial = weight_partial(place, out_home, out_other, cot, cot_other)
+    up, down = partial
+    *up, got = after(*up, got)
+    sums = sum_over_docs(up, down)
     home = exchange(combine(own, got))
-    home, by_doc = after(home, by_doc)
-    pieces = exchange(by_doc.reshape(CHIPS, 16, D))
+    home, *sums = after(home, *sums)
+    by_doc = jnp.concatenate([part.reshape(CHIPS // 2, 16, D) for part in sums], axis=0)
+    pieces = exchange(by_doc)
     weight_grad = jnp.sum(pieces.astype(f32), axis=0)
     gk, gv, gq = unpack(home, 3)
     return gq[None], gk[None], gv[None], weight_grad

time: 202 us -> 205 us (1.015)
  blocking collectives: 47.1 us -> 0 us
  waiting for transfers between devices: 58 us -> 88.7 us
  starting transfers between devices: 24.1 us -> 47 us
  between operations: 14.2 us -> 0.87 us
  other arithmetic: 1.6 us -> 11.3 us
    all_to_all x1 -> x0, blocking collectives: 47.1 us -> none  [exchange(): lax.all_to_all(x, 'seq', 0, 0, axis_index_groups=SAME_CORE, tiled=True)]
    ppermute x0 -> x6, waiting for transfers between devices: none -> 22.9 us  [the longest x3 18.3 us: sum_over_docs(): b = plus(lax.ppermute(b, 'dp', route_down), down[(1 + step) % DOCS])]
    all_to_all x4 -> x5, starting transfers between devices: 23.6 us -> 37 us  [exchange(): lax.all_to_all(x, 'seq', 0, 0, axis_index_groups=SAME_CORE, tiled=True)]
    ppermute x0 -> x6, starting transfers between devices: none -> 9.77 us  [the longest x3 9.62 us: sum_over_docs(): b = plus(lax.ppermute(b, 'dp', route_down), down[(1 + step) % DOCS])]
    all_to_all x4 -> x5, waiting for transfers between devices: 55.3 us -> 63.2 us  [exchange(): lax.all_to_all(x, 'seq', 0, 0, axis_index_groups=SAME_CORE, tiled=True)]
    convert_element_type x0 -> x6, other arithmetic: none -> 4.86 us  [plus(): return (a.astype(f32) + b.astype(f32)).astype(bf16)]
    concatenate x0 -> x1, other arithmetic: none -> 3.05 us  [local(): jnp.concatenate([part.reshape(CHIPS // 2, 16, D) for part in sums], axis=0)]
  transfers between devices with their start and end apart: 9 -> 15, of which waited for: 4 -> 9; matrix products, arithmetic and copies ran while one was open for 0% -> 3% of each run, Pallas kernels for 25% -> 24%
where the time goes in v4:
time: 205 us; the launch traced here: 204 us
  waiting for transfers between devices  88.7 us (43%)
  Pallas kernels  53.5 us (26%)
  starting transfers between devices  47 us (23%)
  other arithmetic  11.3 us (6%)
  local copies, waits for them, and re-layouts  2.49 us (1%)
    all_to_all x5, waiting for transfers between devices, exchange(): lax.all_to_all(x, 'seq', 0, 0, axis_index_groups=SAME_CORE, tiled=True)  63.2 us
    all_to_all x5, starting transfers between devices, exchange(): lax.all_to_all(x, 'seq', 0, 0, axis_index_groups=SAME_CORE, tiled=True)  37 us
    ppermute x3, waiting for transfers between devices, sum_over_docs(): b = plus(lax.ppermute(b, 'dp', route_down), down[(1 + step) % DOCS])  18.3 us
    pallas_call x1, Pallas kernels, attention_backward(): pl.pallas_call(backward_body, out_shape=(jax.ShapeDtypeStruct((CHIPS, 3 *...  17.9 us
    ppermute x3, starting transfers between devices, sum_over_docs(): b = plus(lax.ppermute(b, 'dp', route_down), down[(1 + step) % DOCS])  9.62 us
    pallas_call x1, Pallas kernels, grad_attn_by_head(): pl.pallas_call(grad_attn_body, out_shape=jax.ShapeDtypeStruct((HEADS, TOK...  8.78 us
    pallas_call x1, Pallas kernels, attention_forward(): pl.pallas_call(forward_body, out_shape=(jax.ShapeDtypeStruct((CHIPS, HEAD...  7.87 us
    pallas_call x1, Pallas kernels, weight_partial(): pl.pallas_call(weight_body, out_shape=(jax.ShapeDtypeStruct((CHUNK, D), b...  5.92 us
  transfers between devices with their start and end apart: 15, of which 9 were waited for; matrix products, arithmetic and copies ran while one was open for 3% of the time, Pallas kernels for 24%

profile of v4, /device:TPU:0, one launch (start us, length us, event | category | flops | bytes accessed | tf_op | source)
XLA Modules:
  0.0 204.0 jit_solution(17251169404818520378)
XLA Ops:
  0.6 4.4 %pack.1 = bf16[16,776,128]{2,1,0:T(8,128)(2,1)} custom-call(s32[2,4]{1,0:T(2,128)} %bitcast.20, bf16[256,2048]{1,0:T(8,128)(2,1)} %bitcast.17, bf16[256,2048]{1,0:T(8,128)(2,1)} %bitcast.18, bf16[256,2048]{1,0:T(8,128)(2,1)} %bitcast.19), custom_call_target="tpu_custom_call" | custom-call | tf_op jit(solution)/shard_map/pack/pallas_call | solution.py:74
  5.0 8.1 %all-to-all-start = ((bf16[16,776,128]{2,1,0:T(8,128)(2,1)}), bf16[16,776,128]{2,1,0:T(8,128)(2,1)S(1)}, u32[]{:S(2)}, u32[]{:S(2)}) async-start(bf16[16,776,128]{2,1,0:T(8,128)(2,1)} %pack.1), calls=%async_computation | async-start | bytes 6356992 | tf_op jit(solution)/shard_map/all_to_all | solution.py:53
  13.1 0.1 collective-permute-start
  13.2 8.8 %grad_attn.1 = bf16[16,256,128]{2,1,0:T(8,128)(2,1)} custom-call(bf16[256,2048]{1,0:T(8,128)(2,1)} %bitcast.15, bf16[2048,2048]{1,0:T(8,128)(2,1)} %w_ref.1), custom_call_target="tpu_custom_call" | custom-call | flops 2147483648 | bytes 10485760 | tf_op jit(solution)/shard_map/grad_attn/pallas_call | solution.py:113
  22.0 0.0 collective-permute-done.cb_ref
  22.0 33.9 %all-to-all-done.x_ref = bf16[16,776,128]{2,1,0:T(8,128)(2,1)S(1)} async-done(((bf16[16,776,128]{2,1,0:T(8,128)(2,1)}), bf16[16,776,128]{2,1,0:T(8,128)(2,1)S(1)}, u32[]{:S(2)}, u32[]{:S(2)}) %all-to-all-start) | async-done | bytes 3178528 | tf_op jit(solution)/shard_map/all_to_all | solution.py:53
  56.0 0.0 collective-permute-start.1
  56.0 8.1 %all-to-all-start.1 = ((bf16[16,256,128]{2,1,0:T(8,128)(2,1)}), bf16[16,256,128]{2,1,0:T(8,128)(2,1)}, u32[]{:S(2)}, u32[]{:S(2)}) async-start(bf16[16,256,128]{2,1,0:T(8,128)(2,1)} %grad_attn.1), calls=%async_computation.1 | async-start | bytes 2097152 | tf_op jit(solution)/shard_map/all_to_all | solution.py:53
  64.1 0.1 iota_add_fusion
  64.2 0.1 add.68
  64.3 0.1 reshape.51
  64.4 0.7 add_select_fusion.table
  65.1 7.9 %attn_fwd.1 = (bf16[16,128,256]{2,1,0:T(8,128)(2,1)}, f32[16,8,128]{2,1,0:T(8,128)}) custom-call(s32[32,4]{1,0:T(8,128)} %add_select_fusion.table, bf16[16,776,128]{2,1,0:T(8,128)(2,1)} %copy-done, bf16[16,776,128]{2,1,0:T(8,128)(2,1)} %collective-permute-done.1.y_ref), custom_call_target="tpu_custom_call" | custom-call | flops 1342177280 | bytes 7340032 | tf_op jit(solution)/shard_map/attn_fwd/pallas_call | solution.py:213
  73.0 9.7 %all-to-all-done.1.g_ref = bf16[16,256,128]{2,1,0:T(8,128)(2,1)} async-done(((bf16[16,256,128]{2,1,0:T(8,128)(2,1)}), bf16[16,256,128]{2,1,0:T(8,128)(2,1)}, u32[]{:S(2)}, u32[]{:S(2)}) %all-to-all-start.1) | async-done | bytes 1048608 | tf_op jit(solution)/shard_map/all_to_all | solution.py:53
  82.6 3.8 %all-to-all-start.2 = ((bf16[16,128,256]{2,1,0:T(8,128)(2,1)}), bf16[16,128,256]{2,1,0:T(8,128)(2,1)S(1)}, u32[]{:S(2)}, u32[]{:S(2)}) async-start(bf16[16,128,256]{2,1,0:T(8,128)(2,1)} %get-tuple-element.40), calls=%async_computation.2 | async-start | bytes 2097152 | tf_op jit(solution)/shard_map/all_to_all | solution.py:53
  86.5 17.9 %attn_bwd.1 = (bf16[16,768,128]{2,1,0:T(8,128)(2,1)}, bf16[16,512,128]{2,1,0:T(8,128)(2,1)}) custom-call(s32[32,4]{1,0:T(8,128)} %add_select_fusion.table, bf16[16,776,128]{2,1,0:T(8,128)(2,1)} %copy-done, bf16[16,776,128]{2,1,0:T(8,128)(2,1)} %collective-permute-done.1.y_ref, bf16[16,256,128]{2,1,0:T(8,128)(2,1)} %all-to-all-done.1.g_ref, ...), custom_call_target="tpu_custom_call" | custom-call | flops 3355443200 | bytes 14680064 | tf_op jit(solution)/shard_map/attn_bwd/pallas_call | solution.py:322
  104.4 0.0 copy-start.3
  104.4 0.1 collective-permute-start.2
  104.5 2.6 %collective-permute-done.2.ob_ref = bf16[16,128,256]{2,1,0:T(8,128)(2,1)S(1)} collective-permute-done((bf16[16,128,256]{2,1,0:T(8,128)(2,1)S(1)}, bf16[16,128,256]{2,1,0:T(8,128)(2,1)S(1)}, u32[]{:S(2)}, u32[]{:S(2)}) %collective-permute-start.2) | collective-permute-done | bytes 1048608 | tf_op jit(solution)/shard_map/ppermute | solution.py:450
  107.1 1.0 copy-done.8
  108.1 0.1 collective-permute-start.3
  108.2 0.6 pad_add_fusion.place
  108.8 5.9 %weight_partial.1 = (bf16[128,2048]{1,0:T(8,128)(2,1)}, bf16[128,2048]{1,0:T(8,128)(2,1)}, bf16[128,2048]{1,0:T(8,128)(2,1)}, bf16[128,2048]{1,0:T(8,128)(2,1)},...) custom-call(s32[2]{0:T(128)} %pad_add_fusion.place, ...), custom_call_target="tpu_custom_call" | custom-call | flops 2147483648 | bytes 8388608 | tf_op jit(solution)/shard_map/weight_partial/pallas_call | solution.py:392
  114.8 2.8 %collective-permute-start.7 = (bf16[128,2048]{1,0:T(8,128)(2,1)}, bf16[128,2048]{1,0:T(8,128)(2,1)}, u32[]{:S(2)}, u32[]{:S(2)}) collective-permute-start(bf16[128,2048]{1,0:T(8,128)(2,1)} %get-tuple-element.60), channel_id=1, source_target_pairs={{0,96},{32,0},{64,32},{96,64},{1,97},{33,1},{65,33},{97,65},{2,98}... | collective-permute-start | bytes 1572872 | tf_op jit(solution)/shard_map/ppermute | solution.py:422
  117.6 1.3 copy-done.2
  118.9 4.4 %combine.1 = bf16[16,768,128]{2,1,0:T(8,128)(2,1)} custom-call(bf16[16,768,128]{2,1,0:T(8,128)(2,1)} %get-tuple-element.45.own_ref, bf16[16,512,128]{2,1,0:T(8,128)(2,1)} %copy-done.2), custom_call_target="tpu_custom_call", output_to_operand_aliasing={{}: (0, {})} | custom-call | flops 1048576 | bytes 6291456 | tf_op jit(solution)/shard_map/combine/pallas_call | solution.py:356
  123.3 7.0 %all-to-all-start.3 = ((bf16[16,768,128]{2,1,0:T(8,128)(2,1)}), bf16[16,768,128]{2,1,0:T(8,128)(2,1)S(1)}, u32[]{:S(2)}, u32[]{:S(2)}) async-start(bf16[16,768,128]{2,1,0:T(8,128)(2,1)} %combine.1), calls=%async_computation.3 | async-start | bytes 6291456 | tf_op jit(solution)/shard_map/all_to_all | solution.py:53
  130.3 1.4 add_convert_fusion.2
  131.7 0.0 copy-start.4
  131.8 3.0 %collective-permute-start.8 = (bf16[128,2048]{1,0:T(8,128)(2,1)S(1)}, bf16[128,2048]{1,0:T(8,128)(2,1)S(1)}, u32[]{:S(2)}, u32[]{:S(2)}) collective-permute-start(bf16[128,2048]{1,0:T(8,128)(2,1)S(1)} %add_convert_fusion.2), channel_id=1, source_target_pairs={{0,96},{32,0},{64,32},{96,64},{1,97},{33,1},{65,33},{97,65},{2,98}... | collective-permute-start | bytes 1572872 | tf_op jit(solution)/shard_map/ppermute | solution.py:422
  134.8 1.3 add_convert_fusion.5
  136.1 0.1 collective-permute-start.5
  136.2 9.5 %collective-permute-done.8 = bf16[128,2048]{1,0:T(8,128)(2,1)S(1)} collective-permute-done((bf16[128,2048]{1,0:T(8,128)(2,1)S(1)}, bf16[128,2048]{1,0:T(8,128)(2,1)S(1)}, u32[]{:S(2)}, u32[]{:S(2)}) %collective-permute-start.8) | collective-permute-done | bytes 524320 | tf_op jit(solution)/shard_map/ppermute | solution.py:422
  145.7 0.1 add_convert_fusion.1
  145.8 3.8 %collective-permute-start.9 = (bf16[128,2048]{1,0:T(8,128)(2,1)S(1)}, bf16[128,2048]{1,0:T(8,128)(2,1)S(1)}, u32[]{:S(2)}, u32[]{:S(2)}) collective-permute-start(bf16[128,2048]{1,0:T(8,128)(2,1)S(1)} %add_convert_fusion.1), channel_id=1, source_target_pairs={{0,96},{32,0},{64,32},{96,64},{1,97},{33,1},{65,33},{97,65},{2,98}... | collective-permute-start | bytes 1572872 | tf_op jit(solution)/shard_map/ppermute | solution.py:422
  149.6 0.9 collective-permute-done.5
  150.5 0.1 add_convert_fusion.4
  150.6 0.1 collective-permute-start.6
  150.7 8.9 %collective-permute-done.9 = bf16[128,2048]{1,0:T(8,128)(2,1)S(1)} collective-permute-done((bf16[128,2048]{1,0:T(8,128)(2,1)S(1)}, bf16[128,2048]{1,0:T(8,128)(2,1)S(1)}, u32[]{:S(2)}, u32[]{:S(2)}) %collective-permute-start.9) | collective-permute-done | bytes 524320 | tf_op jit(solution)/shard_map/ppermute | solution.py:422
  159.6 0.9 add_convert_fusion
  160.5 3.6 %collective-permute-done.6 = bf16[128,2048]{1,0:T(8,128)(2,1)S(1)} collective-permute-done((bf16[128,2048]{1,0:T(8,128)(2,1)S(1)}, bf16[128,2048]{1,0:T(8,128)(2,1)S(1)}, u32[]{:S(2)}, u32[]{:S(2)}) %collective-permute-start.6) | collective-permute-done | bytes 524320 | tf_op jit(solution)/shard_map/ppermute | solution.py:421
  164.1 0.9 add_convert_fusion.3
  165.0 7.7 %all-to-all-done.3.r_ref = bf16[16,768,128]{2,1,0:T(8,128)(2,1)S(1)} async-done(((bf16[16,768,128]{2,1,0:T(8,128)(2,1)}), bf16[16,768,128]{2,1,0:T(8,128)(2,1)S(1)}, u32[]{:S(2)}, u32[]{:S(2)}) %all-to-all-start.3) | async-done | bytes 3145760 | tf_op jit(solution)/shard_map/all_to_all | solution.py:53
  172.8 3.0 %pad_maximum_fusion = bf16[16,16,2048]{2,1,0:T(8,128)(2,1)} fusion(bf16[8,16,2048]{2,1,0:T(8,128)(2,1)} %bitcast.12, bf16[8,16,2048]{2,1,0:T(8,128)(2,1)} %bitcast.13), kind=kLoop, calls=%fused_computation.1 | loop fusion | flops 524288 | bytes 2097152 | tf_op jit(solution)/shard_map/concatenate | solution.py:460
  175.8 9.9 %all-to-all-start.4 = ((bf16[16,16,2048]{2,1,0:T(8,128)(2,1)}), bf16[16,16,2048]{2,1,0:T(8,128)(2,1)}, u32[]{:S(2)}, u32[]{:S(2)}) async-start(bf16[16,16,2048]{2,1,0:T(8,128)(2,1)} %pad_maximum_fusion), calls=%async_computation.4 | async-start | bytes 2097152 | tf_op jit(solution)/shard_map/all_to_all | solution.py:53
  185.7 4.4 %unpack.1 = (bf16[256,2048]{1,0:T(8,128)(2,1)}, bf16[256,2048]{1,0:T(8,128)(2,1)}, bf16[256,2048]{1,0:T(8,128)(2,1)}) custom-call(bf16[16,768,128]{2,1,0:T(8,128)(2,1)} %copy-done.1), custom_call_target="tpu_custom_call" | custom-call | bytes 6291456 | tf_op jit(solution)/shard_map/unpack/pallas_call | solution.py:94
  190.1 11.9 %all-to-all-done.4 = bf16[16,16,2048]{2,1,0:T(8,128)(2,1)} async-done(((bf16[16,16,2048]{2,1,0:T(8,128)(2,1)}), bf16[16,16,2048]{2,1,0:T(8,128)(2,1)}, u32[]{:S(2)}, u32[]{:S(2)}) %all-to-all-start.4) | async-done | bytes 1048608 | tf_op jit(solution)/shard_map/all_to_all | solution.py:53
  201.9 2.0 convert_reduce_fusion
  (22 shorter events, 0.1 us)
Async XLA Ops:
  5.0 51.0 %all-to-all-start = ((bf16[16,776,128]{2,1,0:T(8,128)(2,1)}), bf16[16,776,128]{2,1,0:T(8,128)(2,1)S(1)}, u32[]{:S(2)}, u32[]{:S(2)}) async-start(bf16[16,776,128]{2,1,0:T(8,128)(2,1)} %pack.1), calls=%async_computation | async-start | bytes 6356992 | tf_op jit(solution)/shard_map/all_to_all | solution.py:53
  13.1 8.9 %collective-permute-start = (bf16[256,2048]{1,0:T(8,128)(2,1)}, bf16[256,2048]{1,0:T(8,128)(2,1)}, u32[]{:S(2)}, u32[]{:S(2)}) collective-permute-start(bf16[256,2048]{1,0:T(8,128)(2,1)} %bitcast.14), channel_id=1, source_target_pairs={{0,1},{1,0},{2,3},{3,2},{4,5},{5,4},{6,7},{7,6},{8,9},{9,8},{10,11... | collective-permute-start | bytes 3145736 | tf_op jit(solution)/shard_map/ppermute | solution.py:439
  56.0 9.1 %copy-start = (bf16[16,776,128]{2,1,0:T(8,128)(2,1)}, bf16[16,776,128]{2,1,0:T(8,128)(2,1)S(1)}, u32[]{:S(2)}) copy-start(bf16[16,776,128]{2,1,0:T(8,128)(2,1)S(1)} %all-to-all-done.x_ref) | copy-start | bytes 9535492
  56.0 9.1 %collective-permute-start.1 = (bf16[16,776,128]{2,1,0:T(8,128)(2,1)S(1)}, bf16[16,776,128]{2,1,0:T(8,128)(2,1)}, u32[]{:S(2)}, u32[]{:S(2)}) collective-permute-start(bf16[16,776,128]{2,1,0:T(8,128)(2,1)S(1)} %all-to-all-done.x_ref), channel_id=1, source_target_pairs={{0,1},{1,0},{2,3},{3,2},{4,5},{5,4},{6,7},{7,6},{8,9},{9,8},{10,11... | collective-permute-start | bytes 9535496 | tf_op jit(solution)/shard_map/ppermute | solution.py:442
  56.0 26.7 %all-to-all-start.1 = ((bf16[16,256,128]{2,1,0:T(8,128)(2,1)}), bf16[16,256,128]{2,1,0:T(8,128)(2,1)}, u32[]{:S(2)}, u32[]{:S(2)}) async-start(bf16[16,256,128]{2,1,0:T(8,128)(2,1)} %grad_attn.1), calls=%async_computation.1 | async-start | bytes 2097152 | tf_op jit(solution)/shard_map/all_to_all | solution.py:53
  82.6 21.7 %all-to-all-start.2 = ((bf16[16,128,256]{2,1,0:T(8,128)(2,1)}), bf16[16,128,256]{2,1,0:T(8,128)(2,1)S(1)}, u32[]{:S(2)}, u32[]{:S(2)}) async-start(bf16[16,128,256]{2,1,0:T(8,128)(2,1)} %get-tuple-element.40), calls=%async_computation.2 | async-start | bytes 2097152 | tf_op jit(solution)/shard_map/all_to_all | solution.py:53
  104.4 4.5 %copy-start.3 = (bf16[16,128,256]{2,1,0:T(8,128)(2,1)}, bf16[16,128,256]{2,1,0:T(8,128)(2,1)S(1)}, u32[]{:S(2)}) copy-start(bf16[16,128,256]{2,1,0:T(8,128)(2,1)S(1)} %all-to-all-done.2.oa_ref) | copy-start | bytes 3145732
  104.4 2.7 %collective-permute-start.2 = (bf16[16,128,256]{2,1,0:T(8,128)(2,1)S(1)}, bf16[16,128,256]{2,1,0:T(8,128)(2,1)S(1)}, u32[]{:S(2)}, u32[]{:S(2)}) collective-permute-start(bf16[16,128,256]{2,1,0:T(8,128)(2,1)S(1)} %all-to-all-done.2.oa_ref), channel_id=1, source_target_pairs={{0,1},{1,0},{2,3},{3,2},{4,5},{5,4},{6,7},{7,6},{8,9},{9,8},{10,11... | collective-permute-start | bytes 3145736 | tf_op jit(solution)/shard_map/ppermute | solution.py:450
  107.1 1.0 copy-start.8
  108.1 9.5 %collective-permute-start.3 = (bf16[16,512,128]{2,1,0:T(8,128)(2,1)}, bf16[16,512,128]{2,1,0:T(8,128)(2,1)S(1)}, u32[]{:S(2)}, u32[]{:S(2)}) collective-permute-start(bf16[16,512,128]{2,1,0:T(8,128)(2,1)} %get-tuple-element.54), channel_id=1, source_target_pairs={{0,1},{1,0},{2,3},{3,2},{4,5},{5,4},{6,7},{7,6},{8,9},{9,8},{10,11... | collective-permute-start | bytes 6291464 | tf_op jit(solution)/shard_map/ppermute | solution.py:452
  114.8 15.5 %collective-permute-start.7 = (bf16[128,2048]{1,0:T(8,128)(2,1)}, bf16[128,2048]{1,0:T(8,128)(2,1)}, u32[]{:S(2)}, u32[]{:S(2)}) collective-permute-start(bf16[128,2048]{1,0:T(8,128)(2,1)} %get-tuple-element.60), channel_id=1, source_target_pairs={{0,96},{32,0},{64,32},{96,64},{1,97},{33,1},{65,33},{97,65},{2,98}... | collective-permute-start | bytes 1572872 | tf_op jit(solution)/shard_map/ppermute | solution.py:422
  117.6 1.3 copy-start.2
  117.6 17.2 %collective-permute-start.4 = (bf16[128,2048]{1,0:T(8,128)(2,1)}, bf16[128,2048]{1,0:T(8,128)(2,1)}, u32[]{:S(2)}, u32[]{:S(2)}) collective-permute-start(bf16[128,2048]{1,0:T(8,128)(2,1)} %get-tuple-element.56), channel_id=1, source_target_pairs={{0,32},{32,64},{64,96},{96,0},{1,33},{33,65},{65,97},{97,1},{2,34}... | collective-permute-start | bytes 1572872 | tf_op jit(solution)/shard_map/ppermute | solution.py:421
  123.3 49.5 %all-to-all-start.3 = ((bf16[16,768,128]{2,1,0:T(8,128)(2,1)}), bf16[16,768,128]{2,1,0:T(8,128)(2,1)S(1)}, u32[]{:S(2)}, u32[]{:S(2)}) async-start(bf16[16,768,128]{2,1,0:T(8,128)(2,1)} %combine.1), calls=%async_computation.3 | async-start | bytes 6291456 | tf_op jit(solution)/shard_map/all_to_all | solution.py:53
  130.3 15.4 %copy-start.7 = (bf16[128,2048]{1,0:T(8,128)(2,1)S(1)}, bf16[128,2048]{1,0:T(8,128)(2,1)}, u32[]{:S(2)}) copy-start(bf16[128,2048]{1,0:T(8,128)(2,1)} %get-tuple-element.62) | copy-start | bytes 1572868
  130.3 20.2 %copy-start.6 = (bf16[128,2048]{1,0:T(8,128)(2,1)S(1)}, bf16[128,2048]{1,0:T(8,128)(2,1)}, u32[]{:S(2)}) copy-start(bf16[128,2048]{1,0:T(8,128)(2,1)} %get-tuple-element.58) | copy-start | bytes 1572868
  130.3 29.3 %copy-start.5 = (bf16[128,2048]{1,0:T(8,128)(2,1)S(1)}, bf16[128,2048]{1,0:T(8,128)(2,1)}, u32[]{:S(2)}) copy-start(bf16[128,2048]{1,0:T(8,128)(2,1)} %get-tuple-element.63) | copy-start | bytes 1572868
  131.7 32.4 %copy-start.4 = (bf16[128,2048]{1,0:T(8,128)(2,1)S(1)}, bf16[128,2048]{1,0:T(8,128)(2,1)}, u32[]{:S(2)}) copy-start(bf16[128,2048]{1,0:T(8,128)(2,1)} %get-tuple-element.59) | copy-start | bytes 1572868
  131.8 13.9 %collective-permute-start.8 = (bf16[128,2048]{1,0:T(8,128)(2,1)S(1)}, bf16[128,2048]{1,0:T(8,128)(2,1)S(1)}, u32[]{:S(2)}, u32[]{:S(2)}) collective-permute-start(bf16[128,2048]{1,0:T(8,128)(2,1)S(1)} %add_convert_fusion.2), channel_id=1, source_target_pairs={{0,96},{32,0},{64,32},{96,64},{1,97},{33,1},{65,33},{97,65},{2,98}... | collective-permute-start | bytes 1572872 | tf_op jit(solution)/shard_map/ppermute | solution.py:422
  136.1 14.4 %collective-permute-start.5 = (bf16[128,2048]{1,0:T(8,128)(2,1)S(1)}, bf16[128,2048]{1,0:T(8,128)(2,1)S(1)}, u32[]{:S(2)}, u32[]{:S(2)}) collective-permute-start(bf16[128,2048]{1,0:T(8,128)(2,1)S(1)} %add_convert_fusion.5), channel_id=1, source_target_pairs={{0,32},{32,64},{64,96},{96,0},{1,33},{33,65},{65,97},{97,1},{2,34}... | collective-permute-start | bytes 1572872 | tf_op jit(solution)/shard_map/ppermute | solution.py:421
  145.8 13.8 %collective-permute-start.9 = (bf16[128,2048]{1,0:T(8,128)(2,1)S(1)}, bf16[128,2048]{1,0:T(8,128)(2,1)S(1)}, u32[]{:S(2)}, u32[]{:S(2)}) collective-permute-start(bf16[128,2048]{1,0:T(8,128)(2,1)S(1)} %add_convert_fusion.1), channel_id=1, source_target_pairs={{0,96},{32,0},{64,32},{96,64},{1,97},{33,1},{65,33},{97,65},{2,98}... | collective-permute-start | bytes 1572872 | tf_op jit(solution)/shard_map/ppermute | solution.py:422
  150.6 13.5 %collective-permute-start.6 = (bf16[128,2048]{1,0:T(8,128)(2,1)S(1)}, bf16[128,2048]{1,0:T(8,128)(2,1)S(1)}, u32[]{:S(2)}, u32[]{:S(2)}) collective-permute-start(bf16[128,2048]{1,0:T(8,128)(2,1)S(1)} %add_convert_fusion.4), channel_id=1, source_target_pairs={{0,32},{32,64},{64,96},{96,0},{1,33},{33,65},{65,97},{97,1},{2,34}... | collective-permute-start | bytes 1572872 | tf_op jit(solution)/shard_map/ppermute | solution.py:421
  172.8 12.9 %copy-start.1 = (bf16[16,768,128]{2,1,0:T(8,128)(2,1)}, bf16[16,768,128]{2,1,0:T(8,128)(2,1)S(1)}, u32[]{:S(2)}) copy-start(bf16[16,768,128]{2,1,0:T(8,128)(2,1)S(1)} %all-to-all-done.3.r_ref) | copy-start | bytes 9437188
  175.8 26.1 %all-to-all-start.4 = ((bf16[16,16,2048]{2,1,0:T(8,128)(2,1)}), bf16[16,16,2048]{2,1,0:T(8,128)(2,1)}, u32[]{:S(2)}, u32[]{:S(2)}) async-start(bf16[16,16,2048]{2,1,0:T(8,128)(2,1)} %pad_maximum_fusion), calls=%async_computation.4 | async-start | bytes 2097152 | tf_op jit(solution)/shard_map/all_to_all | solution.py:53

commit v5 on v4

--- a/solution.py
+++ b/solution.py
@@ -17,8 +17,8 @@
 BLOCKS = 64
 DOCS = 4
 CHUNK = D // 4 // DOCS
-RIDER = 3 * TOK
-ROWS = 3 * TOK + 8
+RIDER = 4 * TOK
+ROWS = 4 * TOK + 8
 SCALE = HEAD ** (-0.5)
 SCALE2 = SCALE * math.log2(math.e)
 NEG = -1e30
@@ -30,6 +30,7 @@
 
 UNROLL = 4
 GROUP = 4
+JOIN = 2
 PACK = 4
 VMEM_LIMIT = 56 * 1024 * 1024
 
@@ -57,29 +58,40 @@
     return lax.optimization_barrier(values)
 
 
-def pack_body(offs, k_ref, v_ref, q_ref, x_ref):
+def pack_body(offs, k_ref, v_ref, q_ref, c_ref, w_ref, x_ref):
     lane = lax.broadcasted_iota(jnp.int32, (8, 128), 1)
     val = jnp.zeros((8, 128), jnp.int32)
     for j in range(2 * SLOTS):
         val = jnp.where(lane == j, offs[j // SLOTS, j % SLOTS], val)
     rider = val.astype(f32).astype(bf16)
-    for h in range(PACK):
+    g = dot(c_ref[...], w_ref[...], 1, 1).astype(bf16)
+    for h in range(JOIN):
+        columns = slice(h * HEAD, (h + 1) * HEAD)
         for t, ref in enumerate((k_ref, v_ref, q_ref)):
-            x_ref[h, t * TOK : (t + 1) * TOK, :] = ref[:, h * HEAD : (h + 1) * HEAD]
+            x_ref[h, t * TOK : (t + 1) * TOK, :] = ref[:, columns]
+        x_ref[h, 3 * TOK : 4 * TOK, :] = g[:, columns]
         x_ref[h, RIDER : RIDER + 8, :] = rider
 
 
-def pack(offs, k, v, q):
-    rows = pl.BlockSpec((TOK, PACK * HEAD), lambda i: (0, i))
+def pack(offs, k, v, q, cot, weight):
+    rows = pl.BlockSpec((TOK, JOIN * HEAD), lambda i: (0, i))
     return pl.pallas_call(
         pack_body,
         out_shape=jax.ShapeDtypeStruct((HEADS, ROWS, HEAD), bf16),
-        grid=(HEADS // PACK,),
-        in_specs=[pl.BlockSpec(memory_space=pltpu.SMEM), rows, rows, rows],
-        out_specs=pl.BlockSpec((PACK, ROWS, HEAD), lambda i: (i, 0, 0)),
-        compiler_params=pltpu.CompilerParams(vmem_limit_bytes=VMEM_LIMIT),
+        grid=(HEADS // JOIN,),
+        in_specs=[
+            pl.BlockSpec(memory_space=pltpu.SMEM),
+            rows,
+            rows,
+            rows,
+            pl.BlockSpec((TOK, D), lambda i: (0, 0)),
+            pl.BlockSpec((JOIN * HEAD, D), lambda i: (i, 0)),
+        ],
+        out_specs=pl.BlockSpec((JOIN, ROWS, HEAD), lambda i: (i, 0, 0)),
+        compiler_params=pltpu.CompilerParams(vmem_limit_bytes=VMEM_LIMIT),
+        cost_estimate=cost(2 * TOK * D * D, 0, 16 * MIB),
         name="pack",
-    )(offs, k, v, q)
+    )(offs, k, v, q, cot, weight)
 
 
 def unpack_body(r_ref, *refs):
@@ -101,28 +113,6 @@
         cost_estimate=cost(0, 0, 2 * n * MIB),
         name="unpack",
     )(r)
-
-
-def grad_attn_body(c_ref, w_ref, o_ref):
-    g = dot(c_ref[...], w_ref[...], 1, 1).astype(bf16)
-    for j in range(2):
-        o_ref[j] = g[:, j * HEAD : (j + 1) * HEAD]
-
-
-def grad_attn_by_head(cot, weight):
-    return pl.pallas_call(
-        grad_attn_body,
-        out_shape=jax.ShapeDtypeStruct((HEADS, TOK, HEAD), bf16),
-        grid=(HEADS // 2,),
-        in_specs=[
-            pl.BlockSpec((TOK, D), lambda i: (0, 0)),
-            pl.BlockSpec((2 * HEAD, D), lambda i: (i, 0)),
-        ],
-        out_specs=pl.BlockSpec((2, TOK, HEAD), lambda i: (i, 0, 0)),
-        compiler_params=pltpu.CompilerParams(vmem_limit_bytes=VMEM_LIMIT),
-        cost_estimate=cost(2 * TOK * D * D, 0, 10 * MIB),
-        name="grad_attn",
-    )(cot, weight)
 
 
 def load_pool(x_ref, y_ref, kv, qs, sems):
@@ -135,7 +125,7 @@
                     x_ref.at[at, pl.ds(0, 2 * TOK), :], kv.at[at], sems.at[3 * j]
                 ),
                 pltpu.make_async_copy(
-                    y_ref.at[at, pl.ds(0, 2 * TOK), :],
+                    y_ref.at[at],
                     kv.at[pl.ds(CHIPS + j * GROUP, GROUP)],
                     sems.at[3 * j + 1],
                 ),
@@ -196,8 +186,10 @@
         for i in range(2):
             out, lse = block(c, i)
             for g in range(8):
-                row = (g % 2) * 64 + (g // 2) * 16
-                o_ref[c, row : row + 16, i * BLK : (i + 1) * BLK] = out[g * 16 : g * 16 + 16, :]
+                row = (g // 2) * 16
+                o_ref[2 * c + g % 2, row : row + 16, i * BLK : (i + 1) * BLK] = out[
+                    g * 16 : g * 16 + 16, :
+                ]
             lses.append(lse)
         row = lax.broadcasted_iota(jnp.int32, (8, 128), 0)
         lse_ref[c] = jnp.where(row == 0, lses[0], lses[1])
@@ -213,7 +205,7 @@
     return pl.pallas_call(
         forward_body,
         out_shape=(
-            jax.ShapeDtypeStruct((CHIPS, HEAD, TOK), bf16),
+            jax.ShapeDtypeStruct((2 * CHIPS, HEAD // 2, TOK), bf16),
             jax.ShapeDtypeStruct((CHIPS, 8, 128), f32),
         ),
         in_specs=[pl.BlockSpec(memory_space=pltpu.SMEM)] + [pl.BlockSpec(memory_space=pl.ANY)] * 2,
@@ -230,14 +222,18 @@
 
 
 def backward_body(
-    table, x_ref, y_ref, g_ref, lse_ref, home_ref, other_ref, kv, qs, gs, acck, accv, own, other, gq, sems
+    table, x_ref, y_ref, lse_ref, home_ref, other_ref, kv, qs, gs, acck, accv, own, other, gq, sems
 ):
     groups = load_pool(x_ref, y_ref, kv, qs, sems)
     sends = []
     n = CHIPS // GROUP
     for j in range(n):
         at = pl.ds(j * GROUP, GROUP)
-        groups[j].append(pltpu.make_async_copy(g_ref.at[at], gs.at[at], sems.at[3 * n + j]))
+        groups[j].append(
+            pltpu.make_async_copy(
+                x_ref.at[at, pl.ds(3 * TOK, TOK), :], gs.at[at], sems.at[3 * n + j]
+            )
+        )
         sends.append(
             [
                 pltpu.make_async_copy(
@@ -318,7 +314,7 @@
             copy.wait()
 
 
-def attention_backward(table, x, y, g, lse):
+def attention_backward(table, x, y, lse):
     return pl.pallas_call(
         backward_body,
         out_shape=(
@@ -326,7 +322,7 @@
             jax.ShapeDtypeStruct((CHIPS, 2 * TOK, HEAD), bf16),
         ),
         in_specs=[pl.BlockSpec(memory_space=pltpu.SMEM)]
-        + [pl.BlockSpec(memory_space=pl.ANY)] * 3
+        + [pl.BlockSpec(memory_space=pl.ANY)] * 2
         + [pl.BlockSpec(memory_space=pltpu.VMEM)],
         out_specs=[pl.BlockSpec(memory_space=pl.ANY)] * 2,
         scratch_shapes=[
@@ -343,7 +339,7 @@
         compiler_params=pltpu.CompilerParams(vmem_limit_bytes=VMEM_LIMIT),
         cost_estimate=cost(5 * PAIR_FLOPS, PAIRS, 14 * MIB),
         name="attn_bwd",
-    )(table, x, y, g, lse)
+    )(table, x, y, lse)
 
 
 def combine_body(own_ref, got_ref, o_ref):
@@ -386,8 +382,9 @@
         copy.wait()
 
 
-def weight_partial(place, oa, ob, ca, cb):
-    rows = pl.BlockSpec((HEADS, 64, TOK), lambda i, place: (0, place[0], 0))
+def weight_partial(place, out, ca, cb):
+    own = pl.BlockSpec((HEADS, 1, HEAD // 2, TOK), lambda i, place: (0, place[0], 0, 0))
+    other = pl.BlockSpec((HEADS, 1, HEAD // 2, TOK), lambda i, place: (0, 1 - place[0], 0, 0))
     whole = pl.BlockSpec((TOK, D), lambda i, place: (0, 0))
     outs = pl.pallas_call(
         weight_body,
@@ -395,7 +392,7 @@
         grid_spec=pltpu.PrefetchScalarGridSpec(
             num_scalar_prefetch=1,
             grid=(1,),
-            in_specs=[rows, rows, whole, whole],
+            in_specs=[own, other, whole, whole],
             out_specs=[pl.BlockSpec(memory_space=pl.ANY)] * (2 * DOCS),
             scratch_shapes=[
                 pltpu.VMEM((DOCS, 2 * CHUNK, D), bf16),
@@ -405,12 +402,30 @@
         compiler_params=pltpu.CompilerParams(vmem_limit_bytes=VMEM_LIMIT),
         cost_estimate=cost(2 * TOK * D * D, 0, 8 * MIB),
         name="weight_partial",
-    )(place, oa, ob, ca, cb)
+    )(place, out, out, ca, cb)
     return outs[0::2], outs[1::2]
 
 
 def plus(a, b):
     return (a.astype(f32) + b.astype(f32)).astype(bf16)
+
+
+def join_body(a_ref, b_ref, o_ref):
+    n = CHIPS // 2
+    o_ref[0:n] = a_ref[...].reshape(n, 16, D)
+    o_ref[n : 2 * n] = b_ref[...].reshape(n, 16, D)
+
+
+def join(a, b):
+    return pl.pallas_call(
+        join_body,
+        out_shape=jax.ShapeDtypeStruct((CHIPS, 16, D), bf16),
+        in_specs=[pl.BlockSpec(memory_space=pltpu.VMEM)] * 2,
+        out_specs=pl.BlockSpec(memory_space=pltpu.VMEM),
+        compiler_params=pltpu.CompilerParams(vmem_limit_bytes=VMEM_LIMIT),
+        cost_estimate=cost(0, 0, 2 * MIB),
+        name="join",
+    )(a, b)
 
 
 def sum_over_docs(up, down):
@@ -436,29 +451,28 @@
 def local(queries, key_states, value_states, out_weight, cotangent, block_offsets):
     core = lax.axis_index("seq") % 2
     cot = cotangent[0]
+    packed = pack(
+        block_offsets[0], key_states[0], value_states[0], queries[0], cot, out_weight
+    )
     cot_other = lax.ppermute(cot, "seq", CORE_SWAP)
-    x = exchange(pack(block_offsets[0], key_states[0], value_states[0], queries[0]))
-    x, g, cot_other = after(x, grad_attn_by_head(cot, out_weight), cot_other)
-    y = lax.ppermute(x, "seq", CORE_SWAP)
-    g = exchange(g)
+    packed, cot_other = after(packed, cot_other)
+    x = exchange(packed)
+    y = lax.ppermute(x[:, 0 : 2 * TOK], "seq", CORE_SWAP)
     table = block_table(x[:, RIDER, 0 : 2 * SLOTS], core)
+    place = jnp.stack([core, lax.axis_index("dp")])
+    table, place = after(table, place)
     out, lse = attention_forward(table, x, y)
-    g, out = after(g, out)
-    out_home = exchange(out)
-    own, other = attention_backward(table, x, y, g, lse)
+    out_home = lax.all_to_all(out, "seq", 0, 0, tiled=True)
+    own, other = attention_backward(table, x, y, lse)
     out_home, own, other = after(out_home, own, other)
-    out_other = lax.ppermute(out_home, "seq", CORE_SWAP)
-    out_other, other = after(out_other, other)
     got = lax.ppermute(other, "seq", CORE_SWAP)
-    place = jnp.stack([core, lax.axis_index("dp")])
-    partial = weight_partial(place, out_home, out_other, cot, cot_other)
-    up, down = partial
+    by_core = out_home.reshape(HEADS, 2, HEAD // 2, TOK)
+    up, down = weight_partial(place, by_core, cot, cot_other)
     *up, got = after(*up, got)
     sums = sum_over_docs(up, down)
     home = exchange(combine(own, got))
     home, *sums = after(home, *sums)
-    by_doc = jnp.concatenate([part.reshape(CHIPS // 2, 16, D) for part in sums], axis=0)
-    pieces = exchange(by_doc)
+    pieces = exchange(join(*sums))
     weight_grad = jnp.sum(pieces.astype(f32), axis=0)
     gk, gv, gq = unpack(home, 3)
     return gq[None], gk[None], gv[None], weight_grad

time: 205 us -> 205 us (level)
  blocking collectives: 0 us -> 60.1 us
  waiting for transfers between devices: 88.7 us -> 44.6 us
  starting transfers between devices: 47 us -> 28.7 us
  local copies, waits for them, and re-layouts: 2.49 us -> 7.21 us
  other arithmetic: 11.3 us -> 9.06 us
    all_to_all x0 -> x1, blocking collectives: none -> 60.1 us  [exchange(): lax.all_to_all(x, 'seq', 0, 0, axis_index_groups=SAME_CORE, tiled=True)]
    all_to_all x5 -> x2, waiting for transfers between devices: 63.2 us -> 20.3 us  [exchange(): lax.all_to_all(x, 'seq', 0, 0, axis_index_groups=SAME_CORE, tiled=True)]
    all_to_all x5 -> x2, starting transfers between devices: 37 us -> 15.1 us  [exchange(): lax.all_to_all(x, 'seq', 0, 0, axis_index_groups=SAME_CORE, tiled=True)]
    pallas_call x1, Pallas kernels: 4.37 us -> 10.4 us  [pack(): pl.pallas_call(pack_body, out_shape=jax.ShapeDtypeStruct((HEADS, ROWS, HE...]
    pallas_call x2, Pallas kernels: 16.6 us -> 10.9 us  [the longest x1 7.86 us: attention_forward(): pl.pallas_call(forward_body, out_shape=(jax.ShapeDtypeStruct((2 * CHIPS,...]
    all_to_all x0 -> x1, starting transfers between devices: none -> 4.12 us  [local(): out_home = lax.all_to_all(out, 'seq', 0, 0, tiled=True)]
    unnamed x18 -> x20, local copies, waits for them, and re-layouts: 2.33 us -> 5.49 us
    concatenate x1 -> x0, other arithmetic: 3.05 us -> none  [local(): jnp.concatenate([part.reshape(CHIPS // 2, 16, D) for part in sums], axis=0)]
  transfers between devices with their start and end apart: 15 -> 12, of which waited for: 9 -> 7; matrix products, arithmetic and copies ran while one was open for 3% -> 4% of each run, Pallas kernels for 24% -> 21%
where the time goes in v5:
time: 205 us; the launch traced here: 204 us
  blocking collectives  60.1 us (29%)
  Pallas kernels  53.8 us (26%)
  waiting for transfers between devices  44.6 us (22%)
  starting transfers between devices  28.7 us (14%)
  other arithmetic  9.06 us (4%)
  local copies, waits for them, and re-layouts  7.21 us (4%)
    all_to_all x1, blocking collectives, exchange(): lax.all_to_all(x, 'seq', 0, 0, axis_index_groups=SAME_CORE, tiled=True)  60.1 us
    all_to_all x2, waiting for transfers between devices, exchange(): lax.all_to_all(x, 'seq', 0, 0, axis_index_groups=SAME_CORE, tiled=True)  20.3 us
    pallas_call x1, Pallas kernels, attention_backward(): pl.pallas_call(backward_body, out_shape=(jax.ShapeDtypeStruct((CHIPS, 3 *...  17.9 us
    ppermute x3, waiting for transfers between devices, sum_over_docs(): b = plus(lax.ppermute(b, 'dp', route_down), down[(1 + step) % DOCS])  17.7 us
    all_to_all x2, starting transfers between devices, exchange(): lax.all_to_all(x, 'seq', 0, 0, axis_index_groups=SAME_CORE, tiled=True)  15.1 us
    pallas_call x1, Pallas kernels, pack(): pl.pallas_call(pack_body, out_shape=jax.ShapeDtypeStruct((HEADS, ROWS, HE...  10.4 us
    ppermute x3, starting transfers between devices, sum_over_docs(): b = plus(lax.ppermute(b, 'dp', route_down), down[(1 + step) % DOCS])  9.1 us
    pallas_call x1, Pallas kernels, attention_forward(): pl.pallas_call(forward_body, out_shape=(jax.ShapeDtypeStruct((2 * CHIPS,...  7.86 us
  transfers between devices with their start and end apart: 12, of which 7 were waited for; matrix products, arithmetic and copies ran while one was open for 4% of the time, Pallas kernels for 21%

profile of v5, /device:TPU:0, one launch (start us, length us, event | category | flops | bytes accessed | tf_op | source)
XLA Modules:
  0.0 204.3 jit_solution(6632194187554621163)
XLA Ops:
  0.6 0.1 collective-permute-start
  0.7 10.4 %pack.1 = bf16[16,1032,128]{2,1,0:T(8,128)(2,1)} custom-call(s32[2,4]{1,0:T(2,128)} %bitcast.19, bf16[256,2048]{1,0:T(8,128)(2,1)} %bitcast.11, bf16[256,2048]{1,0:T(8,128)(2,1)} %bitcast.12, bf16[256,2048]{1,0:T(8,128)(2,1)} %bitcast.13, bf16[256,2048]{1,0:T(8,128)(2,1)} %bitcast.15, bf16[2048,2048]{1,0:T(8,128)(2,1)} %w_ref.1), custom_call_target="tpu_custom_call" | custom-call | flops 2147483648 | bytes 16777216 | tf_op jit(solution)/shard_map/pack/pallas_call | solution.py:78
  11.2 0.0 collective-permute-done.cb_ref
  11.2 60.1 %all_to_all.20.x_ref = bf16[16,1032,128]{2,1,0:T(8,128)(2,1)S(1)} all-to-all(bf16[16,1032,128]{2,1,0:T(8,128)(2,1)} %pack.1), channel_id=1, replica_groups={{0,2,4,6,8,10,12,14,16,18,20,22,24,26,28,30},{1,3,5,7,9,11,13,15,17,19,..., dimensions={0} | all-to-all | bytes 8454144 | tf_op jit(solution)/shard_map/all_to_all | solution.py:54
  71.3 2.0 copy-done
  73.2 1.6 slice.9
  74.8 0.0 collective-permute-start.1
  74.8 0.1 iota_add_fusion
  74.9 0.1 add.68
  75.0 0.6 pad_add_fusion.place
  75.6 0.8 fusion
  76.4 0.1 reshape.47
  76.4 0.7 add_select_fusion.table
  77.1 2.0 collective-permute-done.1.y_ref
  79.2 1.3 copy-done.2
  80.5 7.9 %attn_fwd.1 = (bf16[32,64,256]{2,1,0:T(8,128)(2,1)}, f32[16,8,128]{2,1,0:T(8,128)}) custom-call(s32[32,4]{1,0:T(8,128)} %add_select_fusion.table, bf16[16,1032,128]{2,1,0:T(8,128)(2,1)} %copy-done, bf16[16,512,128]{2,1,0:T(8,128)(2,1)} %copy-done.2), custom_call_target="tpu_custom_call" | custom-call | flops 1342177280 | bytes 7340032 | tf_op jit(solution)/shard_map/attn_fwd/pallas_call | solution.py:205
  88.4 4.1 %all-to-all-start.1 = ((bf16[32,64,256]{2,1,0:T(8,128)(2,1)}), bf16[32,64,256]{2,1,0:T(8,128)(2,1)S(1)}, u32[]{:S(2)}, u32[]{:S(2)}) async-start(bf16[32,64,256]{2,1,0:T(8,128)(2,1)} %get-tuple-element.36), calls=%async_computation.1 | async-start | bytes 2097152 | tf_op jit(solution)/shard_map/all_to_all | solution.py:465
  92.5 17.9 %attn_bwd.1 = (bf16[16,768,128]{2,1,0:T(8,128)(2,1)}, bf16[16,512,128]{2,1,0:T(8,128)(2,1)}) custom-call(s32[32,4]{1,0:T(8,128)} %add_select_fusion.table, bf16[16,1032,128]{2,1,0:T(8,128)(2,1)} %copy-done, bf16[16,512,128]{2,1,0:T(8,128)(2,1)} %copy-done.2, f32[16,8,128]{2,1,0:T(8,128)} %get-tuple-element.37.lse_ref), custom_call_target="tpu_custom_call" | custom-call | flops 3355443200 | bytes 14680064 | tf_op jit(solution)/shard_map/attn_bwd/pallas_call | solution.py:318
  110.4 0.0 all-to-all-done.1
  110.4 0.0 copy-start.4
  110.4 0.1 collective-permute-start.2
  110.5 0.9 copy-done.4
  111.4 5.9 %weight_partial.1 = (bf16[128,2048]{1,0:T(8,128)(2,1)}, bf16[128,2048]{1,0:T(8,128)(2,1)}, bf16[128,2048]{1,0:T(8,128)(2,1)}, bf16[128,2048]{1,0:T(8,128)(2,1)},...) custom-call(s32[2]{0:T(128)} %pad_add_fusion.place, ...), custom_call_target="tpu_custom_call" | custom-call | flops 2147483648 | bytes 8388608 | tf_op jit(solution)/shard_map/weight_partial/pallas_call | solution.py:389
  117.3 2.8 %collective-permute-start.6 = (bf16[128,2048]{1,0:T(8,128)(2,1)}, bf16[128,2048]{1,0:T(8,128)(2,1)}, u32[]{:S(2)}, u32[]{:S(2)}) collective-permute-start(bf16[128,2048]{1,0:T(8,128)(2,1)} %get-tuple-element.54), channel_id=1, source_target_pairs={{0,96},{32,0},{64,32},{96,64},{1,97},{33,1},{65,33},{97,65},{2,98}... | collective-permute-start | bytes 1572872 | tf_op jit(solution)/shard_map/ppermute | solution.py:437
  120.1 1.3 copy-done.3
  121.4 4.3 %combine.1 = bf16[16,768,128]{2,1,0:T(8,128)(2,1)} custom-call(bf16[16,768,128]{2,1,0:T(8,128)(2,1)} %get-tuple-element.40.own_ref, bf16[16,512,128]{2,1,0:T(8,128)(2,1)} %copy-done.3), custom_call_target="tpu_custom_call", output_to_operand_aliasing={{}: (0, {})} | custom-call | flops 1048576 | bytes 6291456 | tf_op jit(solution)/shard_map/combine/pallas_call | solution.py:352
  125.8 6.9 %all-to-all-start.2 = ((bf16[16,768,128]{2,1,0:T(8,128)(2,1)}), bf16[16,768,128]{2,1,0:T(8,128)(2,1)S(1)}, u32[]{:S(2)}, u32[]{:S(2)}) async-start(bf16[16,768,128]{2,1,0:T(8,128)(2,1)} %combine.1), calls=%async_computation.2 | async-start | bytes 6291456 | tf_op jit(solution)/shard_map/all_to_all | solution.py:54
  132.7 1.4 add_convert_fusion.2
  134.2 0.0 copy-start.5
  134.2 2.8 %collective-permute-start.7 = (bf16[128,2048]{1,0:T(8,128)(2,1)S(1)}, bf16[128,2048]{1,0:T(8,128)(2,1)S(1)}, u32[]{:S(2)}, u32[]{:S(2)}) collective-permute-start(bf16[128,2048]{1,0:T(8,128)(2,1)S(1)} %add_convert_fusion.2), channel_id=1, source_target_pairs={{0,96},{32,0},{64,32},{96,64},{1,97},{33,1},{65,33},{97,65},{2,98}... | collective-permute-start | bytes 1572872 | tf_op jit(solution)/shard_map/ppermute | solution.py:437
  136.9 1.3 add_convert_fusion.5
  138.3 0.1 collective-permute-start.4
  138.4 9.3 %collective-permute-done.7 = bf16[128,2048]{1,0:T(8,128)(2,1)S(1)} collective-permute-done((bf16[128,2048]{1,0:T(8,128)(2,1)S(1)}, bf16[128,2048]{1,0:T(8,128)(2,1)S(1)}, u32[]{:S(2)}, u32[]{:S(2)}) %collective-permute-start.7) | collective-permute-done | bytes 524320 | tf_op jit(solution)/shard_map/ppermute | solution.py:437
  147.7 0.1 add_convert_fusion.1
  147.8 3.5 %collective-permute-start.8 = (bf16[128,2048]{1,0:T(8,128)(2,1)S(1)}, bf16[128,2048]{1,0:T(8,128)(2,1)S(1)}, u32[]{:S(2)}, u32[]{:S(2)}) collective-permute-start(bf16[128,2048]{1,0:T(8,128)(2,1)S(1)} %add_convert_fusion.1), channel_id=1, source_target_pairs={{0,96},{32,0},{64,32},{96,64},{1,97},{33,1},{65,33},{97,65},{2,98}... | collective-permute-start | bytes 1572872 | tf_op jit(solution)/shard_map/ppermute | solution.py:437
  151.3 0.9 collective-permute-done.4
  152.2 0.1 add_convert_fusion.4
  152.4 0.1 collective-permute-start.5
  152.5 8.4 %collective-permute-done.8 = bf16[128,2048]{1,0:T(8,128)(2,1)S(1)} collective-permute-done((bf16[128,2048]{1,0:T(8,128)(2,1)S(1)}, bf16[128,2048]{1,0:T(8,128)(2,1)S(1)}, u32[]{:S(2)}, u32[]{:S(2)}) %collective-permute-start.8) | collective-permute-done | bytes 524320 | tf_op jit(solution)/shard_map/ppermute | solution.py:437
  160.9 0.9 add_convert_fusion.b_ref
  161.8 3.6 %collective-permute-done.5 = bf16[128,2048]{1,0:T(8,128)(2,1)S(1)} collective-permute-done((bf16[128,2048]{1,0:T(8,128)(2,1)S(1)}, bf16[128,2048]{1,0:T(8,128)(2,1)S(1)}, u32[]{:S(2)}, u32[]{:S(2)}) %collective-permute-start.5) | collective-permute-done | bytes 524320 | tf_op jit(solution)/shard_map/ppermute | solution.py:436
  165.4 0.9 add_convert_fusion.3.a_ref
  166.4 8.8 %all-to-all-done.2.r_ref = bf16[16,768,128]{2,1,0:T(8,128)(2,1)S(1)} async-done(((bf16[16,768,128]{2,1,0:T(8,128)(2,1)}), bf16[16,768,128]{2,1,0:T(8,128)(2,1)S(1)}, u32[]{:S(2)}, u32[]{:S(2)}) %all-to-all-start.2) | async-done | bytes 3145760 | tf_op jit(solution)/shard_map/all_to_all | solution.py:54
  175.1 3.0 %join.1 = bf16[16,16,2048]{2,1,0:T(8,128)(2,1)} custom-call(bf16[128,2048]{1,0:T(8,128)(2,1)} %add_convert_fusion.3.a_ref, bf16[128,2048]{1,0:T(8,128)(2,1)} %add_convert_fusion.b_ref), custom_call_target="tpu_custom_call" | custom-call | bytes 2097152 | tf_op jit(solution)/shard_map/join/pallas_call | solution.py:420
  178.1 8.2 %all-to-all-start.3 = ((bf16[16,16,2048]{2,1,0:T(8,128)(2,1)}), bf16[16,16,2048]{2,1,0:T(8,128)(2,1)}, u32[]{:S(2)}, u32[]{:S(2)}) async-start(bf16[16,16,2048]{2,1,0:T(8,128)(2,1)} %join.1), calls=%async_computation.3 | async-start | bytes 2097152 | tf_op jit(solution)/shard_map/all_to_all | solution.py:54
  186.4 4.4 %unpack.1 = (bf16[256,2048]{1,0:T(8,128)(2,1)}, bf16[256,2048]{1,0:T(8,128)(2,1)}, bf16[256,2048]{1,0:T(8,128)(2,1)}) custom-call(bf16[16,768,128]{2,1,0:T(8,128)(2,1)} %copy-done.1), custom_call_target="tpu_custom_call" | custom-call | bytes 6291456 | tf_op jit(solution)/shard_map/unpack/pallas_call | solution.py:106
  190.7 11.5 %all-to-all-done.3 = bf16[16,16,2048]{2,1,0:T(8,128)(2,1)} async-done(((bf16[16,16,2048]{2,1,0:T(8,128)(2,1)}), bf16[16,16,2048]{2,1,0:T(8,128)(2,1)}, u32[]{:S(2)}, u32[]{:S(2)}) %all-to-all-start.3) | async-done | bytes 1048608 | tf_op jit(solution)/shard_map/all_to_all | solution.py:54
  202.2 2.0 convert_reduce_fusion
  (19 shorter events, 0.0 us)
Async XLA Ops:
  0.6 10.5 %collective-permute-start = (bf16[256,2048]{1,0:T(8,128)(2,1)}, bf16[256,2048]{1,0:T(8,128)(2,1)S(1)}, u32[]{:S(2)}, u32[]{:S(2)}) collective-permute-start(bf16[256,2048]{1,0:T(8,128)(2,1)} %bitcast.14), channel_id=1, source_target_pairs={{0,1},{1,0},{2,3},{3,2},{4,5},{5,4},{6,7},{7,6},{8,9},{9,8},{10,11... | collective-permute-start | bytes 3145736 | tf_op jit(solution)/shard_map/ppermute | solution.py:457
  11.2 60.1 %copy-start.9 = (bf16[256,2048]{1,0:T(8,128)(2,1)}, bf16[256,2048]{1,0:T(8,128)(2,1)S(1)}, u32[]{:S(2)}) copy-start(bf16[256,2048]{1,0:T(8,128)(2,1)S(1)} %collective-permute-done.cb_ref) | copy-start | bytes 3145732
  71.3 2.0 copy-start
  74.8 4.4 %collective-permute-start.1 = (bf16[16,512,128]{2,1,0:T(8,128)(2,1)}, bf16[16,512,128]{2,1,0:T(8,128)(2,1)S(1)}, u32[]{:S(2)}, u32[]{:S(2)}) collective-permute-start(bf16[16,512,128]{2,1,0:T(8,128)(2,1)} %slice.9), channel_id=1, source_target_pairs={{0,1},{1,0},{2,3},{3,2},{4,5},{5,4},{6,7},{7,6},{8,9},{9,8},{10,11... | collective-permute-start | bytes 6291464 | tf_op jit(solution)/shard_map/ppermute | solution.py:460
  79.2 1.3 copy-start.2
  88.4 22.0 %all-to-all-start.1 = ((bf16[32,64,256]{2,1,0:T(8,128)(2,1)}), bf16[32,64,256]{2,1,0:T(8,128)(2,1)S(1)}, u32[]{:S(2)}, u32[]{:S(2)}) async-start(bf16[32,64,256]{2,1,0:T(8,128)(2,1)} %get-tuple-element.36), calls=%async_computation.1 | async-start | bytes 2097152 | tf_op jit(solution)/shard_map/all_to_all | solution.py:465
  110.4 1.0 copy-start.4
  110.4 9.7 %collective-permute-start.2 = (bf16[16,512,128]{2,1,0:T(8,128)(2,1)}, bf16[16,512,128]{2,1,0:T(8,128)(2,1)S(1)}, u32[]{:S(2)}, u32[]{:S(2)}) collective-permute-start(bf16[16,512,128]{2,1,0:T(8,128)(2,1)} %get-tuple-element.48), channel_id=1, source_target_pairs={{0,1},{1,0},{2,3},{3,2},{4,5},{5,4},{6,7},{7,6},{8,9},{9,8},{10,11... | collective-permute-start | bytes 6291464 | tf_op jit(solution)/shard_map/ppermute | solution.py:468
  117.3 15.4 %collective-permute-start.6 = (bf16[128,2048]{1,0:T(8,128)(2,1)}, bf16[128,2048]{1,0:T(8,128)(2,1)}, u32[]{:S(2)}, u32[]{:S(2)}) collective-permute-start(bf16[128,2048]{1,0:T(8,128)(2,1)} %get-tuple-element.54), channel_id=1, source_target_pairs={{0,96},{32,0},{64,32},{96,64},{1,97},{33,1},{65,33},{97,65},{2,98}... | collective-permute-start | bytes 1572872 | tf_op jit(solution)/shard_map/ppermute | solution.py:437
  120.1 1.3 copy-start.3
  120.1 16.8 %collective-permute-start.3 = (bf16[128,2048]{1,0:T(8,128)(2,1)}, bf16[128,2048]{1,0:T(8,128)(2,1)}, u32[]{:S(2)}, u32[]{:S(2)}) collective-permute-start(bf16[128,2048]{1,0:T(8,128)(2,1)} %get-tuple-element.50), channel_id=1, source_target_pairs={{0,32},{32,64},{64,96},{96,0},{1,33},{33,65},{65,97},{97,1},{2,34}... | collective-permute-start | bytes 1572872 | tf_op jit(solution)/shard_map/ppermute | solution.py:436
  125.8 49.4 %all-to-all-start.2 = ((bf16[16,768,128]{2,1,0:T(8,128)(2,1)}), bf16[16,768,128]{2,1,0:T(8,128)(2,1)S(1)}, u32[]{:S(2)}, u32[]{:S(2)}) async-start(bf16[16,768,128]{2,1,0:T(8,128)(2,1)} %combine.1), calls=%async_computation.2 | async-start | bytes 6291456 | tf_op jit(solution)/shard_map/all_to_all | solution.py:54
  132.7 15.0 %copy-start.8 = (bf16[128,2048]{1,0:T(8,128)(2,1)S(1)}, bf16[128,2048]{1,0:T(8,128)(2,1)}, u32[]{:S(2)}) copy-start(bf16[128,2048]{1,0:T(8,128)(2,1)} %get-tuple-element.56) | copy-start | bytes 1572868
  132.7 19.6 %copy-start.7 = (bf16[128,2048]{1,0:T(8,128)(2,1)S(1)}, bf16[128,2048]{1,0:T(8,128)(2,1)}, u32[]{:S(2)}) copy-start(bf16[128,2048]{1,0:T(8,128)(2,1)} %get-tuple-element.52) | copy-start | bytes 1572868
  132.7 28.2 %copy-start.6 = (bf16[128,2048]{1,0:T(8,128)(2,1)S(1)}, bf16[128,2048]{1,0:T(8,128)(2,1)}, u32[]{:S(2)}) copy-start(bf16[128,2048]{1,0:T(8,128)(2,1)} %get-tuple-element.57) | copy-start | bytes 1572868
  134.2 31.3 %copy-start.5 = (bf16[128,2048]{1,0:T(8,128)(2,1)S(1)}, bf16[128,2048]{1,0:T(8,128)(2,1)}, u32[]{:S(2)}) copy-start(bf16[128,2048]{1,0:T(8,128)(2,1)} %get-tuple-element.53) | copy-start | bytes 1572868
  134.2 13.5 %collective-permute-start.7 = (bf16[128,2048]{1,0:T(8,128)(2,1)S(1)}, bf16[128,2048]{1,0:T(8,128)(2,1)S(1)}, u32[]{:S(2)}, u32[]{:S(2)}) collective-permute-start(bf16[128,2048]{1,0:T(8,128)(2,1)S(1)} %add_convert_fusion.2), channel_id=1, source_target_pairs={{0,96},{32,0},{64,32},{96,64},{1,97},{33,1},{65,33},{97,65},{2,98}... | collective-permute-start | bytes 1572872 | tf_op jit(solution)/shard_map/ppermute | solution.py:437
  138.3 14.0 %collective-permute-start.4 = (bf16[128,2048]{1,0:T(8,128)(2,1)S(1)}, bf16[128,2048]{1,0:T(8,128)(2,1)S(1)}, u32[]{:S(2)}, u32[]{:S(2)}) collective-permute-start(bf16[128,2048]{1,0:T(8,128)(2,1)S(1)} %add_convert_fusion.5), channel_id=1, source_target_pairs={{0,32},{32,64},{64,96},{96,0},{1,33},{33,65},{65,97},{97,1},{2,34}... | collective-permute-start | bytes 1572872 | tf_op jit(solution)/shard_map/ppermute | solution.py:436
  147.8 13.1 %collective-permute-start.8 = (bf16[128,2048]{1,0:T(8,128)(2,1)S(1)}, bf16[128,2048]{1,0:T(8,128)(2,1)S(1)}, u32[]{:S(2)}, u32[]{:S(2)}) collective-permute-start(bf16[128,2048]{1,0:T(8,128)(2,1)S(1)} %add_convert_fusion.1), channel_id=1, source_target_pairs={{0,96},{32,0},{64,32},{96,64},{1,97},{33,1},{65,33},{97,65},{2,98}... | collective-permute-start | bytes 1572872 | tf_op jit(solution)/shard_map/ppermute | solution.py:437
  152.4 13.1 %collective-permute-start.5 = (bf16[128,2048]{1,0:T(8,128)(2,1)S(1)}, bf16[128,2048]{1,0:T(8,128)(2,1)S(1)}, u32[]{:S(2)}, u32[]{:S(2)}) collective-permute-start(bf16[128,2048]{1,0:T(8,128)(2,1)S(1)} %add_convert_fusion.4), channel_id=1, source_target_pairs={{0,32},{32,64},{64,96},{96,0},{1,33},{33,65},{65,97},{97,1},{2,34}... | collective-permute-start | bytes 1572872 | tf_op jit(solution)/shard_map/ppermute | solution.py:436
  175.1 11.2 %copy-start.1 = (bf16[16,768,128]{2,1,0:T(8,128)(2,1)}, bf16[16,768,128]{2,1,0:T(8,128)(2,1)S(1)}, u32[]{:S(2)}) copy-start(bf16[16,768,128]{2,1,0:T(8,128)(2,1)S(1)} %all-to-all-done.2.r_ref) | copy-start | bytes 9437188
  178.1 24.1 %all-to-all-start.3 = ((bf16[16,16,2048]{2,1,0:T(8,128)(2,1)}), bf16[16,16,2048]{2,1,0:T(8,128)(2,1)}, u32[]{:S(2)}, u32[]{:S(2)}) async-start(bf16[16,16,2048]{2,1,0:T(8,128)(2,1)} %join.1), calls=%async_computation.3 | async-start | bytes 2097152 | tf_op jit(solution)/shard_map/all_to_all | solution.py:54

commit v6 on v4

--- a/solution.py
+++ b/solution.py
@@ -196,8 +196,10 @@
         for i in range(2):
             out, lse = block(c, i)
             for g in range(8):
-                row = (g % 2) * 64 + (g // 2) * 16
-                o_ref[c, row : row + 16, i * BLK : (i + 1) * BLK] = out[g * 16 : g * 16 + 16, :]
+                row = (g // 2) * 16
+                o_ref[2 * c + g % 2, row : row + 16, i * BLK : (i + 1) * BLK] = out[
+                    g * 16 : g * 16 + 16, :
+                ]
             lses.append(lse)
         row = lax.broadcasted_iota(jnp.int32, (8, 128), 0)
         lse_ref[c] = jnp.where(row == 0, lses[0], lses[1])
@@ -213,7 +215,7 @@
     return pl.pallas_call(
         forward_body,
         out_shape=(
-            jax.ShapeDtypeStruct((CHIPS, HEAD, TOK), bf16),
+            jax.ShapeDtypeStruct((2 * CHIPS, HEAD // 2, TOK), bf16),
             jax.ShapeDtypeStruct((CHIPS, 8, 128), f32),
         ),
         in_specs=[pl.BlockSpec(memory_space=pltpu.SMEM)] + [pl.BlockSpec(memory_space=pl.ANY)] * 2,
@@ -230,7 +232,7 @@
 
 
 def backward_body(
-    table, x_ref, y_ref, g_ref, lse_ref, home_ref, other_ref, kv, qs, gs, acck, accv, own, other, gq, sems
+    table, x_ref, y_ref, g_ref, lse_ref, own_ref, other_ref, gq_ref, kv, qs, gs, acck, accv, own, other, gq, sems
 ):
     groups = load_pool(x_ref, y_ref, kv, qs, sems)
     sends = []
@@ -241,10 +243,10 @@
         sends.append(
             [
                 pltpu.make_async_copy(
-                    gq.at[at], home_ref.at[at, pl.ds(2 * TOK, TOK), :], sems.at[4 * n + j]
+                    gq.at[at], gq_ref.at[at], sems.at[4 * n + j]
                 ),
                 pltpu.make_async_copy(
-                    own.at[at], home_ref.at[at, pl.ds(0, 2 * TOK), :], sems.at[5 * n + j]
+                    own.at[at], own_ref.at[at], sems.at[5 * n + j]
                 ),
                 pltpu.make_async_copy(other.at[at], other_ref.at[at], sems.at[6 * n + j]),
             ]
@@ -322,13 +324,14 @@
     return pl.pallas_call(
         backward_body,
         out_shape=(
-            jax.ShapeDtypeStruct((CHIPS, 3 * TOK, HEAD), bf16),
             jax.ShapeDtypeStruct((CHIPS, 2 * TOK, HEAD), bf16),
+            jax.ShapeDtypeStruct((CHIPS, 2 * TOK, HEAD), bf16),
+            jax.ShapeDtypeStruct((CHIPS, TOK, HEAD), bf16),
         ),
         in_specs=[pl.BlockSpec(memory_space=pltpu.SMEM)]
         + [pl.BlockSpec(memory_space=pl.ANY)] * 3
         + [pl.BlockSpec(memory_space=pltpu.VMEM)],
-        out_specs=[pl.BlockSpec(memory_space=pl.ANY)] * 2,
+        out_specs=[pl.BlockSpec(memory_space=pl.ANY)] * 3,
         scratch_shapes=[
             pltpu.VMEM((2 * CHIPS, 2 * TOK, HEAD), bf16),
             pltpu.VMEM((CHIPS, TOK, HEAD), bf16),
@@ -350,20 +353,19 @@
     o_ref[...] = (own_ref[...].astype(f32) + got_ref[...].astype(f32)).astype(bf16)
 
 
-def combine(home, got):
+def combine(own, got):
     n = 4
     rows = pl.BlockSpec((n, 2 * TOK, HEAD), lambda i: (i, 0, 0))
     return pl.pallas_call(
         combine_body,
-        out_shape=jax.ShapeDtypeStruct((CHIPS, 3 * TOK, HEAD), bf16),
+        out_shape=jax.ShapeDtypeStruct((CHIPS, 2 * TOK, HEAD), bf16),
         grid=(CHIPS // n,),
         in_specs=[rows, rows],
         out_specs=rows,
-        input_output_aliases={0: 0},
         compiler_params=pltpu.CompilerParams(vmem_limit_bytes=VMEM_LIMIT),
         cost_estimate=cost(CHIPS * 2 * TOK * HEAD, 0, 6 * MIB),
         name="combine",
-    )(home, got)
+    )(own, got)
 
 
 def weight_body(place, oa_ref, ob_ref, ca_ref, cb_ref, *rest):
@@ -386,8 +388,9 @@
         copy.wait()
 
 
-def weight_partial(place, oa, ob, ca, cb):
-    rows = pl.BlockSpec((HEADS, 64, TOK), lambda i, place: (0, place[0], 0))
+def weight_partial(place, out, ca, cb):
+    own = pl.BlockSpec((HEADS, 1, HEAD // 2, TOK), lambda i, place: (0, place[0], 0, 0))
+    other = pl.BlockSpec((HEADS, 1, HEAD // 2, TOK), lambda i, place: (0, 1 - place[0], 0, 0))
     whole = pl.BlockSpec((TOK, D), lambda i, place: (0, 0))
     outs = pl.pallas_call(
         weight_body,
@@ -395,7 +398,7 @@
         grid_spec=pltpu.PrefetchScalarGridSpec(
             num_scalar_prefetch=1,
             grid=(1,),
-            in_specs=[rows, rows, whole, whole],
+            in_specs=[own, other, whole, whole],
             out_specs=[pl.BlockSpec(memory_space=pl.ANY)] * (2 * DOCS),
             scratch_shapes=[
                 pltpu.VMEM((DOCS, 2 * CHUNK, D), bf16),
@@ -405,12 +408,33 @@
         compiler_params=pltpu.CompilerParams(vmem_limit_bytes=VMEM_LIMIT),
         cost_estimate=cost(2 * TOK * D * D, 0, 8 * MIB),
         name="weight_partial",
-    )(place, oa, ob, ca, cb)
+    )(place, out, out, ca, cb)
     return outs[0::2], outs[1::2]
 
 
 def plus(a, b):
     return (a.astype(f32) + b.astype(f32)).astype(bf16)
+
+
+def half_sum_body(a_ref, b_ref, *rest):
+    o_ref = rest[-1]
+    o_ref[...] = plus(a_ref[...], b_ref[...]).reshape(CHIPS // 2, 16, D)
+
+
+def half_sum(a, b, half, joined=None):
+    whole = pl.BlockSpec((CHUNK, D), lambda i: (0, 0))
+    args = (a, b) if joined is None else (a, b, joined)
+    return pl.pallas_call(
+        half_sum_body,
+        out_shape=jax.ShapeDtypeStruct((CHIPS, 16, D), bf16),
+        grid=(1,),
+        in_specs=[whole, whole] + [pl.BlockSpec(memory_space=pl.ANY)] * (len(args) - 2),
+        out_specs=pl.BlockSpec((CHIPS // 2, 16, D), lambda i: (half, 0, 0)),
+        input_output_aliases={} if joined is None else {2: 0},
+        compiler_params=pltpu.CompilerParams(vmem_limit_bytes=VMEM_LIMIT),
+        cost_estimate=cost(CHUNK * D, 0, 3 * MIB // 2),
+        name="half_sum",
+    )(*args)
 
 
 def sum_over_docs(up, down):
@@ -418,9 +442,12 @@
     route_down = [(i, (i - 1) % DOCS) for i in range(DOCS)]
     a, b = up[3], down[1]
     for step in range(1, DOCS):
-        a = plus(lax.ppermute(a, "dp", route_up), up[3 - step])
-        b = plus(lax.ppermute(b, "dp", route_down), down[(1 + step) % DOCS])
-    return a, b
+        a = lax.ppermute(a, "dp", route_up)
+        b = lax.ppermute(b, "dp", route_down)
+        if step < DOCS - 1:
+            a = plus(a, up[3 - step])
+            b = plus(b, down[1 + step])
+    return half_sum(b, down[0], 1, half_sum(a, up[0], 0))
 
 
 def block_table(rider, core):
@@ -442,25 +469,25 @@
     y = lax.ppermute(x, "seq", CORE_SWAP)
     g = exchange(g)
     table = block_table(x[:, RIDER, 0 : 2 * SLOTS], core)
+    table, place = after(table, jnp.stack([core, lax.axis_index("dp")]))
     out, lse = attention_forward(table, x, y)
     g, out = after(g, out)
-    out_home = exchange(out)
-    own, other = attention_backward(table, x, y, g, lse)
-    out_home, own, other = after(out_home, own, other)
-    out_other = lax.ppermute(out_home, "seq", CORE_SWAP)
-    out_other, other = after(out_other, other)
+    out_home = lax.all_to_all(out, "seq", 0, 0, tiled=True)
+    own, other, gq = attention_backward(table, x, y, g, lse)
+    out_home, own, other, gq = after(out_home, own, other, gq)
+    gq_home = exchange(gq)
     got = lax.ppermute(other, "seq", CORE_SWAP)
-    place = jnp.stack([core, lax.axis_index("dp")])
-    partial = weight_partial(place, out_home, out_other, cot, cot_other)
-    up, down = partial
+    got, out_home = after(got, out_home)
+    by_core = out_home.reshape(HEADS, 2, HEAD // 2, TOK)
+    up, down = weight_partial(place, by_core, cot, cot_other)
     *up, got = after(*up, got)
-    sums = sum_over_docs(up, down)
-    home = exchange(combine(own, got))
-    home, *sums = after(home, *sums)
-    by_doc = jnp.concatenate([part.reshape(CHIPS // 2, 16, D) for part in sums], axis=0)
-    pieces = exchange(by_doc)
-    weight_grad = jnp.sum(pieces.astype(f32), axis=0)
-    gk, gv, gq = unpack(home, 3)
+    by_doc = sum_over_docs(up, down)
+    gq_home, gathered = after(gq_home, combine(own, got))
+    kv_home = exchange(gathered)
+    kv_home, by_doc = after(kv_home, by_doc)
+    weight_grad = jnp.sum(exchange(by_doc).astype(f32), axis=0)
+    (gq,) = unpack(gq_home, 1)
+    gk, gv = unpack(kv_home, 2)
     return gq[None], gk[None], gv[None], weight_grad
 
 

time: 205 us -> 192 us (0.937)
  waiting for transfers between devices: 88.7 us -> 72.2 us
  Pallas kernels: 53.5 us -> 60.7 us
  other arithmetic: 11.3 us -> 5.17 us
    all_to_all x5, waiting for transfers between devices: 63.2 us -> 54.2 us  [exchange(): lax.all_to_all(x, 'seq', 0, 0, axis_index_groups=SAME_CORE, tiled=True)]
    ppermute x7 -> x6, waiting for transfers between devices: 25.5 us -> 18 us  [the longest x3 17.1 us: sum_over_docs(): a = lax.ppermute(a, 'dp', route_up)]
    pallas_call x3 -> x5, Pallas kernels: 30.1 us -> 34.3 us  [the longest x1 17.8 us: attention_backward(): pl.pallas_call(backward_body, out_shape=(jax.ShapeDtypeStruct((CHIPS, 2 *...]
    all_to_all x0 -> x1, starting transfers between devices: none -> 4.11 us  [local(): out_home = lax.all_to_all(out, 'seq', 0, 0, tiled=True)]
    all_to_all x5, starting transfers between devices: 37 us -> 33.8 us  [exchange(): lax.all_to_all(x, 'seq', 0, 0, axis_index_groups=SAME_CORE, tiled=True)]
    concatenate x1 -> x0, other arithmetic: 3.05 us -> none  [local(): jnp.concatenate([part.reshape(CHIPS // 2, 16, D) for part in sums], axis=0)]
    pallas_call x1 -> x2, Pallas kernels: 4.36 us -> 7.3 us  [unpack(): pl.pallas_call(unpack_body, out_shape=(out,) * n, grid=(HEADS // PACK,),...]
    convert_element_type x6 -> x4, other arithmetic: 4.86 us -> 2.98 us  [plus(): return (a.astype(f32) + b.astype(f32)).astype(bf16)]
  transfers between devices with their start and end apart: 15 -> 15, of which waited for: 9 -> 7; matrix products, arithmetic and copies ran while one was open for 3% -> 2% of each run, Pallas kernels for 24% -> 30%
where the time goes in v6:
time: 192 us; the launch traced here: 191 us
  waiting for transfers between devices  72.2 us (38%)
  Pallas kernels  60.7 us (32%)
  starting transfers between devices  48 us (25%)
  other arithmetic  5.17 us (3%)
  local copies, waits for them, and re-layouts  3.7 us (2%)
    all_to_all x5, waiting for transfers between devices, exchange(): lax.all_to_all(x, 'seq', 0, 0, axis_index_groups=SAME_CORE, tiled=True)  54.2 us
    all_to_all x5, starting transfers between devices, exchange(): lax.all_to_all(x, 'seq', 0, 0, axis_index_groups=SAME_CORE, tiled=True)  33.8 us
    pallas_call x1, Pallas kernels, attention_backward(): pl.pallas_call(backward_body, out_shape=(jax.ShapeDtypeStruct((CHIPS, 2 *...  17.8 us
    ppermute x3, waiting for transfers between devices, sum_over_docs(): a = lax.ppermute(a, 'dp', route_up)  17.1 us
    pallas_call x1, Pallas kernels, grad_attn_by_head(): pl.pallas_call(grad_attn_body, out_shape=jax.ShapeDtypeStruct((HEADS, TOK...  8.78 us
    pallas_call x1, Pallas kernels, attention_forward(): pl.pallas_call(forward_body, out_shape=(jax.ShapeDtypeStruct((2 * CHIPS,...  7.86 us
    pallas_call x2, Pallas kernels, unpack(): pl.pallas_call(unpack_body, out_shape=(out,) * n, grid=(HEADS // PACK,),...  7.3 us
    ppermute x3, starting transfers between devices, sum_over_docs(): b = lax.ppermute(b, 'dp', route_down)  6.56 us
  transfers between devices with their start and end apart: 15, of which 7 were waited for; matrix products, arithmetic and copies ran while one was open for 2% of the time, Pallas kernels for 30%

profile of v6, /device:TPU:0, one launch (start us, length us, event | category | flops | bytes accessed | tf_op | source)
XLA Modules:
  0.0 190.7 jit_solution(10819675493696812237)
XLA Ops:
  0.6 4.4 %pack.1 = bf16[16,776,128]{2,1,0:T(8,128)(2,1)} custom-call(s32[2,4]{1,0:T(2,128)} %bitcast.20, bf16[256,2048]{1,0:T(8,128)(2,1)} %bitcast.17, bf16[256,2048]{1,0:T(8,128)(2,1)} %bitcast.18, bf16[256,2048]{1,0:T(8,128)(2,1)} %bitcast.19), custom_call_target="tpu_custom_call" | custom-call | tf_op jit(solution)/shard_map/pack/pallas_call | solution.py:74
  5.0 8.1 %all-to-all-start = ((bf16[16,776,128]{2,1,0:T(8,128)(2,1)}), bf16[16,776,128]{2,1,0:T(8,128)(2,1)S(1)}, u32[]{:S(2)}, u32[]{:S(2)}) async-start(bf16[16,776,128]{2,1,0:T(8,128)(2,1)} %pack.1), calls=%async_computation | async-start | bytes 6356992 | tf_op jit(solution)/shard_map/all_to_all | solution.py:53
  13.1 0.1 collective-permute-start
  13.2 8.8 %grad_attn.1 = bf16[16,256,128]{2,1,0:T(8,128)(2,1)} custom-call(bf16[256,2048]{1,0:T(8,128)(2,1)} %bitcast.12, bf16[2048,2048]{1,0:T(8,128)(2,1)} %w_ref.1), custom_call_target="tpu_custom_call" | custom-call | flops 2147483648 | bytes 10485760 | tf_op jit(solution)/shard_map/grad_attn/pallas_call | solution.py:113
  22.0 33.9 %all-to-all-done.x_ref = bf16[16,776,128]{2,1,0:T(8,128)(2,1)S(1)} async-done(((bf16[16,776,128]{2,1,0:T(8,128)(2,1)}), bf16[16,776,128]{2,1,0:T(8,128)(2,1)S(1)}, u32[]{:S(2)}, u32[]{:S(2)}) %all-to-all-start) | async-done | bytes 3178528 | tf_op jit(solution)/shard_map/all_to_all | solution.py:53
  56.0 8.1 %all-to-all-start.1 = ((bf16[16,256,128]{2,1,0:T(8,128)(2,1)}), bf16[16,256,128]{2,1,0:T(8,128)(2,1)}, u32[]{:S(2)}, u32[]{:S(2)}) async-start(bf16[16,256,128]{2,1,0:T(8,128)(2,1)} %grad_attn.1), calls=%async_computation.1 | async-start | bytes 2097152 | tf_op jit(solution)/shard_map/all_to_all | solution.py:53
  64.1 0.1 iota_add_fusion
  64.2 0.1 add.62
  64.3 0.6 pad_add_fusion.place
  64.9 0.1 reshape.47
  65.0 0.7 add_select_fusion.table
  65.7 0.0 collective-permute-done.1.y_ref
  65.7 7.9 %attn_fwd.1 = (bf16[32,64,256]{2,1,0:T(8,128)(2,1)}, f32[16,8,128]{2,1,0:T(8,128)}) custom-call(s32[32,4]{1,0:T(8,128)} %add_select_fusion.table, bf16[16,776,128]{2,1,0:T(8,128)(2,1)} %copy-done, bf16[16,776,128]{2,1,0:T(8,128)(2,1)} %collective-permute-done.1.y_ref), custom_call_target="tpu_custom_call" | custom-call | flops 1342177280 | bytes 7340032 | tf_op jit(solution)/shard_map/attn_fwd/pallas_call | solution.py:215
  73.5 9.1 %all-to-all-done.1.g_ref = bf16[16,256,128]{2,1,0:T(8,128)(2,1)} async-done(((bf16[16,256,128]{2,1,0:T(8,128)(2,1)}), bf16[16,256,128]{2,1,0:T(8,128)(2,1)}, u32[]{:S(2)}, u32[]{:S(2)}) %all-to-all-start.1) | async-done | bytes 1048608 | tf_op jit(solution)/shard_map/all_to_all | solution.py:53
  82.6 4.1 %all-to-all-start.2 = ((bf16[32,64,256]{2,1,0:T(8,128)(2,1)}), bf16[32,64,256]{2,1,0:T(8,128)(2,1)S(1)}, u32[]{:S(2)}, u32[]{:S(2)}) async-start(bf16[32,64,256]{2,1,0:T(8,128)(2,1)} %get-tuple-element.45), calls=%async_computation.2 | async-start | bytes 2097152 | tf_op jit(solution)/shard_map/all_to_all | solution.py:475
  86.7 17.8 %attn_bwd.1 = (bf16[16,512,128]{2,1,0:T(8,128)(2,1)}, bf16[16,512,128]{2,1,0:T(8,128)(2,1)}, bf16[16,256,128]{2,1,0:T(8,128)(2,1)}) custom-call(s32[32,4]{1,0:T(8,128)} %add_select_fusion.table, bf16[16,776,128]{2,1,0:T(8,128)(2,1)} %copy-done, bf16[16,776,128]{2,1,0:T(8,128)(2,1)} %collective-permute-done.1.y_ref, ...), custom_call_target="tpu_custom_call" | custom-call | flops 3355443200 | bytes 14680064 | tf_op jit(solution)/shard_map/attn_bwd/pallas_call | solution.py:324
  104.6 0.0 copy-start.4
  104.6 1.0 copy-done.4
  105.6 7.1 %all-to-all-start.3 = ((bf16[16,256,128]{2,1,0:T(8,128)(2,1)}), bf16[16,256,128]{2,1,0:T(8,128)(2,1)S(1)}, u32[]{:S(2)}, u32[]{:S(2)}) async-start(bf16[16,256,128]{2,1,0:T(8,128)(2,1)} %get-tuple-element.51), calls=%async_computation.3 | async-start | bytes 2097152 | tf_op jit(solution)/shard_map/all_to_all | solution.py:53
  112.7 0.0 collective-permute-done.2.got_ref
  112.7 6.0 %weight_partial.1 = (bf16[128,2048]{1,0:T(8,128)(2,1)}, bf16[128,2048]{1,0:T(8,128)(2,1)}, bf16[128,2048]{1,0:T(8,128)(2,1)}, bf16[128,2048]{1,0:T(8,128)(2,1)},...) custom-call(s32[2]{0:T(128)} %pad_add_fusion.place, ...), custom_call_target="tpu_custom_call" | custom-call | flops 2147483648 | bytes 8388608 | tf_op jit(solution)/shard_map/weight_partial/pallas_call | solution.py:395
  118.7 1.6 collective-permute-start.6
  120.3 1.7 collective-permute-start.3
  122.0 4.3 %combine.1 = bf16[16,512,128]{2,1,0:T(8,128)(2,1)} custom-call(bf16[16,512,128]{2,1,0:T(8,128)(2,1)} %get-tuple-element.52.own_ref, bf16[16,512,128]{2,1,0:T(8,128)(2,1)} %copy-done.3), custom_call_target="tpu_custom_call" | custom-call | flops 1048576 | bytes 6291456 | tf_op jit(solution)/shard_map/combine/pallas_call | solution.py:359
  126.3 4.6 %all-to-all-done.3.r_ref = bf16[16,256,128]{2,1,0:T(8,128)(2,1)S(1)} async-done(((bf16[16,256,128]{2,1,0:T(8,128)(2,1)}), bf16[16,256,128]{2,1,0:T(8,128)(2,1)S(1)}, u32[]{:S(2)}, u32[]{:S(2)}) %all-to-all-start.3) | async-done | bytes 1048608 | tf_op jit(solution)/shard_map/all_to_all | solution.py:53
  131.0 1.0 copy-done.2
  131.9 3.7 %all-to-all-start.4 = ((bf16[16,512,128]{2,1,0:T(8,128)(2,1)}), bf16[16,512,128]{2,1,0:T(8,128)(2,1)S(1)}, u32[]{:S(2)}, u32[]{:S(2)}) async-start(bf16[16,512,128]{2,1,0:T(8,128)(2,1)} %combine.1), calls=%async_computation.4 | async-start | bytes 4194304 | tf_op jit(solution)/shard_map/all_to_all | solution.py:53
  135.7 1.4 add_convert_fusion.1
  137.1 1.6 collective-permute-start.7
  138.7 1.3 add_convert_fusion.3
  140.0 1.8 collective-permute-start.4
  141.8 8.9 %collective-permute-done.7 = bf16[128,2048]{1,0:T(8,128)(2,1)S(1)} collective-permute-done((bf16[128,2048]{1,0:T(8,128)(2,1)S(1)}, bf16[128,2048]{1,0:T(8,128)(2,1)S(1)}, u32[]{:S(2)}, u32[]{:S(2)}) %collective-permute-start.7) | collective-permute-done | bytes 524320 | tf_op jit(solution)/shard_map/ppermute | solution.py:445
  150.7 0.1 add_convert_fusion
  150.8 0.4 collective-permute-start.8
  151.2 0.9 collective-permute-done.4
  152.1 0.1 add_convert_fusion.2
  152.3 3.0 %collective-permute-start.5 = (bf16[128,2048]{1,0:T(8,128)(2,1)S(1)}, bf16[128,2048]{1,0:T(8,128)(2,1)S(1)}, u32[]{:S(2)}, u32[]{:S(2)}) collective-permute-start(bf16[128,2048]{1,0:T(8,128)(2,1)S(1)} %add_convert_fusion.2), channel_id=1, source_target_pairs={{0,96},{32,0},{64,32},{96,64},{1,97},{33,1},{65,33},{97,65},{2,98}... | collective-permute-start | bytes 1572872 | tf_op jit(solution)/shard_map/ppermute | solution.py:446
  155.3 8.2 %collective-permute-done.8.a_ref = bf16[128,2048]{1,0:T(8,128)(2,1)S(1)} collective-permute-done((bf16[128,2048]{1,0:T(8,128)(2,1)S(1)}, bf16[128,2048]{1,0:T(8,128)(2,1)S(1)}, u32[]{:S(2)}, u32[]{:S(2)}) %collective-permute-start.8) | collective-permute-done | bytes 524320 | tf_op jit(solution)/shard_map/ppermute | solution.py:445
  163.5 0.8 copy-done.7
  164.3 2.1 %half_sum.2.rest_0_ = bf16[16,16,2048]{2,1,0:T(8,128)(2,1)} custom-call(bf16[128,2048]{1,0:T(8,128)(2,1)} %copy-done.7, bf16[128,2048]{1,0:T(8,128)(2,1)} %get-tuple-element.73.b_ref), custom_call_target="tpu_custom_call" | custom-call | flops 262144 | bytes 1572864 | tf_op jit(solution)/shard_map/half_sum/pallas_call | solution.py:427
  166.4 0.0 collective-permute-done.5.a_ref
  166.4 0.8 copy-done.8
  167.2 2.1 %half_sum.3 = bf16[16,16,2048]{2,1,0:T(8,128)(2,1)} custom-call(bf16[128,2048]{1,0:T(8,128)(2,1)} %copy-done.8, bf16[128,2048]{1,0:T(8,128)(2,1)} %get-tuple-element.69.b_ref, bf16[16,16,2048]{2,1,0:T(8,128)(2,1)} %half_sum.2.rest_0_), custom_call_target="tpu_custom_call", output_to_operand_aliasing={{}: (2, {})} | custom-call | flops 262144 | bytes 1572864 | tf_op jit(solution)/shard_map/half_sum/pallas_call | solution.py:427
  169.4 6.7 %all-to-all-start.5 = ((bf16[16,16,2048]{2,1,0:T(8,128)(2,1)}), bf16[16,16,2048]{2,1,0:T(8,128)(2,1)S(1)}, u32[]{:S(2)}, u32[]{:S(2)}) async-start(bf16[16,16,2048]{2,1,0:T(8,128)(2,1)} %half_sum.3), calls=%async_computation.5 | async-start | bytes 2097152 | tf_op jit(solution)/shard_map/all_to_all | solution.py:53
  176.1 3.4 %unpack.2 = bf16[256,2048]{1,0:T(8,128)(2,1)} custom-call(bf16[16,256,128]{2,1,0:T(8,128)(2,1)} %copy-done.2), custom_call_target="tpu_custom_call" | custom-call | bytes 2097152 | tf_op jit(solution)/shard_map/unpack/pallas_call | solution.py:94
  179.5 3.9 %unpack.3 = (bf16[256,2048]{1,0:T(8,128)(2,1)}, bf16[256,2048]{1,0:T(8,128)(2,1)}) custom-call(bf16[16,512,128]{2,1,0:T(8,128)(2,1)} %copy-done.1), custom_call_target="tpu_custom_call" | custom-call | bytes 4194304 | tf_op jit(solution)/shard_map/unpack/pallas_call | solution.py:94
  183.4 6.5 %all-to-all-done.5 = bf16[16,16,2048]{2,1,0:T(8,128)(2,1)S(1)} async-done(((bf16[16,16,2048]{2,1,0:T(8,128)(2,1)}), bf16[16,16,2048]{2,1,0:T(8,128)(2,1)S(1)}, u32[]{:S(2)}, u32[]{:S(2)}) %all-to-all-start.5) | async-done | bytes 1048608 | tf_op jit(solution)/shard_map/all_to_all | solution.py:53
  189.9 0.8 convert_reduce_fusion
  (22 shorter events, 0.1 us)
Async XLA Ops:
  5.0 51.0 %all-to-all-start = ((bf16[16,776,128]{2,1,0:T(8,128)(2,1)}), bf16[16,776,128]{2,1,0:T(8,128)(2,1)S(1)}, u32[]{:S(2)}, u32[]{:S(2)}) async-start(bf16[16,776,128]{2,1,0:T(8,128)(2,1)} %pack.1), calls=%async_computation | async-start | bytes 6356992 | tf_op jit(solution)/shard_map/all_to_all | solution.py:53
  13.1 8.9 %collective-permute-start = (bf16[256,2048]{1,0:T(8,128)(2,1)}, bf16[256,2048]{1,0:T(8,128)(2,1)}, u32[]{:S(2)}, u32[]{:S(2)}) collective-permute-start(bf16[256,2048]{1,0:T(8,128)(2,1)} %bitcast.11), channel_id=1, source_target_pairs={{0,1},{1,0},{2,3},{3,2},{4,5},{5,4},{6,7},{7,6},{8,9},{9,8},{10,11... | collective-permute-start | bytes 3145736 | tf_op jit(solution)/shard_map/ppermute | solution.py:466
  56.0 9.7 %copy-start = (bf16[16,776,128]{2,1,0:T(8,128)(2,1)}, bf16[16,776,128]{2,1,0:T(8,128)(2,1)S(1)}, u32[]{:S(2)}) copy-start(bf16[16,776,128]{2,1,0:T(8,128)(2,1)S(1)} %all-to-all-done.x_ref) | copy-start | bytes 9535492
  56.0 9.7 %collective-permute-start.1 = (bf16[16,776,128]{2,1,0:T(8,128)(2,1)S(1)}, bf16[16,776,128]{2,1,0:T(8,128)(2,1)}, u32[]{:S(2)}, u32[]{:S(2)}) collective-permute-start(bf16[16,776,128]{2,1,0:T(8,128)(2,1)S(1)} %all-to-all-done.x_ref), channel_id=1, source_target_pairs={{0,1},{1,0},{2,3},{3,2},{4,5},{5,4},{6,7},{7,6},{8,9},{9,8},{10,11... | collective-permute-start | bytes 9535496 | tf_op jit(solution)/shard_map/ppermute | solution.py:469
  56.0 26.7 %all-to-all-start.1 = ((bf16[16,256,128]{2,1,0:T(8,128)(2,1)}), bf16[16,256,128]{2,1,0:T(8,128)(2,1)}, u32[]{:S(2)}, u32[]{:S(2)}) async-start(bf16[16,256,128]{2,1,0:T(8,128)(2,1)} %grad_attn.1), calls=%async_computation.1 | async-start | bytes 2097152 | tf_op jit(solution)/shard_map/all_to_all | solution.py:53
  82.6 22.0 %all-to-all-start.2 = ((bf16[32,64,256]{2,1,0:T(8,128)(2,1)}), bf16[32,64,256]{2,1,0:T(8,128)(2,1)S(1)}, u32[]{:S(2)}, u32[]{:S(2)}) async-start(bf16[32,64,256]{2,1,0:T(8,128)(2,1)} %get-tuple-element.45), calls=%async_computation.2 | async-start | bytes 2097152 | tf_op jit(solution)/shard_map/all_to_all | solution.py:475
  104.6 1.0 copy-start.4
  105.6 7.1 %collective-permute-start.2 = (bf16[16,512,128]{2,1,0:T(8,128)(2,1)}, bf16[16,512,128]{2,1,0:T(8,128)(2,1)S(1)}, u32[]{:S(2)}, u32[]{:S(2)}) collective-permute-start(bf16[16,512,128]{2,1,0:T(8,128)(2,1)} %get-tuple-element.54), channel_id=1, source_target_pairs={{0,1},{1,0},{2,3},{3,2},{4,5},{5,4},{6,7},{7,6},{8,9},{9,8},{10,11... | collective-permute-start | bytes 6291464 | tf_op jit(solution)/shard_map/ppermute | solution.py:479
  105.6 25.4 %all-to-all-start.3 = ((bf16[16,256,128]{2,1,0:T(8,128)(2,1)}), bf16[16,256,128]{2,1,0:T(8,128)(2,1)S(1)}, u32[]{:S(2)}, u32[]{:S(2)}) async-start(bf16[16,256,128]{2,1,0:T(8,128)(2,1)} %get-tuple-element.51), calls=%async_computation.3 | async-start | bytes 2097152 | tf_op jit(solution)/shard_map/all_to_all | solution.py:53
  112.7 6.0 %copy-start.3 = (bf16[16,512,128]{2,1,0:T(8,128)(2,1)}, bf16[16,512,128]{2,1,0:T(8,128)(2,1)S(1)}, u32[]{:S(2)}) copy-start(bf16[16,512,128]{2,1,0:T(8,128)(2,1)S(1)} %collective-permute-done.2.got_ref) | copy-start | bytes 6291460
  118.7 17.0 %collective-permute-start.6 = (bf16[128,2048]{1,0:T(8,128)(2,1)}, bf16[128,2048]{1,0:T(8,128)(2,1)}, u32[]{:S(2)}, u32[]{:S(2)}) collective-permute-start(bf16[128,2048]{1,0:T(8,128)(2,1)} %get-tuple-element.70), channel_id=1, source_target_pairs={{0,32},{32,64},{64,96},{96,0},{1,33},{33,65},{65,97},{97,1},{2,34}... | collective-permute-start | bytes 1572872 | tf_op jit(solution)/shard_map/ppermute | solution.py:445
  120.3 18.4 %collective-permute-start.3 = (bf16[128,2048]{1,0:T(8,128)(2,1)}, bf16[128,2048]{1,0:T(8,128)(2,1)}, u32[]{:S(2)}, u32[]{:S(2)}) collective-permute-start(bf16[128,2048]{1,0:T(8,128)(2,1)} %get-tuple-element.66), channel_id=1, source_target_pairs={{0,96},{32,0},{64,32},{96,64},{1,97},{33,1},{65,33},{97,65},{2,98}... | collective-permute-start | bytes 1572872 | tf_op jit(solution)/shard_map/ppermute | solution.py:446
  131.0 1.0 copy-start.2
  131.9 37.4 %all-to-all-start.4 = ((bf16[16,512,128]{2,1,0:T(8,128)(2,1)}), bf16[16,512,128]{2,1,0:T(8,128)(2,1)S(1)}, u32[]{:S(2)}, u32[]{:S(2)}) async-start(bf16[16,512,128]{2,1,0:T(8,128)(2,1)} %combine.1), calls=%async_computation.4 | async-start | bytes 4194304 | tf_op jit(solution)/shard_map/all_to_all | solution.py:53
  135.7 15.0 %copy-start.6 = (bf16[128,2048]{1,0:T(8,128)(2,1)S(1)}, bf16[128,2048]{1,0:T(8,128)(2,1)}, u32[]{:S(2)}) copy-start(bf16[128,2048]{1,0:T(8,128)(2,1)} %get-tuple-element.72) | copy-start | bytes 1572868
  135.7 16.4 %copy-start.5 = (bf16[128,2048]{1,0:T(8,128)(2,1)S(1)}, bf16[128,2048]{1,0:T(8,128)(2,1)}, u32[]{:S(2)}) copy-start(bf16[128,2048]{1,0:T(8,128)(2,1)} %get-tuple-element.68) | copy-start | bytes 1572868
  137.1 13.6 %collective-permute-start.7 = (bf16[128,2048]{1,0:T(8,128)(2,1)S(1)}, bf16[128,2048]{1,0:T(8,128)(2,1)S(1)}, u32[]{:S(2)}, u32[]{:S(2)}) collective-permute-start(bf16[128,2048]{1,0:T(8,128)(2,1)S(1)} %add_convert_fusion.1), channel_id=1, source_target_pairs={{0,32},{32,64},{64,96},{96,0},{1,33},{33,65},{65,97},{97,1},{2,34}... | collective-permute-start | bytes 1572872 | tf_op jit(solution)/shard_map/ppermute | solution.py:445
  140.0 12.1 %collective-permute-start.4 = (bf16[128,2048]{1,0:T(8,128)(2,1)S(1)}, bf16[128,2048]{1,0:T(8,128)(2,1)S(1)}, u32[]{:S(2)}, u32[]{:S(2)}) collective-permute-start(bf16[128,2048]{1,0:T(8,128)(2,1)S(1)} %add_convert_fusion.3), channel_id=1, source_target_pairs={{0,96},{32,0},{64,32},{96,64},{1,97},{33,1},{65,33},{97,65},{2,98}... | collective-permute-start | bytes 1572872 | tf_op jit(solution)/shard_map/ppermute | solution.py:446
  150.8 12.7 %collective-permute-start.8 = (bf16[128,2048]{1,0:T(8,128)(2,1)S(1)}, bf16[128,2048]{1,0:T(8,128)(2,1)S(1)}, u32[]{:S(2)}, u32[]{:S(2)}) collective-permute-start(bf16[128,2048]{1,0:T(8,128)(2,1)S(1)} %add_convert_fusion), channel_id=1, source_target_pairs={{0,32},{32,64},{64,96},{96,0},{1,33},{33,65},{65,97},{97,1},{2,34}... | collective-permute-start | bytes 1572872 | tf_op jit(solution)/shard_map/ppermute | solution.py:445
  152.3 14.2 %collective-permute-start.5 = (bf16[128,2048]{1,0:T(8,128)(2,1)S(1)}, bf16[128,2048]{1,0:T(8,128)(2,1)S(1)}, u32[]{:S(2)}, u32[]{:S(2)}) collective-permute-start(bf16[128,2048]{1,0:T(8,128)(2,1)S(1)} %add_convert_fusion.2), channel_id=1, source_target_pairs={{0,96},{32,0},{64,32},{96,64},{1,97},{33,1},{65,33},{97,65},{2,98}... | collective-permute-start | bytes 1572872 | tf_op jit(solution)/shard_map/ppermute | solution.py:446
  163.5 0.8 copy-start.7
  166.4 0.8 copy-start.8
  169.4 10.2 %copy-start.1 = (bf16[16,512,128]{2,1,0:T(8,128)(2,1)}, bf16[16,512,128]{2,1,0:T(8,128)(2,1)S(1)}, u32[]{:S(2)}) copy-start(bf16[16,512,128]{2,1,0:T(8,128)(2,1)S(1)} %all-to-all-done.4.r_ref) | copy-start | bytes 6291460
  169.4 20.5 %all-to-all-start.5 = ((bf16[16,16,2048]{2,1,0:T(8,128)(2,1)}), bf16[16,16,2048]{2,1,0:T(8,128)(2,1)S(1)}, u32[]{:S(2)}, u32[]{:S(2)}) async-start(bf16[16,16,2048]{2,1,0:T(8,128)(2,1)} %half_sum.3), calls=%async_computation.5 | async-start | bytes 2097152 | tf_op jit(solution)/shard_map/all_to_all | solution.py:53

commit v7 on v6

--- a/solution.py
+++ b/solution.py
@@ -15,6 +15,7 @@
 TOK = 256
 CHIPS = 16
 BLOCKS = 64
+WIDTH = (1 + SLOTS) * BLK
 DOCS = 4
 CHUNK = D // 4 // DOCS
 RIDER = 3 * TOK
@@ -163,7 +164,7 @@
     return u <= t
 
 
-def forward_body(table, x_ref, y_ref, o_ref, lse_ref, kv, qs, sems):
+def forward_body(table, x_ref, y_ref, o_ref, p_ref, kv, qs, ps, sems):
     groups = load_pool(x_ref, y_ref, kv, qs, sems)
     for copies in groups:
         for copy in copies:
@@ -186,29 +187,33 @@
             w = jnp.exp2(s * SCALE2 - (peak if bias is None else peak + bias))
             part = jnp.sum(w, axis=0, keepdims=True)
             total = part if total is None else total + part
-            weights.append(w.astype(bf16))
+            weights.append(w)
+        inverse = 1.0 / total
+        prob = jnp.concatenate([(w * inverse).astype(bf16) for w in weights], axis=0)
+        ps[2 * c + i] = prob
         values = jnp.concatenate([kv[p, pl.ds(TOK + r, BLK), :] for p, r, _ in places], axis=0)
-        out = dot(values, jnp.concatenate(weights, axis=0), 0, 0) * (1.0 / total)
-        return out.astype(bf16), peak + jnp.log2(total)
+        return dot(values, prob, 0, 0).astype(bf16)
 
     def step(c, carry):
-        lses = []
         for i in range(2):
-            out, lse = block(c, i)
+            out = block(c, i)
             for g in range(8):
                 row = (g // 2) * 16
                 o_ref[2 * c + g % 2, row : row + 16, i * BLK : (i + 1) * BLK] = out[
                     g * 16 : g * 16 + 16, :
                 ]
-            lses.append(lse)
-        row = lax.broadcasted_iota(jnp.int32, (8, 128), 0)
-        lse_ref[c] = jnp.where(row == 0, lses[0], lses[1])
         return carry
 
+    sends = []
     for j, copies in enumerate(groups):
         for copy in copies:
             copy.wait()
         lax.fori_loop(j * GROUP, (j + 1) * GROUP, step, 0, unroll=UNROLL)
+        at = pl.ds(2 * j * GROUP, 2 * GROUP)
+        sends.append(pltpu.make_async_copy(ps.at[at], p_ref.at[at], sems.at[3 * len(groups) + j]))
+        sends[j].start()
+    for copy in sends:
+        copy.wait()
 
 
 def attention_forward(table, x, y):
@@ -216,23 +221,24 @@
         forward_body,
         out_shape=(
             jax.ShapeDtypeStruct((2 * CHIPS, HEAD // 2, TOK), bf16),
-            jax.ShapeDtypeStruct((CHIPS, 8, 128), f32),
+            jax.ShapeDtypeStruct((2 * CHIPS, WIDTH, BLK), bf16),
         ),
         in_specs=[pl.BlockSpec(memory_space=pltpu.SMEM)] + [pl.BlockSpec(memory_space=pl.ANY)] * 2,
-        out_specs=[pl.BlockSpec(memory_space=pltpu.VMEM)] * 2,
+        out_specs=[pl.BlockSpec(memory_space=pltpu.VMEM), pl.BlockSpec(memory_space=pl.ANY)],
         scratch_shapes=[
             pltpu.VMEM((2 * CHIPS, 2 * TOK, HEAD), bf16),
             pltpu.VMEM((CHIPS, TOK, HEAD), bf16),
-            pltpu.SemaphoreType.DMA((3 * (CHIPS // GROUP),)),
+            pltpu.VMEM((2 * CHIPS, WIDTH, BLK), bf16),
+            pltpu.SemaphoreType.DMA((4 * (CHIPS // GROUP),)),
         ],
         compiler_params=pltpu.CompilerParams(vmem_limit_bytes=VMEM_LIMIT),
-        cost_estimate=cost(2 * PAIR_FLOPS, PAIRS, 7 * MIB),
+        cost_estimate=cost(2 * PAIR_FLOPS, PAIRS, 12 * MIB),
         name="attn_fwd",
     )(table, x, y)
 
 
 def backward_body(
-    table, x_ref, y_ref, g_ref, lse_ref, own_ref, other_ref, gq_ref, kv, qs, gs, acck, accv, own, other, gq, sems
+    table, x_ref, y_ref, g_ref, p_ref, own_ref, other_ref, gq_ref, kv, qs, gs, ps, acck, accv, own, other, gq, sems
 ):
     groups = load_pool(x_ref, y_ref, kv, qs, sems)
     sends = []
@@ -240,6 +246,8 @@
     for j in range(n):
         at = pl.ds(j * GROUP, GROUP)
         groups[j].append(pltpu.make_async_copy(g_ref.at[at], gs.at[at], sems.at[3 * n + j]))
+        two = pl.ds(2 * j * GROUP, 2 * GROUP)
+        groups[j].append(pltpu.make_async_copy(p_ref.at[two], ps.at[two], sems.at[7 * n + j]))
         sends.append(
             [
                 pltpu.make_async_copy(
@@ -266,23 +274,15 @@
         places = listed(table, c, i)
         q = qs[c, pl.ds(i * BLK, BLK), :]
         g = gs[c, pl.ds(i * BLK, BLK), :]
-        lse = lse_ref[c, i : i + 1, :]
         keys = jnp.concatenate([kv[p, pl.ds(r, BLK), :] for p, r, _ in places], axis=0)
         values = jnp.concatenate([kv[p, pl.ds(TOK + r, BLK), :] for p, r, _ in places], axis=0)
-        every = dot(keys, q, 1, 1)
         grads = dot(values, g, 1, 1)
-        probs = []
-        for j, (_, _, bias) in enumerate(places):
-            s = every[j * BLK : (j + 1) * BLK, :]
-            prob = jnp.exp2(s * SCALE2 - (lse if bias is None else lse + bias))
-            if bias is None:
-                prob = jnp.where(causal(), prob, 0.0)
-            probs.append(prob)
-        prob = jnp.concatenate(probs, axis=0)
+        low = ps[2 * c + i]
+        prob = low.astype(f32)
         row_dot = jnp.sum(prob * grads, axis=0, keepdims=True)
         score = (prob * (grads - row_dot)).astype(bf16)
         gk = dot(score, q, 1, 0)
-        gv = dot(prob.astype(bf16), g, 1, 0)
+        gv = dot(low, g, 1, 0)
         for j, (p, r, _) in enumerate(places):
             at = pl.ds(r, BLK)
             if j == 0:
@@ -320,7 +320,7 @@
             copy.wait()
 
 
-def attention_backward(table, x, y, g, lse):
+def attention_backward(table, x, y, g, prob):
     return pl.pallas_call(
         backward_body,
         out_shape=(
@@ -329,24 +329,24 @@
             jax.ShapeDtypeStruct((CHIPS, TOK, HEAD), bf16),
         ),
         in_specs=[pl.BlockSpec(memory_space=pltpu.SMEM)]
-        + [pl.BlockSpec(memory_space=pl.ANY)] * 3
-        + [pl.BlockSpec(memory_space=pltpu.VMEM)],
+        + [pl.BlockSpec(memory_space=pl.ANY)] * 4,
         out_specs=[pl.BlockSpec(memory_space=pl.ANY)] * 3,
         scratch_shapes=[
             pltpu.VMEM((2 * CHIPS, 2 * TOK, HEAD), bf16),
             pltpu.VMEM((CHIPS, TOK, HEAD), bf16),
             pltpu.VMEM((CHIPS, TOK, HEAD), bf16),
+            pltpu.VMEM((2 * CHIPS, WIDTH, BLK), bf16),
             pltpu.VMEM((2 * CHIPS, TOK, HEAD), f32),
             pltpu.VMEM((2 * CHIPS, TOK, HEAD), f32),
             pltpu.VMEM((CHIPS, 2 * TOK, HEAD), bf16),
             pltpu.VMEM((CHIPS, 2 * TOK, HEAD), bf16),
             pltpu.VMEM((CHIPS, TOK, HEAD), bf16),
-            pltpu.SemaphoreType.DMA((7 * (CHIPS // GROUP),)),
+            pltpu.SemaphoreType.DMA((8 * (CHIPS // GROUP),)),
         ],
         compiler_params=pltpu.CompilerParams(vmem_limit_bytes=VMEM_LIMIT),
-        cost_estimate=cost(5 * PAIR_FLOPS, PAIRS, 14 * MIB),
+        cost_estimate=cost(4 * PAIR_FLOPS, 0, 17 * MIB),
         name="attn_bwd",
-    )(table, x, y, g, lse)
+    )(table, x, y, g, prob)
 
 
 def combine_body(own_ref, got_ref, o_ref):
@@ -416,38 +416,20 @@
     return (a.astype(f32) + b.astype(f32)).astype(bf16)
 
 
-def half_sum_body(a_ref, b_ref, *rest):
-    o_ref = rest[-1]
-    o_ref[...] = plus(a_ref[...], b_ref[...]).reshape(CHIPS // 2, 16, D)
-
-
-def half_sum(a, b, half, joined=None):
-    whole = pl.BlockSpec((CHUNK, D), lambda i: (0, 0))
-    args = (a, b) if joined is None else (a, b, joined)
-    return pl.pallas_call(
-        half_sum_body,
-        out_shape=jax.ShapeDtypeStruct((CHIPS, 16, D), bf16),
-        grid=(1,),
-        in_specs=[whole, whole] + [pl.BlockSpec(memory_space=pl.ANY)] * (len(args) - 2),
-        out_specs=pl.BlockSpec((CHIPS // 2, 16, D), lambda i: (half, 0, 0)),
-        input_output_aliases={} if joined is None else {2: 0},
-        compiler_params=pltpu.CompilerParams(vmem_limit_bytes=VMEM_LIMIT),
-        cost_estimate=cost(CHUNK * D, 0, 3 * MIB // 2),
-        name="half_sum",
-    )(*args)
-
-
-def sum_over_docs(up, down):
+def sum_over_docs(up, down, room, first):
     route_up = [(i, (i + 1) % DOCS) for i in range(DOCS)]
     route_down = [(i, (i - 1) % DOCS) for i in range(DOCS)]
     a, b = up[3], down[1]
     for step in range(1, DOCS):
         a = lax.ppermute(a, "dp", route_up)
         b = lax.ppermute(b, "dp", route_down)
-        if step < DOCS - 1:
-            a = plus(a, up[3 - step])
-            b = plus(b, down[1 + step])
-    return half_sum(b, down[0], 1, half_sum(a, up[0], 0))
+        if step == 1:
+            a, b, first = after(a, b, first)
+        a = plus(a, up[3 - step])
+        b = plus(b, down[(1 + step) % DOCS])
+    n = CHIPS // 2
+    joined = lax.dynamic_update_slice(room, a.reshape(n, 16, D), (0, 0, 0))
+    return lax.dynamic_update_slice(joined, b.reshape(n, 16, D), (n, 0, 0)), first
 
 
 def block_table(rider, core):
@@ -470,10 +452,10 @@
     g = exchange(g)
     table = block_table(x[:, RIDER, 0 : 2 * SLOTS], core)
     table, place = after(table, jnp.stack([core, lax.axis_index("dp")]))
-    out, lse = attention_forward(table, x, y)
+    out, prob = attention_forward(table, x, y)
     g, out = after(g, out)
     out_home = lax.all_to_all(out, "seq", 0, 0, tiled=True)
-    own, other, gq = attention_backward(table, x, y, g, lse)
+    own, other, gq = attention_backward(table, x, y, g, prob)
     out_home, own, other, gq = after(out_home, own, other, gq)
     gq_home = exchange(gq)
     got = lax.ppermute(other, "seq", CORE_SWAP)
@@ -481,8 +463,8 @@
     by_core = out_home.reshape(HEADS, 2, HEAD // 2, TOK)
     up, down = weight_partial(place, by_core, cot, cot_other)
     *up, got = after(*up, got)
-    by_doc = sum_over_docs(up, down)
-    gq_home, gathered = after(gq_home, combine(own, got))
+    room = jnp.zeros((CHIPS, 16, D), bf16)
+    by_doc, (gq_home, gathered) = sum_over_docs(up, down, room, (gq_home, combine(own, got)))
     kv_home = exchange(gathered)
     kv_home, by_doc = after(kv_home, by_doc)
     weight_grad = jnp.sum(exchange(by_doc).astype(f32), axis=0)

time: 192 us -> 191 us (level)
  waiting for transfers between devices: 72.2 us -> 81.8 us
  Pallas kernels: 60.7 us -> 52.9 us
  local copies, waits for them, and re-layouts: 3.7 us -> 0.79 us
  other arithmetic: 5.17 us -> 8.06 us
  starting transfers between devices: 48 us -> 45.2 us
    all_to_all x5, waiting for transfers between devices: 54.2 us -> 61.5 us  [exchange(): lax.all_to_all(x, 'seq', 0, 0, axis_index_groups=SAME_CORE, tiled=True)]
    pallas_call x1, Pallas kernels: 17.8 us -> 12.6 us  [attention_backward(): pl.pallas_call(backward_body, out_shape=(jax.ShapeDtypeStruct((CHIPS, 2 *...]
    pallas_call x2 -> x0, Pallas kernels: 4.26 us -> none  [half_sum(): pl.pallas_call(half_sum_body, out_shape=jax.ShapeDtypeStruct((CHIPS, 16,...]
    all_to_all x1, waiting for transfers between devices: 0.01 us -> 4.01 us  [local(): out_home = lax.all_to_all(out, 'seq', 0, 0, tiled=True)]
    all_to_all x5, starting transfers between devices: 33.8 us -> 30.7 us  [exchange(): lax.all_to_all(x, 'seq', 0, 0, axis_index_groups=SAME_CORE, tiled=True)]
    unnamed x18, local copies, waits for them, and re-layouts: 3.54 us -> 0.63 us
    convert_element_type x4 -> x6, other arithmetic: 2.98 us -> 4.76 us  [plus(): return (a.astype(f32) + b.astype(f32)).astype(bf16)]
  transfers between devices with their start and end apart: 15 -> 15, of which waited for: 7 -> 10; matrix products, arithmetic and copies ran while one was open for 2% -> 3% of each run, Pallas kernels for 30% -> 26%
where the time goes in v7:
time: 191 us; the launch traced here: 190 us
  waiting for transfers between devices  81.8 us (43%)
  Pallas kernels  52.9 us (28%)
  starting transfers between devices  45.2 us (24%)
  other arithmetic  8.06 us (4%)
    all_to_all x5, waiting for transfers between devices, exchange(): lax.all_to_all(x, 'seq', 0, 0, axis_index_groups=SAME_CORE, tiled=True)  61.5 us
    all_to_all x5, starting transfers between devices, exchange(): lax.all_to_all(x, 'seq', 0, 0, axis_index_groups=SAME_CORE, tiled=True)  30.7 us
    ppermute x3, waiting for transfers between devices, sum_over_docs(): a = lax.ppermute(a, 'dp', route_up)  15.8 us
    pallas_call x1, Pallas kernels, attention_backward(): pl.pallas_call(backward_body, out_shape=(jax.ShapeDtypeStruct((CHIPS, 2 *...  12.6 us
    pallas_call x1, Pallas kernels, attention_forward(): pl.pallas_call(forward_body, out_shape=(jax.ShapeDtypeStruct((2 * CHIPS,...  9.6 us
    pallas_call x1, Pallas kernels, grad_attn_by_head(): pl.pallas_call(grad_attn_body, out_shape=jax.ShapeDtypeStruct((HEADS, TOK...  8.78 us
    pallas_call x2, Pallas kernels, unpack(): pl.pallas_call(unpack_body, out_shape=(out,) * n, grid=(HEADS // PACK,),...  7.3 us
    ppermute x3, starting transfers between devices, sum_over_docs(): b = lax.ppermute(b, 'dp', route_down)  6.78 us
  transfers between devices with their start and end apart: 15, of which 10 were waited for; matrix products, arithmetic and copies ran while one was open for 3% of the time, Pallas kernels for 26%

profile of v7, /device:TPU:0, one launch (start us, length us, event | category | flops | bytes accessed | tf_op | source)
XLA Modules:
  0.0 189.6 jit_solution(6506048811245201614)
XLA Ops:
  0.6 4.4 %pack.1 = bf16[16,776,128]{2,1,0:T(8,128)(2,1)} custom-call(s32[2,4]{1,0:T(2,128)} %bitcast.24, bf16[256,2048]{1,0:T(8,128)(2,1)} %bitcast.21, bf16[256,2048]{1,0:T(8,128)(2,1)} %bitcast.22, bf16[256,2048]{1,0:T(8,128)(2,1)} %bitcast.23), custom_call_target="tpu_custom_call" | custom-call | tf_op jit(solution)/shard_map/pack/pallas_call | solution.py:75
  5.0 8.1 %all-to-all-start = ((bf16[16,776,128]{2,1,0:T(8,128)(2,1)}), bf16[16,776,128]{2,1,0:T(8,128)(2,1)S(1)}, u32[]{:S(2)}, u32[]{:S(2)}) async-start(bf16[16,776,128]{2,1,0:T(8,128)(2,1)} %pack.1), calls=%async_computation | async-start | bytes 6356992 | tf_op jit(solution)/shard_map/all_to_all | solution.py:54
  13.1 0.1 collective-permute-start
  13.2 8.8 %grad_attn.1 = bf16[16,256,128]{2,1,0:T(8,128)(2,1)} custom-call(bf16[256,2048]{1,0:T(8,128)(2,1)} %bitcast.16, bf16[2048,2048]{1,0:T(8,128)(2,1)} %w_ref.1), custom_call_target="tpu_custom_call" | custom-call | flops 2147483648 | bytes 10485760 | tf_op jit(solution)/shard_map/grad_attn/pallas_call | solution.py:114
  22.0 0.0 collective-permute-done.cb_ref
  22.0 33.9 %all-to-all-done.x_ref = bf16[16,776,128]{2,1,0:T(8,128)(2,1)S(1)} async-done(((bf16[16,776,128]{2,1,0:T(8,128)(2,1)}), bf16[16,776,128]{2,1,0:T(8,128)(2,1)S(1)}, u32[]{:S(2)}, u32[]{:S(2)}) %all-to-all-start) | async-done | bytes 3178528 | tf_op jit(solution)/shard_map/all_to_all | solution.py:54
  56.0 8.1 %all-to-all-start.1 = ((bf16[16,256,128]{2,1,0:T(8,128)(2,1)}), bf16[16,256,128]{2,1,0:T(8,128)(2,1)}, u32[]{:S(2)}, u32[]{:S(2)}) async-start(bf16[16,256,128]{2,1,0:T(8,128)(2,1)} %grad_attn.1), calls=%async_computation.1 | async-start | bytes 2097152 | tf_op jit(solution)/shard_map/all_to_all | solution.py:54
  64.1 0.1 iota_add_fusion
  64.2 0.1 add.68
  64.3 0.6 pad_add_fusion.place
  64.9 0.1 reshape.55
  65.0 0.7 add_select_fusion.table
  65.7 9.6 %attn_fwd.1 = (bf16[32,64,256]{2,1,0:T(8,128)(2,1)}, bf16[32,640,128]{2,1,0:T(8,128)(2,1)}) custom-call(s32[32,4]{1,0:T(8,128)} %add_select_fusion.table, bf16[16,776,128]{2,1,0:T(8,128)(2,1)} %copy-done, bf16[16,776,128]{2,1,0:T(8,128)(2,1)} %collective-permute-done.1.y_ref), custom_call_target="tpu_custom_call" | custom-call | flops 1342177280 | bytes 12582912 | tf_op jit(solution)/shard_map/attn_fwd/pallas_call | solution.py:220
  75.3 7.3 %all-to-all-done.1.g_ref = bf16[16,256,128]{2,1,0:T(8,128)(2,1)} async-done(((bf16[16,256,128]{2,1,0:T(8,128)(2,1)}), bf16[16,256,128]{2,1,0:T(8,128)(2,1)}, u32[]{:S(2)}, u32[]{:S(2)}) %all-to-all-start.1) | async-done | bytes 1048608 | tf_op jit(solution)/shard_map/all_to_all | solution.py:54
  82.6 4.1 %all-to-all-start.2 = ((bf16[32,64,256]{2,1,0:T(8,128)(2,1)}), bf16[32,64,256]{2,1,0:T(8,128)(2,1)S(1)}, u32[]{:S(2)}, u32[]{:S(2)}) async-start(bf16[32,64,256]{2,1,0:T(8,128)(2,1)} %get-tuple-element.48), calls=%async_computation.2 | async-start | bytes 2097152 | tf_op jit(solution)/shard_map/all_to_all | solution.py:457
  86.7 12.6 %attn_bwd.1 = (bf16[16,512,128]{2,1,0:T(8,128)(2,1)}, bf16[16,512,128]{2,1,0:T(8,128)(2,1)}, bf16[16,256,128]{2,1,0:T(8,128)(2,1)}) custom-call(s32[32,4]{1,0:T(8,128)} %add_select_fusion.table, bf16[16,776,128]{2,1,0:T(8,128)(2,1)} %copy-done, bf16[16,776,128]{2,1,0:T(8,128)(2,1)} %collective-permute-done.1.y_ref, ...), custom_call_target="tpu_custom_call" | custom-call | flops 2684354560 | bytes 17825792 | tf_op jit(solution)/shard_map/attn_bwd/pallas_call | solution.py:324
  99.3 4.0 %all-to-all-done.2 = bf16[32,64,256]{2,1,0:T(8,128)(2,1)S(1)} async-done(((bf16[32,64,256]{2,1,0:T(8,128)(2,1)}), bf16[32,64,256]{2,1,0:T(8,128)(2,1)S(1)}, u32[]{:S(2)}, u32[]{:S(2)}) %all-to-all-start.2) | async-done | bytes 1048608 | tf_op jit(solution)/shard_map/all_to_all | solution.py:457
  103.4 0.4 collective-permute-start.2
  103.7 0.6 copy-done.4
  104.3 3.7 %all-to-all-start.3 = ((bf16[16,256,128]{2,1,0:T(8,128)(2,1)}), bf16[16,256,128]{2,1,0:T(8,128)(2,1)S(1)}, u32[]{:S(2)}, u32[]{:S(2)}) async-start(bf16[16,256,128]{2,1,0:T(8,128)(2,1)} %get-tuple-element.65), calls=%async_computation.3 | async-start | bytes 2097152 | tf_op jit(solution)/shard_map/all_to_all | solution.py:54
  108.1 5.9 %weight_partial.1 = (bf16[128,2048]{1,0:T(8,128)(2,1)}, bf16[128,2048]{1,0:T(8,128)(2,1)}, bf16[128,2048]{1,0:T(8,128)(2,1)}, bf16[128,2048]{1,0:T(8,128)(2,1)},...) custom-call(s32[2]{0:T(128)} %pad_add_fusion.place, ...), custom_call_target="tpu_custom_call" | custom-call | flops 2147483648 | bytes 8388608 | tf_op jit(solution)/shard_map/weight_partial/pallas_call | solution.py:395
  114.1 1.6 collective-permute-start.3
  115.6 1.7 collective-permute-start.4
  117.4 4.3 %combine.1 = bf16[16,512,128]{2,1,0:T(8,128)(2,1)} custom-call(bf16[16,512,128]{2,1,0:T(8,128)(2,1)} %get-tuple-element.66.own_ref, bf16[16,512,128]{2,1,0:T(8,128)(2,1)} %copy-done.3), custom_call_target="tpu_custom_call" | custom-call | flops 1048576 | bytes 6291456 | tf_op jit(solution)/shard_map/combine/pallas_call | solution.py:359
  121.7 4.8 %all-to-all-done.3.r_ref = bf16[16,256,128]{2,1,0:T(8,128)(2,1)S(1)} async-done(((bf16[16,256,128]{2,1,0:T(8,128)(2,1)}), bf16[16,256,128]{2,1,0:T(8,128)(2,1)S(1)}, u32[]{:S(2)}, u32[]{:S(2)}) %all-to-all-start.3) | async-done | bytes 1048608 | tf_op jit(solution)/shard_map/all_to_all | solution.py:54
  126.5 3.1 %collective-permute-done.3 = bf16[128,2048]{1,0:T(8,128)(2,1)S(1)} collective-permute-done((bf16[128,2048]{1,0:T(8,128)(2,1)}, bf16[128,2048]{1,0:T(8,128)(2,1)S(1)}, u32[]{:S(2)}, u32[]{:S(2)}) %collective-permute-start.3) | collective-permute-done | bytes 524320 | tf_op jit(solution)/shard_map/ppermute | solution.py:424
  129.7 0.9 add_convert_fusion.5
  130.6 1.5 collective-permute-start.5
  132.1 0.9 add_convert_fusion.2
  133.0 1.7 collective-permute-start.7
  134.8 6.9 %all-to-all-start.4 = ((bf16[16,512,128]{2,1,0:T(8,128)(2,1)}), bf16[16,512,128]{2,1,0:T(8,128)(2,1)S(1)}, u32[]{:S(2)}, u32[]{:S(2)}) async-start(bf16[16,512,128]{2,1,0:T(8,128)(2,1)} %combine.1), calls=%async_computation.4 | async-start | bytes 4194304 | tf_op jit(solution)/shard_map/all_to_all | solution.py:54
  141.7 0.0 copy-start.6
  141.7 3.8 %collective-permute-done.5 = bf16[128,2048]{1,0:T(8,128)(2,1)} collective-permute-done((bf16[128,2048]{1,0:T(8,128)(2,1)}, bf16[128,2048]{1,0:T(8,128)(2,1)}, u32[]{:S(2)}, u32[]{:S(2)}) %collective-permute-start.5) | collective-permute-done | bytes 524320 | tf_op jit(solution)/shard_map/ppermute | solution.py:424
  145.4 1.3 add_convert_fusion.4
  146.8 0.1 collective-permute-start.6
  146.9 1.3 add_convert_fusion.1
  148.2 3.3 %collective-permute-start.8 = (bf16[128,2048]{1,0:T(8,128)(2,1)S(1)}, bf16[128,2048]{1,0:T(8,128)(2,1)S(1)}, u32[]{:S(2)}, u32[]{:S(2)}) collective-permute-start(bf16[128,2048]{1,0:T(8,128)(2,1)S(1)} %add_convert_fusion.1), channel_id=1, source_target_pairs={{0,96},{32,0},{64,32},{96,64},{1,97},{33,1},{65,33},{97,65},{2,98}... | collective-permute-start | bytes 1572872 | tf_op jit(solution)/shard_map/ppermute | solution.py:425
  151.5 8.9 %collective-permute-done.6 = bf16[128,2048]{1,0:T(8,128)(2,1)S(1)} collective-permute-done((bf16[128,2048]{1,0:T(8,128)(2,1)S(1)}, bf16[128,2048]{1,0:T(8,128)(2,1)S(1)}, u32[]{:S(2)}, u32[]{:S(2)}) %collective-permute-start.6) | collective-permute-done | bytes 524320 | tf_op jit(solution)/shard_map/ppermute | solution.py:424
  160.4 0.1 add_convert_fusion.3
  160.6 0.5 collective-permute-done.8
  161.1 0.1 add_convert_fusion
  161.2 1.1 pad_maximum_fusion
  162.3 7.8 %all-to-all-done.4.r_ref = bf16[16,512,128]{2,1,0:T(8,128)(2,1)S(1)} async-done(((bf16[16,512,128]{2,1,0:T(8,128)(2,1)}), bf16[16,512,128]{2,1,0:T(8,128)(2,1)S(1)}, u32[]{:S(2)}, u32[]{:S(2)}) %all-to-all-start.4) | async-done | bytes 2097184 | tf_op jit(solution)/shard_map/all_to_all | solution.py:54
  170.1 3.8 %all-to-all-start.5 = ((bf16[16,16,2048]{2,1,0:T(8,128)(2,1)}), bf16[16,16,2048]{2,1,0:T(8,128)(2,1)S(1)}, u32[]{:S(2)}, u32[]{:S(2)}) async-start(bf16[16,16,2048]{2,1,0:T(8,128)(2,1)} %pad_maximum_fusion), calls=%async_computation.5 | async-start | bytes 2097152 | tf_op jit(solution)/shard_map/all_to_all | solution.py:54
  173.9 3.4 %unpack.2 = bf16[256,2048]{1,0:T(8,128)(2,1)} custom-call(bf16[16,256,128]{2,1,0:T(8,128)(2,1)} %copy-done.2), custom_call_target="tpu_custom_call" | custom-call | bytes 2097152 | tf_op jit(solution)/shard_map/unpack/pallas_call | solution.py:95
  177.3 3.9 %unpack.3 = (bf16[256,2048]{1,0:T(8,128)(2,1)}, bf16[256,2048]{1,0:T(8,128)(2,1)}) custom-call(bf16[16,512,128]{2,1,0:T(8,128)(2,1)} %copy-done.1), custom_call_target="tpu_custom_call" | custom-call | bytes 4194304 | tf_op jit(solution)/shard_map/unpack/pallas_call | solution.py:95
  181.2 7.6 %all-to-all-done.5 = bf16[16,16,2048]{2,1,0:T(8,128)(2,1)S(1)} async-done(((bf16[16,16,2048]{2,1,0:T(8,128)(2,1)}), bf16[16,16,2048]{2,1,0:T(8,128)(2,1)S(1)}, u32[]{:S(2)}, u32[]{:S(2)}) %all-to-all-start.5) | async-done | bytes 1048608 | tf_op jit(solution)/shard_map/all_to_all | solution.py:54
  188.8 0.8 convert_reduce_fusion
  (23 shorter events, 0.1 us)
Async XLA Ops:
  5.0 51.0 %all-to-all-start = ((bf16[16,776,128]{2,1,0:T(8,128)(2,1)}), bf16[16,776,128]{2,1,0:T(8,128)(2,1)S(1)}, u32[]{:S(2)}, u32[]{:S(2)}) async-start(bf16[16,776,128]{2,1,0:T(8,128)(2,1)} %pack.1), calls=%async_computation | async-start | bytes 6356992 | tf_op jit(solution)/shard_map/all_to_all | solution.py:54
  13.1 8.9 %collective-permute-start = (bf16[256,2048]{1,0:T(8,128)(2,1)}, bf16[256,2048]{1,0:T(8,128)(2,1)}, u32[]{:S(2)}, u32[]{:S(2)}) collective-permute-start(bf16[256,2048]{1,0:T(8,128)(2,1)} %bitcast.15), channel_id=1, source_target_pairs={{0,1},{1,0},{2,3},{3,2},{4,5},{5,4},{6,7},{7,6},{8,9},{9,8},{10,11... | collective-permute-start | bytes 3145736 | tf_op jit(solution)/shard_map/ppermute | solution.py:448
  56.0 9.7 %copy-start = (bf16[16,776,128]{2,1,0:T(8,128)(2,1)}, bf16[16,776,128]{2,1,0:T(8,128)(2,1)S(1)}, u32[]{:S(2)}) copy-start(bf16[16,776,128]{2,1,0:T(8,128)(2,1)S(1)} %all-to-all-done.x_ref) | copy-start | bytes 9535492
  56.0 9.7 %collective-permute-start.1 = (bf16[16,776,128]{2,1,0:T(8,128)(2,1)S(1)}, bf16[16,776,128]{2,1,0:T(8,128)(2,1)}, u32[]{:S(2)}, u32[]{:S(2)}) collective-permute-start(bf16[16,776,128]{2,1,0:T(8,128)(2,1)S(1)} %all-to-all-done.x_ref), channel_id=1, source_target_pairs={{0,1},{1,0},{2,3},{3,2},{4,5},{5,4},{6,7},{7,6},{8,9},{9,8},{10,11... | collective-permute-start | bytes 9535496 | tf_op jit(solution)/shard_map/ppermute | solution.py:451
  56.0 26.7 %all-to-all-start.1 = ((bf16[16,256,128]{2,1,0:T(8,128)(2,1)}), bf16[16,256,128]{2,1,0:T(8,128)(2,1)}, u32[]{:S(2)}, u32[]{:S(2)}) async-start(bf16[16,256,128]{2,1,0:T(8,128)(2,1)} %grad_attn.1), calls=%async_computation.1 | async-start | bytes 2097152 | tf_op jit(solution)/shard_map/all_to_all | solution.py:54
  82.6 20.7 %all-to-all-start.2 = ((bf16[32,64,256]{2,1,0:T(8,128)(2,1)}), bf16[32,64,256]{2,1,0:T(8,128)(2,1)S(1)}, u32[]{:S(2)}, u32[]{:S(2)}) async-start(bf16[32,64,256]{2,1,0:T(8,128)(2,1)} %get-tuple-element.48), calls=%async_computation.2 | async-start | bytes 2097152 | tf_op jit(solution)/shard_map/all_to_all | solution.py:457
  103.4 1.0 copy-start.4
  103.4 4.7 %collective-permute-start.2 = (bf16[16,512,128]{2,1,0:T(8,128)(2,1)}, bf16[16,512,128]{2,1,0:T(8,128)(2,1)S(1)}, u32[]{:S(2)}, u32[]{:S(2)}) collective-permute-start(bf16[16,512,128]{2,1,0:T(8,128)(2,1)} %get-tuple-element.54), channel_id=1, source_target_pairs={{0,1},{1,0},{2,3},{3,2},{4,5},{5,4},{6,7},{7,6},{8,9},{9,8},{10,11... | collective-permute-start | bytes 6291464 | tf_op jit(solution)/shard_map/ppermute | solution.py:461
  104.3 22.2 %all-to-all-start.3 = ((bf16[16,256,128]{2,1,0:T(8,128)(2,1)}), bf16[16,256,128]{2,1,0:T(8,128)(2,1)S(1)}, u32[]{:S(2)}, u32[]{:S(2)}) async-start(bf16[16,256,128]{2,1,0:T(8,128)(2,1)} %get-tuple-element.65), calls=%async_computation.3 | async-start | bytes 2097152 | tf_op jit(solution)/shard_map/all_to_all | solution.py:54
  108.1 6.0 %copy-start.3 = (bf16[16,512,128]{2,1,0:T(8,128)(2,1)}, bf16[16,512,128]{2,1,0:T(8,128)(2,1)S(1)}, u32[]{:S(2)}) copy-start(bf16[16,512,128]{2,1,0:T(8,128)(2,1)S(1)} %collective-permute-done.2.got_ref) | copy-start | bytes 6291460
  114.1 15.6 %copy-start.8 = (bf16[128,2048]{1,0:T(8,128)(2,1)S(1)}, bf16[128,2048]{1,0:T(8,128)(2,1)}, u32[]{:S(2)}) copy-start(bf16[128,2048]{1,0:T(8,128)(2,1)} %get-tuple-element.71) | copy-start | bytes 1572868
  114.1 15.6 %collective-permute-start.3 = (bf16[128,2048]{1,0:T(8,128)(2,1)}, bf16[128,2048]{1,0:T(8,128)(2,1)S(1)}, u32[]{:S(2)}, u32[]{:S(2)}) collective-permute-start(bf16[128,2048]{1,0:T(8,128)(2,1)} %get-tuple-element.63), channel_id=1, source_target_pairs={{0,32},{32,64},{64,96},{96,0},{1,33},{33,65},{65,97},{97,1},{2,34}... | collective-permute-start | bytes 1572872 | tf_op jit(solution)/shard_map/ppermute | solution.py:424
  115.6 16.5 %copy-start.7 = (bf16[128,2048]{1,0:T(8,128)(2,1)S(1)}, bf16[128,2048]{1,0:T(8,128)(2,1)}, u32[]{:S(2)}) copy-start(bf16[128,2048]{1,0:T(8,128)(2,1)} %get-tuple-element.75) | copy-start | bytes 1572868
  115.6 14.0 %collective-permute-start.4 = (bf16[128,2048]{1,0:T(8,128)(2,1)}, bf16[128,2048]{1,0:T(8,128)(2,1)S(1)}, u32[]{:S(2)}, u32[]{:S(2)}) collective-permute-start(bf16[128,2048]{1,0:T(8,128)(2,1)} %get-tuple-element.64), channel_id=1, source_target_pairs={{0,96},{32,0},{64,32},{96,64},{1,97},{33,1},{65,33},{97,65},{2,98}... | collective-permute-start | bytes 1572872 | tf_op jit(solution)/shard_map/ppermute | solution.py:425
  126.5 8.2 %copy-start.2 = (bf16[16,256,128]{2,1,0:T(8,128)(2,1)}, bf16[16,256,128]{2,1,0:T(8,128)(2,1)S(1)}, u32[]{:S(2)}) copy-start(bf16[16,256,128]{2,1,0:T(8,128)(2,1)S(1)} %all-to-all-done.3.r_ref) | copy-start | bytes 3145732
  130.6 14.8 %collective-permute-start.5 = (bf16[128,2048]{1,0:T(8,128)(2,1)}, bf16[128,2048]{1,0:T(8,128)(2,1)}, u32[]{:S(2)}, u32[]{:S(2)}) collective-permute-start(bf16[128,2048]{1,0:T(8,128)(2,1)} %add_convert_fusion.5), channel_id=1, source_target_pairs={{0,32},{32,64},{64,96},{96,0},{1,33},{33,65},{65,97},{97,1},{2,34}... | collective-permute-start | bytes 1572872 | tf_op jit(solution)/shard_map/ppermute | solution.py:424
  133.0 13.8 %collective-permute-start.7 = (bf16[128,2048]{1,0:T(8,128)(2,1)}, bf16[128,2048]{1,0:T(8,128)(2,1)}, u32[]{:S(2)}, u32[]{:S(2)}) collective-permute-start(bf16[128,2048]{1,0:T(8,128)(2,1)} %add_convert_fusion.2), channel_id=1, source_target_pairs={{0,96},{32,0},{64,32},{96,64},{1,97},{33,1},{65,33},{97,65},{2,98}... | collective-permute-start | bytes 1572872 | tf_op jit(solution)/shard_map/ppermute | solution.py:425
  134.8 35.3 %all-to-all-start.4 = ((bf16[16,512,128]{2,1,0:T(8,128)(2,1)}), bf16[16,512,128]{2,1,0:T(8,128)(2,1)S(1)}, u32[]{:S(2)}, u32[]{:S(2)}) async-start(bf16[16,512,128]{2,1,0:T(8,128)(2,1)} %combine.1), calls=%async_computation.4 | async-start | bytes 4194304 | tf_op jit(solution)/shard_map/all_to_all | solution.py:54
  141.7 18.8 %copy-start.6 = (bf16[128,2048]{1,0:T(8,128)(2,1)S(1)}, bf16[128,2048]{1,0:T(8,128)(2,1)}, u32[]{:S(2)}) copy-start(bf16[128,2048]{1,0:T(8,128)(2,1)} %get-tuple-element.73) | copy-start | bytes 1572868
  141.7 19.4 %copy-start.5 = (bf16[128,2048]{1,0:T(8,128)(2,1)S(1)}, bf16[128,2048]{1,0:T(8,128)(2,1)}, u32[]{:S(2)}) copy-start(bf16[128,2048]{1,0:T(8,128)(2,1)} %get-tuple-element.77) | copy-start | bytes 1572868
  146.8 13.7 %collective-permute-start.6 = (bf16[128,2048]{1,0:T(8,128)(2,1)S(1)}, bf16[128,2048]{1,0:T(8,128)(2,1)S(1)}, u32[]{:S(2)}, u32[]{:S(2)}) collective-permute-start(bf16[128,2048]{1,0:T(8,128)(2,1)S(1)} %add_convert_fusion.4), channel_id=1, source_target_pairs={{0,32},{32,64},{64,96},{96,0},{1,33},{33,65},{65,97},{97,1},{2,34}... | collective-permute-start | bytes 1572872 | tf_op jit(solution)/shard_map/ppermute | solution.py:424
  148.2 12.9 %collective-permute-start.8 = (bf16[128,2048]{1,0:T(8,128)(2,1)S(1)}, bf16[128,2048]{1,0:T(8,128)(2,1)S(1)}, u32[]{:S(2)}, u32[]{:S(2)}) collective-permute-start(bf16[128,2048]{1,0:T(8,128)(2,1)S(1)} %add_convert_fusion.1), channel_id=1, source_target_pairs={{0,96},{32,0},{64,32},{96,64},{1,97},{33,1},{65,33},{97,65},{2,98}... | collective-permute-start | bytes 1572872 | tf_op jit(solution)/shard_map/ppermute | solution.py:425
  170.1 7.3 %copy-start.1 = (bf16[16,512,128]{2,1,0:T(8,128)(2,1)}, bf16[16,512,128]{2,1,0:T(8,128)(2,1)S(1)}, u32[]{:S(2)}) copy-start(bf16[16,512,128]{2,1,0:T(8,128)(2,1)S(1)} %all-to-all-done.4.r_ref) | copy-start | bytes 6291460
  170.1 18.7 %all-to-all-start.5 = ((bf16[16,16,2048]{2,1,0:T(8,128)(2,1)}), bf16[16,16,2048]{2,1,0:T(8,128)(2,1)S(1)}, u32[]{:S(2)}, u32[]{:S(2)}) async-start(bf16[16,16,2048]{2,1,0:T(8,128)(2,1)} %pad_maximum_fusion), calls=%async_computation.5 | async-start | bytes 2097152 | tf_op jit(solution)/shard_map/all_to_all | solution.py:54

commit v8 on v7

--- a/solution.py
+++ b/solution.py
@@ -31,7 +31,7 @@
 
 UNROLL = 4
 GROUP = 4
-PACK = 4
+PACK = 8
 VMEM_LIMIT = 56 * 1024 * 1024
 
 
@@ -354,7 +354,7 @@
 
 
 def combine(own, got):
-    n = 4
+    n = 8
     rows = pl.BlockSpec((n, 2 * TOK, HEAD), lambda i: (i, 0, 0))
     return pl.pallas_call(
         combine_body,
@@ -416,7 +416,7 @@
     return (a.astype(f32) + b.astype(f32)).astype(bf16)
 
 
-def sum_over_docs(up, down, room, first):
+def sum_over_docs(up, down, first):
     route_up = [(i, (i + 1) % DOCS) for i in range(DOCS)]
     route_down = [(i, (i - 1) % DOCS) for i in range(DOCS)]
     a, b = up[3], down[1]
@@ -425,11 +425,16 @@
         b = lax.ppermute(b, "dp", route_down)
         if step == 1:
             a, b, first = after(a, b, first)
-        a = plus(a, up[3 - step])
-        b = plus(b, down[(1 + step) % DOCS])
+        if step < DOCS - 1:
+            a = plus(a, up[3 - step])
+            b = plus(b, down[1 + step])
+    return (a, up[0], b, down[0]), first
+
+
+def join(a, own_a, b, own_b):
     n = CHIPS // 2
-    joined = lax.dynamic_update_slice(room, a.reshape(n, 16, D), (0, 0, 0))
-    return lax.dynamic_update_slice(joined, b.reshape(n, 16, D), (n, 0, 0)), first
+    parts = (plus(a, own_a), plus(b, own_b))
+    return jnp.concatenate([part.reshape(n, 16, D) for part in parts], axis=0)
 
 
 def block_table(rider, core):
@@ -463,11 +468,11 @@
     by_core = out_home.reshape(HEADS, 2, HEAD // 2, TOK)
     up, down = weight_partial(place, by_core, cot, cot_other)
     *up, got = after(*up, got)
-    room = jnp.zeros((CHIPS, 16, D), bf16)
-    by_doc, (gq_home, gathered) = sum_over_docs(up, down, room, (gq_home, combine(own, got)))
+    gq_home, gathered = after(gq_home, combine(own, got))
+    sums, gq_home = sum_over_docs(up, down, gq_home)
     kv_home = exchange(gathered)
-    kv_home, by_doc = after(kv_home, by_doc)
-    weight_grad = jnp.sum(exchange(by_doc).astype(f32), axis=0)
+    kv_home, *sums = after(kv_home, *sums)
+    weight_grad = jnp.sum(exchange(join(*sums)).astype(f32), axis=0)
     (gq,) = unpack(gq_home, 1)
     gk, gv = unpack(kv_home, 2)
     return gq[None], gk[None], gv[None], weight_grad

time: 191 us -> 185 us (0.969)
  Pallas kernels: 52.9 us -> 48.6 us
  waiting for transfers between devices: 81.8 us -> 79.8 us
    all_to_all x5, waiting for transfers between devices: 61.5 us -> 55.5 us  [exchange(): lax.all_to_all(x, 'seq', 0, 0, axis_index_groups=SAME_CORE, tiled=True)]
    ppermute x3, waiting for transfers between devices: 15.8 us -> 19 us  [sum_over_docs(): a = lax.ppermute(a, 'dp', route_up)]
    pallas_call x2, Pallas kernels: 7.3 us -> 5 us  [unpack(): pl.pallas_call(unpack_body, out_shape=(out,) * n, grid=(HEADS // PACK,),...]
    all_to_all x5, starting transfers between devices: 30.7 us -> 28.6 us  [exchange(): lax.all_to_all(x, 'seq', 0, 0, axis_index_groups=SAME_CORE, tiled=True)]
    convert_element_type x6 -> x5, other arithmetic: 4.76 us -> 5.32 us  [plus(): return (a.astype(f32) + b.astype(f32)).astype(bf16)]
  transfers between devices with their start and end apart: 15 -> 15, of which waited for: 10 -> 9; matrix products, arithmetic and copies ran while one was open for 3% -> 2% of each run, Pallas kernels for 26% -> 25%
where the time goes in v8:
time: 185 us; the launch traced here: 183 us
  waiting for transfers between devices  79.8 us (43%)
  Pallas kernels  48.6 us (26%)
  starting transfers between devices  43.5 us (24%)
  other arithmetic  8.6 us (5%)
  local copies, waits for them, and re-layouts  1.95 us (1%)
    all_to_all x5, waiting for transfers between devices, exchange(): lax.all_to_all(x, 'seq', 0, 0, axis_index_groups=SAME_CORE, tiled=True)  55.5 us
    all_to_all x5, starting transfers between devices, exchange(): lax.all_to_all(x, 'seq', 0, 0, axis_index_groups=SAME_CORE, tiled=True)  28.6 us
    ppermute x3, waiting for transfers between devices, sum_over_docs(): a = lax.ppermute(a, 'dp', route_up)  19 us
    pallas_call x1, Pallas kernels, attention_backward(): pl.pallas_call(backward_body, out_shape=(jax.ShapeDtypeStruct((CHIPS, 2 *...  12.6 us
    pallas_call x1, Pallas kernels, attention_forward(): pl.pallas_call(forward_body, out_shape=(jax.ShapeDtypeStruct((2 * CHIPS,...  9.59 us
    pallas_call x1, Pallas kernels, grad_attn_by_head(): pl.pallas_call(grad_attn_body, out_shape=jax.ShapeDtypeStruct((HEADS, TOK...  8.78 us
    ppermute x3, starting transfers between devices, sum_over_docs(): b = lax.ppermute(b, 'dp', route_down)  6.9 us
    pallas_call x1, Pallas kernels, weight_partial(): pl.pallas_call(weight_body, out_shape=(jax.ShapeDtypeStruct((CHUNK, D), b...  5.93 us
  transfers between devices with their start and end apart: 15, of which 9 were waited for; matrix products, arithmetic and copies ran while one was open for 2% of the time, Pallas kernels for 25%

profile of v8, /device:TPU:0, one launch (start us, length us, event | category | flops | bytes accessed | tf_op | source)
XLA Modules:
  0.0 183.3 jit_solution(12423474608080161423)
XLA Ops:
  0.6 3.3 %pack.1 = bf16[16,776,128]{2,1,0:T(8,128)(2,1)} custom-call(s32[2,4]{1,0:T(2,128)} %bitcast.24, bf16[256,2048]{1,0:T(8,128)(2,1)} %bitcast.21, bf16[256,2048]{1,0:T(8,128)(2,1)} %bitcast.22, bf16[256,2048]{1,0:T(8,128)(2,1)} %bitcast.23), custom_call_target="tpu_custom_call" | custom-call | tf_op jit(solution)/shard_map/pack/pallas_call | solution.py:75
  3.9 8.1 %all-to-all-start = ((bf16[16,776,128]{2,1,0:T(8,128)(2,1)}), bf16[16,776,128]{2,1,0:T(8,128)(2,1)S(1)}, u32[]{:S(2)}, u32[]{:S(2)}) async-start(bf16[16,776,128]{2,1,0:T(8,128)(2,1)} %pack.1), calls=%async_computation | async-start | bytes 6356992 | tf_op jit(solution)/shard_map/all_to_all | solution.py:54
  12.1 0.1 collective-permute-start
  12.2 8.8 %grad_attn.1 = bf16[16,256,128]{2,1,0:T(8,128)(2,1)} custom-call(bf16[256,2048]{1,0:T(8,128)(2,1)} %bitcast.16, bf16[2048,2048]{1,0:T(8,128)(2,1)} %w_ref.1), custom_call_target="tpu_custom_call" | custom-call | flops 2147483648 | bytes 10485760 | tf_op jit(solution)/shard_map/grad_attn/pallas_call | solution.py:114
  21.0 0.0 collective-permute-done.cb_ref
  21.0 33.9 %all-to-all-done.x_ref = bf16[16,776,128]{2,1,0:T(8,128)(2,1)S(1)} async-done(((bf16[16,776,128]{2,1,0:T(8,128)(2,1)}), bf16[16,776,128]{2,1,0:T(8,128)(2,1)S(1)}, u32[]{:S(2)}, u32[]{:S(2)}) %all-to-all-start) | async-done | bytes 3178528 | tf_op jit(solution)/shard_map/all_to_all | solution.py:54
  54.9 0.0 collective-permute-start.1
  54.9 8.1 %all-to-all-start.1 = ((bf16[16,256,128]{2,1,0:T(8,128)(2,1)}), bf16[16,256,128]{2,1,0:T(8,128)(2,1)}, u32[]{:S(2)}, u32[]{:S(2)}) async-start(bf16[16,256,128]{2,1,0:T(8,128)(2,1)} %grad_attn.1), calls=%async_computation.1 | async-start | bytes 2097152 | tf_op jit(solution)/shard_map/all_to_all | solution.py:54
  63.1 0.1 iota_add_fusion
  63.1 0.1 add.68
  63.2 0.6 pad_add_fusion.place
  63.9 0.1 reshape.55
  63.9 0.7 add_select_fusion.table
  64.6 0.0 collective-permute-done.1.y_ref
  64.6 9.6 %attn_fwd.1 = (bf16[32,64,256]{2,1,0:T(8,128)(2,1)}, bf16[32,640,128]{2,1,0:T(8,128)(2,1)}) custom-call(s32[32,4]{1,0:T(8,128)} %add_select_fusion.table, bf16[16,776,128]{2,1,0:T(8,128)(2,1)} %copy-done, bf16[16,776,128]{2,1,0:T(8,128)(2,1)} %collective-permute-done.1.y_ref), custom_call_target="tpu_custom_call" | custom-call | flops 1342177280 | bytes 12582912 | tf_op jit(solution)/shard_map/attn_fwd/pallas_call | solution.py:220
  74.2 7.3 %all-to-all-done.1.g_ref = bf16[16,256,128]{2,1,0:T(8,128)(2,1)} async-done(((bf16[16,256,128]{2,1,0:T(8,128)(2,1)}), bf16[16,256,128]{2,1,0:T(8,128)(2,1)}, u32[]{:S(2)}, u32[]{:S(2)}) %all-to-all-start.1) | async-done | bytes 1048608 | tf_op jit(solution)/shard_map/all_to_all | solution.py:54
  81.6 4.1 %all-to-all-start.2 = ((bf16[32,64,256]{2,1,0:T(8,128)(2,1)}), bf16[32,64,256]{2,1,0:T(8,128)(2,1)S(1)}, u32[]{:S(2)}, u32[]{:S(2)}) async-start(bf16[32,64,256]{2,1,0:T(8,128)(2,1)} %get-tuple-element.52), calls=%async_computation.2 | async-start | bytes 2097152 | tf_op jit(solution)/shard_map/all_to_all | solution.py:462
  85.7 12.6 %attn_bwd.1 = (bf16[16,512,128]{2,1,0:T(8,128)(2,1)}, bf16[16,512,128]{2,1,0:T(8,128)(2,1)}, bf16[16,256,128]{2,1,0:T(8,128)(2,1)}) custom-call(s32[32,4]{1,0:T(8,128)} %add_select_fusion.table, bf16[16,776,128]{2,1,0:T(8,128)(2,1)} %copy-done, bf16[16,776,128]{2,1,0:T(8,128)(2,1)} %collective-permute-done.1.y_ref, ...), custom_call_target="tpu_custom_call" | custom-call | flops 2684354560 | bytes 17825792 | tf_op jit(solution)/shard_map/attn_bwd/pallas_call | solution.py:324
  98.3 4.0 %all-to-all-done.2 = bf16[32,64,256]{2,1,0:T(8,128)(2,1)S(1)} async-done(((bf16[32,64,256]{2,1,0:T(8,128)(2,1)}), bf16[32,64,256]{2,1,0:T(8,128)(2,1)S(1)}, u32[]{:S(2)}, u32[]{:S(2)}) %all-to-all-start.2) | async-done | bytes 1048608 | tf_op jit(solution)/shard_map/all_to_all | solution.py:462
  102.3 1.0 copy-done.4
  103.3 0.4 collective-permute-start.2
  103.6 3.7 %all-to-all-start.3 = ((bf16[16,256,128]{2,1,0:T(8,128)(2,1)}), bf16[16,256,128]{2,1,0:T(8,128)(2,1)S(1)}, u32[]{:S(2)}, u32[]{:S(2)}) async-start(bf16[16,256,128]{2,1,0:T(8,128)(2,1)} %get-tuple-element.69), calls=%async_computation.3 | async-start | bytes 2097152 | tf_op jit(solution)/shard_map/all_to_all | solution.py:54
  107.3 0.3 collective-permute-done.2.got_ref
  107.6 5.9 %weight_partial.1 = (bf16[128,2048]{1,0:T(8,128)(2,1)}, bf16[128,2048]{1,0:T(8,128)(2,1)}, bf16[128,2048]{1,0:T(8,128)(2,1)}, bf16[128,2048]{1,0:T(8,128)(2,1)},...) custom-call(s32[2]{0:T(128)} %pad_add_fusion.place, ...), custom_call_target="tpu_custom_call" | custom-call | flops 2147483648 | bytes 8388608 | tf_op jit(solution)/shard_map/weight_partial/pallas_call | solution.py:395
  113.6 1.6 collective-permute-start.3
  115.2 1.7 collective-permute-start.4
  116.9 3.4 %combine.1 = bf16[16,512,128]{2,1,0:T(8,128)(2,1)} custom-call(bf16[16,512,128]{2,1,0:T(8,128)(2,1)} %get-tuple-element.70.own_ref, bf16[16,512,128]{2,1,0:T(8,128)(2,1)} %copy-done.3), custom_call_target="tpu_custom_call" | custom-call | flops 1048576 | bytes 6291456 | tf_op jit(solution)/shard_map/combine/pallas_call | solution.py:359
  120.3 5.3 %all-to-all-done.3.r_ref = bf16[16,256,128]{2,1,0:T(8,128)(2,1)S(1)} async-done(((bf16[16,256,128]{2,1,0:T(8,128)(2,1)}), bf16[16,256,128]{2,1,0:T(8,128)(2,1)S(1)}, u32[]{:S(2)}, u32[]{:S(2)}) %all-to-all-start.3) | async-done | bytes 1048608 | tf_op jit(solution)/shard_map/all_to_all | solution.py:54
  125.7 3.7 %all-to-all-start.4 = ((bf16[16,512,128]{2,1,0:T(8,128)(2,1)}), bf16[16,512,128]{2,1,0:T(8,128)(2,1)S(1)}, u32[]{:S(2)}, u32[]{:S(2)}) async-start(bf16[16,512,128]{2,1,0:T(8,128)(2,1)} %combine.1), calls=%async_computation.4 | async-start | bytes 4194304 | tf_op jit(solution)/shard_map/all_to_all | solution.py:54
  129.4 1.4 add_convert_fusion.5
  130.8 1.8 collective-permute-start.5
  132.6 1.3 add_convert_fusion.3
  134.0 1.8 collective-permute-start.7
  135.8 9.8 %collective-permute-done.5 = bf16[128,2048]{1,0:T(8,128)(2,1)S(1)} collective-permute-done((bf16[128,2048]{1,0:T(8,128)(2,1)S(1)}, bf16[128,2048]{1,0:T(8,128)(2,1)S(1)}, u32[]{:S(2)}, u32[]{:S(2)}) %collective-permute-start.5) | collective-permute-done | bytes 524320 | tf_op jit(solution)/shard_map/ppermute | solution.py:424
  145.6 0.1 add_convert_fusion.4
  145.7 0.1 collective-permute-start.6
  145.8 0.9 collective-permute-done.7
  146.7 0.1 add_convert_fusion.2
  146.8 3.3 %collective-permute-start.8 = (bf16[128,2048]{1,0:T(8,128)(2,1)S(1)}, bf16[128,2048]{1,0:T(8,128)(2,1)}, u32[]{:S(2)}, u32[]{:S(2)}) collective-permute-start(bf16[128,2048]{1,0:T(8,128)(2,1)S(1)} %add_convert_fusion.2), channel_id=1, source_target_pairs={{0,96},{32,0},{64,32},{96,64},{1,97},{33,1},{65,33},{97,65},{2,98}... | collective-permute-start | bytes 1572872 | tf_op jit(solution)/shard_map/ppermute | solution.py:425
  150.2 9.2 %collective-permute-done.6 = bf16[128,2048]{1,0:T(8,128)(2,1)S(1)} collective-permute-done((bf16[128,2048]{1,0:T(8,128)(2,1)S(1)}, bf16[128,2048]{1,0:T(8,128)(2,1)S(1)}, u32[]{:S(2)}, u32[]{:S(2)}) %collective-permute-start.6) | collective-permute-done | bytes 524320 | tf_op jit(solution)/shard_map/ppermute | solution.py:424
  159.4 0.8 copy-done.9
  160.2 2.3 %add_convert_fusion = (bf16[128,2048]{1,0:T(8,128)(2,1)S(1)}, bf16[128,2048]{1,0:T(8,128)(2,1)S(1)}) fusion(bf16[128,2048]{1,0:T(8,128)(2,1)S(1)} %copy-done.8, bf16[128,2048]{1,0:T(8,128)(2,1)} %collective-permute-done.8, bf16[128,2048]{1,0:T(8,128)(2,1)S(1)} %copy-done.7, bf16[128,2048]{1,0:T(8,128)(2,1)} %copy-done.9), kind=kLoop, calls=%fused_computation.2 | loop fusion | flops 2097152 | bytes 3145728 | tf_op jit(solution)/shard_map/convert_element_type | solution.py:416
  162.5 1.1 pad_maximum_fusion
  163.6 5.0 %all-to-all-start.5 = ((bf16[16,16,2048]{2,1,0:T(8,128)(2,1)}), bf16[16,16,2048]{2,1,0:T(8,128)(2,1)S(1)}, u32[]{:S(2)}, u32[]{:S(2)}) async-start(bf16[16,16,2048]{2,1,0:T(8,128)(2,1)} %pad_maximum_fusion), calls=%async_computation.5 | async-start | bytes 2097152 | tf_op jit(solution)/shard_map/all_to_all | solution.py:54
  168.6 2.2 %unpack.2 = bf16[256,2048]{1,0:T(8,128)(2,1)} custom-call(bf16[16,256,128]{2,1,0:T(8,128)(2,1)} %copy-done.2), custom_call_target="tpu_custom_call" | custom-call | bytes 2097152 | tf_op jit(solution)/shard_map/unpack/pallas_call | solution.py:95
  170.8 2.8 %unpack.3 = (bf16[256,2048]{1,0:T(8,128)(2,1)}, bf16[256,2048]{1,0:T(8,128)(2,1)}) custom-call(bf16[16,512,128]{2,1,0:T(8,128)(2,1)} %copy-done.1), custom_call_target="tpu_custom_call" | custom-call | bytes 4194304 | tf_op jit(solution)/shard_map/unpack/pallas_call | solution.py:95
  173.6 8.9 %all-to-all-done.5 = bf16[16,16,2048]{2,1,0:T(8,128)(2,1)S(1)} async-done(((bf16[16,16,2048]{2,1,0:T(8,128)(2,1)}), bf16[16,16,2048]{2,1,0:T(8,128)(2,1)S(1)}, u32[]{:S(2)}, u32[]{:S(2)}) %all-to-all-start.5) | async-done | bytes 1048608 | tf_op jit(solution)/shard_map/all_to_all | solution.py:54
  182.5 0.8 convert_reduce_fusion
  (24 shorter events, 0.1 us)
Async XLA Ops:
  3.9 51.0 %all-to-all-start = ((bf16[16,776,128]{2,1,0:T(8,128)(2,1)}), bf16[16,776,128]{2,1,0:T(8,128)(2,1)S(1)}, u32[]{:S(2)}, u32[]{:S(2)}) async-start(bf16[16,776,128]{2,1,0:T(8,128)(2,1)} %pack.1), calls=%async_computation | async-start | bytes 6356992 | tf_op jit(solution)/shard_map/all_to_all | solution.py:54
  12.1 8.9 %collective-permute-start = (bf16[256,2048]{1,0:T(8,128)(2,1)}, bf16[256,2048]{1,0:T(8,128)(2,1)}, u32[]{:S(2)}, u32[]{:S(2)}) collective-permute-start(bf16[256,2048]{1,0:T(8,128)(2,1)} %bitcast.15), channel_id=1, source_target_pairs={{0,1},{1,0},{2,3},{3,2},{4,5},{5,4},{6,7},{7,6},{8,9},{9,8},{10,11... | collective-permute-start | bytes 3145736 | tf_op jit(solution)/shard_map/ppermute | solution.py:453
  54.9 9.7 %copy-start = (bf16[16,776,128]{2,1,0:T(8,128)(2,1)}, bf16[16,776,128]{2,1,0:T(8,128)(2,1)S(1)}, u32[]{:S(2)}) copy-start(bf16[16,776,128]{2,1,0:T(8,128)(2,1)S(1)} %all-to-all-done.x_ref) | copy-start | bytes 9535492
  54.9 9.7 %collective-permute-start.1 = (bf16[16,776,128]{2,1,0:T(8,128)(2,1)S(1)}, bf16[16,776,128]{2,1,0:T(8,128)(2,1)}, u32[]{:S(2)}, u32[]{:S(2)}) collective-permute-start(bf16[16,776,128]{2,1,0:T(8,128)(2,1)S(1)} %all-to-all-done.x_ref), channel_id=1, source_target_pairs={{0,1},{1,0},{2,3},{3,2},{4,5},{5,4},{6,7},{7,6},{8,9},{9,8},{10,11... | collective-permute-start | bytes 9535496 | tf_op jit(solution)/shard_map/ppermute | solution.py:456
  54.9 26.7 %all-to-all-start.1 = ((bf16[16,256,128]{2,1,0:T(8,128)(2,1)}), bf16[16,256,128]{2,1,0:T(8,128)(2,1)}, u32[]{:S(2)}, u32[]{:S(2)}) async-start(bf16[16,256,128]{2,1,0:T(8,128)(2,1)} %grad_attn.1), calls=%async_computation.1 | async-start | bytes 2097152 | tf_op jit(solution)/shard_map/all_to_all | solution.py:54
  81.6 20.7 %all-to-all-start.2 = ((bf16[32,64,256]{2,1,0:T(8,128)(2,1)}), bf16[32,64,256]{2,1,0:T(8,128)(2,1)S(1)}, u32[]{:S(2)}, u32[]{:S(2)}) async-start(bf16[32,64,256]{2,1,0:T(8,128)(2,1)} %get-tuple-element.52), calls=%async_computation.2 | async-start | bytes 2097152 | tf_op jit(solution)/shard_map/all_to_all | solution.py:462
  102.3 1.0 copy-start.4
  103.3 4.4 %collective-permute-start.2 = (bf16[16,512,128]{2,1,0:T(8,128)(2,1)}, bf16[16,512,128]{2,1,0:T(8,128)(2,1)S(1)}, u32[]{:S(2)}, u32[]{:S(2)}) collective-permute-start(bf16[16,512,128]{2,1,0:T(8,128)(2,1)} %get-tuple-element.58), channel_id=1, source_target_pairs={{0,1},{1,0},{2,3},{3,2},{4,5},{5,4},{6,7},{7,6},{8,9},{9,8},{10,11... | collective-permute-start | bytes 6291464 | tf_op jit(solution)/shard_map/ppermute | solution.py:466
  103.6 22.0 %all-to-all-start.3 = ((bf16[16,256,128]{2,1,0:T(8,128)(2,1)}), bf16[16,256,128]{2,1,0:T(8,128)(2,1)S(1)}, u32[]{:S(2)}, u32[]{:S(2)}) async-start(bf16[16,256,128]{2,1,0:T(8,128)(2,1)} %get-tuple-element.69), calls=%async_computation.3 | async-start | bytes 2097152 | tf_op jit(solution)/shard_map/all_to_all | solution.py:54
  107.6 5.9 %copy-start.3 = (bf16[16,512,128]{2,1,0:T(8,128)(2,1)}, bf16[16,512,128]{2,1,0:T(8,128)(2,1)S(1)}, u32[]{:S(2)}) copy-start(bf16[16,512,128]{2,1,0:T(8,128)(2,1)S(1)} %collective-permute-done.2.got_ref) | copy-start | bytes 6291460
  113.6 15.8 %collective-permute-start.3 = (bf16[128,2048]{1,0:T(8,128)(2,1)}, bf16[128,2048]{1,0:T(8,128)(2,1)}, u32[]{:S(2)}, u32[]{:S(2)}) collective-permute-start(bf16[128,2048]{1,0:T(8,128)(2,1)} %get-tuple-element.67), channel_id=1, source_target_pairs={{0,32},{32,64},{64,96},{96,0},{1,33},{33,65},{65,97},{97,1},{2,34}... | collective-permute-start | bytes 1572872 | tf_op jit(solution)/shard_map/ppermute | solution.py:424
  115.2 14.2 %collective-permute-start.4 = (bf16[128,2048]{1,0:T(8,128)(2,1)}, bf16[128,2048]{1,0:T(8,128)(2,1)}, u32[]{:S(2)}, u32[]{:S(2)}) collective-permute-start(bf16[128,2048]{1,0:T(8,128)(2,1)} %get-tuple-element.68), channel_id=1, source_target_pairs={{0,96},{32,0},{64,32},{96,64},{1,97},{33,1},{65,33},{97,65},{2,98}... | collective-permute-start | bytes 1572872 | tf_op jit(solution)/shard_map/ppermute | solution.py:425
  125.6 8.3 %copy-start.2 = (bf16[16,256,128]{2,1,0:T(8,128)(2,1)}, bf16[16,256,128]{2,1,0:T(8,128)(2,1)S(1)}, u32[]{:S(2)}) copy-start(bf16[16,256,128]{2,1,0:T(8,128)(2,1)S(1)} %all-to-all-done.3.r_ref) | copy-start | bytes 3145732
  125.7 34.5 %all-to-all-start.4 = ((bf16[16,512,128]{2,1,0:T(8,128)(2,1)}), bf16[16,512,128]{2,1,0:T(8,128)(2,1)S(1)}, u32[]{:S(2)}, u32[]{:S(2)}) async-start(bf16[16,512,128]{2,1,0:T(8,128)(2,1)} %combine.1), calls=%async_computation.4 | async-start | bytes 4194304 | tf_op jit(solution)/shard_map/all_to_all | solution.py:54
  129.4 16.2 %copy-start.6 = (bf16[128,2048]{1,0:T(8,128)(2,1)S(1)}, bf16[128,2048]{1,0:T(8,128)(2,1)}, u32[]{:S(2)}) copy-start(bf16[128,2048]{1,0:T(8,128)(2,1)} %get-tuple-element.77) | copy-start | bytes 1572868
  129.4 17.3 %copy-start.5 = (bf16[128,2048]{1,0:T(8,128)(2,1)S(1)}, bf16[128,2048]{1,0:T(8,128)(2,1)}, u32[]{:S(2)}) copy-start(bf16[128,2048]{1,0:T(8,128)(2,1)} %get-tuple-element.81) | copy-start | bytes 1572868
  130.8 14.8 %collective-permute-start.5 = (bf16[128,2048]{1,0:T(8,128)(2,1)S(1)}, bf16[128,2048]{1,0:T(8,128)(2,1)S(1)}, u32[]{:S(2)}, u32[]{:S(2)}) collective-permute-start(bf16[128,2048]{1,0:T(8,128)(2,1)S(1)} %add_convert_fusion.5), channel_id=1, source_target_pairs={{0,32},{32,64},{64,96},{96,0},{1,33},{33,65},{65,97},{97,1},{2,34}... | collective-permute-start | bytes 1572872 | tf_op jit(solution)/shard_map/ppermute | solution.py:424
  134.0 12.7 %collective-permute-start.7 = (bf16[128,2048]{1,0:T(8,128)(2,1)S(1)}, bf16[128,2048]{1,0:T(8,128)(2,1)S(1)}, u32[]{:S(2)}, u32[]{:S(2)}) collective-permute-start(bf16[128,2048]{1,0:T(8,128)(2,1)S(1)} %add_convert_fusion.3), channel_id=1, source_target_pairs={{0,96},{32,0},{64,32},{96,64},{1,97},{33,1},{65,33},{97,65},{2,98}... | collective-permute-start | bytes 1572872 | tf_op jit(solution)/shard_map/ppermute | solution.py:425
  135.8 24.4 %copy-start.7 = (bf16[128,2048]{1,0:T(8,128)(2,1)S(1)}, bf16[128,2048]{1,0:T(8,128)(2,1)}, u32[]{:S(2)}) copy-start(bf16[128,2048]{1,0:T(8,128)(2,1)} %get-tuple-element.87) | copy-start | bytes 1572868
  135.8 24.4 %copy-start.8 = (bf16[128,2048]{1,0:T(8,128)(2,1)S(1)}, bf16[128,2048]{1,0:T(8,128)(2,1)}, u32[]{:S(2)}) copy-start(bf16[128,2048]{1,0:T(8,128)(2,1)} %get-tuple-element.89) | copy-start | bytes 1572868
  145.7 13.6 %collective-permute-start.6 = (bf16[128,2048]{1,0:T(8,128)(2,1)S(1)}, bf16[128,2048]{1,0:T(8,128)(2,1)S(1)}, u32[]{:S(2)}, u32[]{:S(2)}) collective-permute-start(bf16[128,2048]{1,0:T(8,128)(2,1)S(1)} %add_convert_fusion.4), channel_id=1, source_target_pairs={{0,32},{32,64},{64,96},{96,0},{1,33},{33,65},{65,97},{97,1},{2,34}... | collective-permute-start | bytes 1572872 | tf_op jit(solution)/shard_map/ppermute | solution.py:424
  146.8 13.3 %collective-permute-start.8 = (bf16[128,2048]{1,0:T(8,128)(2,1)S(1)}, bf16[128,2048]{1,0:T(8,128)(2,1)}, u32[]{:S(2)}, u32[]{:S(2)}) collective-permute-start(bf16[128,2048]{1,0:T(8,128)(2,1)S(1)} %add_convert_fusion.2), channel_id=1, source_target_pairs={{0,96},{32,0},{64,32},{96,64},{1,97},{33,1},{65,33},{97,65},{2,98}... | collective-permute-start | bytes 1572872 | tf_op jit(solution)/shard_map/ppermute | solution.py:425
  159.4 0.8 copy-start.9
  160.2 3.4 %copy-start.1 = (bf16[16,512,128]{2,1,0:T(8,128)(2,1)}, bf16[16,512,128]{2,1,0:T(8,128)(2,1)S(1)}, u32[]{:S(2)}) copy-start(bf16[16,512,128]{2,1,0:T(8,128)(2,1)S(1)} %all-to-all-done.4.r_ref) | copy-start | bytes 6291460
  163.6 18.9 %all-to-all-start.5 = ((bf16[16,16,2048]{2,1,0:T(8,128)(2,1)}), bf16[16,16,2048]{2,1,0:T(8,128)(2,1)S(1)}, u32[]{:S(2)}, u32[]{:S(2)}) async-start(bf16[16,16,2048]{2,1,0:T(8,128)(2,1)} %pad_maximum_fusion), calls=%async_computation.5 | async-start | bytes 2097152 | tf_op jit(solution)/shard_map/all_to_all | solution.py:54

commit v9 on v8

--- a/solution.py
+++ b/solution.py
@@ -136,7 +136,7 @@
                     x_ref.at[at, pl.ds(0, 2 * TOK), :], kv.at[at], sems.at[3 * j]
                 ),
                 pltpu.make_async_copy(
-                    y_ref.at[at, pl.ds(0, 2 * TOK), :],
+                    y_ref.at[at],
                     kv.at[pl.ds(CHIPS + j * GROUP, GROUP)],
                     sems.at[3 * j + 1],
                 ),
@@ -431,10 +431,21 @@
     return (a, up[0], b, down[0]), first
 
 
-def join(a, own_a, b, own_b):
+def join_body(a_ref, own_a_ref, b_ref, own_b_ref, o_ref):
     n = CHIPS // 2
-    parts = (plus(a, own_a), plus(b, own_b))
-    return jnp.concatenate([part.reshape(n, 16, D) for part in parts], axis=0)
+    o_ref[0:n] = plus(a_ref[...], own_a_ref[...]).reshape(n, 16, D)
+    o_ref[n : 2 * n] = plus(b_ref[...], own_b_ref[...]).reshape(n, 16, D)
+
+
+def join(*parts):
+    return pl.pallas_call(
+        join_body,
+        out_shape=jax.ShapeDtypeStruct((CHIPS, 16, D), bf16),
+        in_specs=[pl.BlockSpec(memory_space=pltpu.VMEM)] * 4,
+        out_specs=pl.BlockSpec(memory_space=pltpu.VMEM),
+        compiler_params=pltpu.CompilerParams(vmem_limit_bytes=VMEM_LIMIT),
+        name="join",
+    )(*parts)
 
 
 def block_table(rider, core):
@@ -453,7 +464,7 @@
     cot_other = lax.ppermute(cot, "seq", CORE_SWAP)
     x = exchange(pack(block_offsets[0], key_states[0], value_states[0], queries[0]))
     x, g, cot_other = after(x, grad_attn_by_head(cot, out_weight), cot_other)
-    y = lax.ppermute(x, "seq", CORE_SWAP)
+    y = lax.ppermute(x[:, 0 : 2 * TOK], "seq", CORE_SWAP)
     g = exchange(g)
     table = block_table(x[:, RIDER, 0 : 2 * SLOTS], core)
     table, place = after(table, jnp.stack([core, lax.axis_index("dp")]))
@@ -471,8 +482,8 @@
     gq_home, gathered = after(gq_home, combine(own, got))
     sums, gq_home = sum_over_docs(up, down, gq_home)
     kv_home = exchange(gathered)
-    kv_home, *sums = after(kv_home, *sums)
-    weight_grad = jnp.sum(exchange(join(*sums)).astype(f32), axis=0)
+    kv_home, joined = after(kv_home, join(*sums))
+    weight_grad = jnp.sum(exchange(joined).astype(f32), axis=0)
     (gq,) = unpack(gq_home, 1)
     gk, gv = unpack(kv_home, 2)
     return gq[None], gk[None], gv[None], weight_grad

time: 185 us -> 187 us (1.011)
  other arithmetic: 8.6 us -> 5.19 us
  Pallas kernels: 48.6 us -> 51.4 us
  local copies, waits for them, and re-layouts: 1.95 us -> 4.68 us
    pallas_call x0 -> x1, Pallas kernels: none -> 2.74 us  [join(): pl.pallas_call(join_body, out_shape=jax.ShapeDtypeStruct((CHIPS, 16, D),...]
    convert_element_type x5 -> x4, other arithmetic: 5.32 us -> 2.98 us  [plus(): return (a.astype(f32) + b.astype(f32)).astype(bf16)]
  transfers between devices with their start and end apart: 15 -> 15, of which waited for: 9 -> 10; matrix products, arithmetic and copies ran while one was open for 2% -> 2% of each run, Pallas kernels for 25% -> 26%
where the time goes in v9:
time: 187 us; the launch traced here: 186 us
  waiting for transfers between devices  78.3 us (42%)
  Pallas kernels  51.4 us (27%)
  starting transfers between devices  45.2 us (24%)
  other arithmetic  5.19 us (3%)
  local copies, waits for them, and re-layouts  4.68 us (3%)
    all_to_all x5, waiting for transfers between devices, exchange(): lax.all_to_all(x, 'seq', 0, 0, axis_index_groups=SAME_CORE, tiled=True)  55.3 us
    all_to_all x5, starting transfers between devices, exchange(): lax.all_to_all(x, 'seq', 0, 0, axis_index_groups=SAME_CORE, tiled=True)  30.3 us
    ppermute x3, waiting for transfers between devices, sum_over_docs(): a = lax.ppermute(a, 'dp', route_up)  17.4 us
    pallas_call x1, Pallas kernels, attention_backward(): pl.pallas_call(backward_body, out_shape=(jax.ShapeDtypeStruct((CHIPS, 2 *...  12.6 us
    pallas_call x1, Pallas kernels, attention_forward(): pl.pallas_call(forward_body, out_shape=(jax.ShapeDtypeStruct((2 * CHIPS,...  9.6 us
    pallas_call x1, Pallas kernels, grad_attn_by_head(): pl.pallas_call(grad_attn_body, out_shape=jax.ShapeDtypeStruct((HEADS, TOK...  8.78 us
    ppermute x3, starting transfers between devices, sum_over_docs(): b = lax.ppermute(b, 'dp', route_down)  6.6 us
    pallas_call x1, Pallas kernels, weight_partial(): pl.pallas_call(weight_body, out_shape=(jax.ShapeDtypeStruct((CHUNK, D), b...  5.97 us
  transfers between devices with their start and end apart: 15, of which 10 were waited for; matrix products, arithmetic and copies ran while one was open for 2% of the time, Pallas kernels for 26%

profile of v9, /device:TPU:0, one launch (start us, length us, event | category | flops | bytes accessed | tf_op | source)
XLA Modules:
  0.0 185.5 jit_solution(15224346734895305439)
XLA Ops:
  0.6 3.3 %pack.1 = bf16[16,776,128]{2,1,0:T(8,128)(2,1)} custom-call(s32[2,4]{1,0:T(2,128)} %bitcast.20, bf16[256,2048]{1,0:T(8,128)(2,1)} %bitcast.17, bf16[256,2048]{1,0:T(8,128)(2,1)} %bitcast.18, bf16[256,2048]{1,0:T(8,128)(2,1)} %bitcast.19), custom_call_target="tpu_custom_call" | custom-call | tf_op jit(solution)/shard_map/pack/pallas_call | solution.py:75
  3.9 8.1 %all-to-all-start = ((bf16[16,776,128]{2,1,0:T(8,128)(2,1)}), bf16[16,776,128]{2,1,0:T(8,128)(2,1)S(1)}, u32[]{:S(2)}, u32[]{:S(2)}) async-start(bf16[16,776,128]{2,1,0:T(8,128)(2,1)} %pack.1), calls=%async_computation | async-start | bytes 6356992 | tf_op jit(solution)/shard_map/all_to_all | solution.py:54
  12.1 0.1 collective-permute-start
  12.2 8.8 %grad_attn.1 = bf16[16,256,128]{2,1,0:T(8,128)(2,1)} custom-call(bf16[256,2048]{1,0:T(8,128)(2,1)} %bitcast.12, bf16[2048,2048]{1,0:T(8,128)(2,1)} %w_ref.1), custom_call_target="tpu_custom_call" | custom-call | flops 2147483648 | bytes 10485760 | tf_op jit(solution)/shard_map/grad_attn/pallas_call | solution.py:114
  21.0 33.9 %all-to-all-done.x_ref = bf16[16,776,128]{2,1,0:T(8,128)(2,1)S(1)} async-done(((bf16[16,776,128]{2,1,0:T(8,128)(2,1)}), bf16[16,776,128]{2,1,0:T(8,128)(2,1)S(1)}, u32[]{:S(2)}, u32[]{:S(2)}) %all-to-all-start) | async-done | bytes 3178528 | tf_op jit(solution)/shard_map/all_to_all | solution.py:54
  54.9 1.8 slice.7
  56.7 8.1 %all-to-all-start.1 = ((bf16[16,256,128]{2,1,0:T(8,128)(2,1)}), bf16[16,256,128]{2,1,0:T(8,128)(2,1)}, u32[]{:S(2)}, u32[]{:S(2)}) async-start(bf16[16,256,128]{2,1,0:T(8,128)(2,1)} %grad_attn.1), calls=%async_computation.1 | async-start | bytes 2097152 | tf_op jit(solution)/shard_map/all_to_all | solution.py:54
  64.8 0.1 iota_add_fusion
  64.9 0.1 add.62
  65.0 0.6 pad_add_fusion.place
  65.6 0.1 reshape.47
  65.7 0.7 add_select_fusion.table
  66.4 9.6 %attn_fwd.1 = (bf16[32,64,256]{2,1,0:T(8,128)(2,1)}, bf16[32,640,128]{2,1,0:T(8,128)(2,1)}) custom-call(s32[32,4]{1,0:T(8,128)} %add_select_fusion.table, bf16[16,776,128]{2,1,0:T(8,128)(2,1)} %copy-done, bf16[16,512,128]{2,1,0:T(8,128)(2,1)} %collective-permute-done.1.y_ref), custom_call_target="tpu_custom_call" | custom-call | flops 1342177280 | bytes 12582912 | tf_op jit(solution)/shard_map/attn_fwd/pallas_call | solution.py:220
  76.0 7.3 %all-to-all-done.1.g_ref = bf16[16,256,128]{2,1,0:T(8,128)(2,1)} async-done(((bf16[16,256,128]{2,1,0:T(8,128)(2,1)}), bf16[16,256,128]{2,1,0:T(8,128)(2,1)}, u32[]{:S(2)}, u32[]{:S(2)}) %all-to-all-start.1) | async-done | bytes 1048608 | tf_op jit(solution)/shard_map/all_to_all | solution.py:54
  83.3 4.1 %all-to-all-start.2 = ((bf16[32,64,256]{2,1,0:T(8,128)(2,1)}), bf16[32,64,256]{2,1,0:T(8,128)(2,1)S(1)}, u32[]{:S(2)}, u32[]{:S(2)}) async-start(bf16[32,64,256]{2,1,0:T(8,128)(2,1)} %get-tuple-element.49), calls=%async_computation.2 | async-start | bytes 2097152 | tf_op jit(solution)/shard_map/all_to_all | solution.py:473
  87.4 12.6 %attn_bwd.1 = (bf16[16,512,128]{2,1,0:T(8,128)(2,1)}, bf16[16,512,128]{2,1,0:T(8,128)(2,1)}, bf16[16,256,128]{2,1,0:T(8,128)(2,1)}) custom-call(s32[32,4]{1,0:T(8,128)} %add_select_fusion.table, bf16[16,776,128]{2,1,0:T(8,128)(2,1)} %copy-done, bf16[16,512,128]{2,1,0:T(8,128)(2,1)} %collective-permute-done.1.y_ref, ...), custom_call_target="tpu_custom_call" | custom-call | flops 2684354560 | bytes 17825792 | tf_op jit(solution)/shard_map/attn_bwd/pallas_call | solution.py:324
  100.1 4.0 %all-to-all-done.2 = bf16[32,64,256]{2,1,0:T(8,128)(2,1)S(1)} async-done(((bf16[32,64,256]{2,1,0:T(8,128)(2,1)}), bf16[32,64,256]{2,1,0:T(8,128)(2,1)S(1)}, u32[]{:S(2)}, u32[]{:S(2)}) %all-to-all-start.2) | async-done | bytes 1048608 | tf_op jit(solution)/shard_map/all_to_all | solution.py:473
  104.0 1.0 copy-done.4
  105.0 0.4 collective-permute-start.2
  105.4 3.7 %all-to-all-start.3 = ((bf16[16,256,128]{2,1,0:T(8,128)(2,1)}), bf16[16,256,128]{2,1,0:T(8,128)(2,1)S(1)}, u32[]{:S(2)}, u32[]{:S(2)}) async-start(bf16[16,256,128]{2,1,0:T(8,128)(2,1)} %get-tuple-element.66), calls=%async_computation.3 | async-start | bytes 2097152 | tf_op jit(solution)/shard_map/all_to_all | solution.py:54
  109.0 0.3 collective-permute-done.2.got_ref
  109.4 6.0 %weight_partial.1 = (bf16[128,2048]{1,0:T(8,128)(2,1)}, bf16[128,2048]{1,0:T(8,128)(2,1)}, bf16[128,2048]{1,0:T(8,128)(2,1)}, bf16[128,2048]{1,0:T(8,128)(2,1)},...) custom-call(s32[2]{0:T(128)} %pad_add_fusion.place, ...), custom_call_target="tpu_custom_call" | custom-call | flops 2147483648 | bytes 8388608 | tf_op jit(solution)/shard_map/weight_partial/pallas_call | solution.py:395
  115.4 1.6 collective-permute-start.3
  117.0 1.7 collective-permute-start.4
  118.7 3.4 %combine.1 = bf16[16,512,128]{2,1,0:T(8,128)(2,1)} custom-call(bf16[16,512,128]{2,1,0:T(8,128)(2,1)} %get-tuple-element.67.own_ref, bf16[16,512,128]{2,1,0:T(8,128)(2,1)} %copy-done.3), custom_call_target="tpu_custom_call" | custom-call | flops 1048576 | bytes 6291456 | tf_op jit(solution)/shard_map/combine/pallas_call | solution.py:359
  122.1 5.3 %all-to-all-done.3.r_ref = bf16[16,256,128]{2,1,0:T(8,128)(2,1)S(1)} async-done(((bf16[16,256,128]{2,1,0:T(8,128)(2,1)}), bf16[16,256,128]{2,1,0:T(8,128)(2,1)S(1)}, u32[]{:S(2)}, u32[]{:S(2)}) %all-to-all-start.3) | async-done | bytes 1048608 | tf_op jit(solution)/shard_map/all_to_all | solution.py:54
  127.4 1.0 copy-done.2
  128.4 3.7 %all-to-all-start.4 = ((bf16[16,512,128]{2,1,0:T(8,128)(2,1)}), bf16[16,512,128]{2,1,0:T(8,128)(2,1)S(1)}, u32[]{:S(2)}, u32[]{:S(2)}) async-start(bf16[16,512,128]{2,1,0:T(8,128)(2,1)} %combine.1), calls=%async_computation.4 | async-start | bytes 4194304 | tf_op jit(solution)/shard_map/all_to_all | solution.py:54
  132.1 1.4 add_convert_fusion.3
  133.5 1.8 collective-permute-start.5
  135.3 1.3 add_convert_fusion.1
  136.7 1.8 collective-permute-start.7
  138.5 9.0 %collective-permute-done.5 = bf16[128,2048]{1,0:T(8,128)(2,1)S(1)} collective-permute-done((bf16[128,2048]{1,0:T(8,128)(2,1)S(1)}, bf16[128,2048]{1,0:T(8,128)(2,1)S(1)}, u32[]{:S(2)}, u32[]{:S(2)}) %collective-permute-start.5) | collective-permute-done | bytes 524320 | tf_op jit(solution)/shard_map/ppermute | solution.py:424
  147.5 0.1 add_convert_fusion.2
  147.6 0.3 collective-permute-start.6
  147.9 0.9 collective-permute-done.7
  148.9 0.1 add_convert_fusion
  149.0 3.0 %collective-permute-start.8 = (bf16[128,2048]{1,0:T(8,128)(2,1)S(1)}, bf16[128,2048]{1,0:T(8,128)(2,1)S(1)}, u32[]{:S(2)}, u32[]{:S(2)}) collective-permute-start(bf16[128,2048]{1,0:T(8,128)(2,1)S(1)} %add_convert_fusion), channel_id=1, source_target_pairs={{0,96},{32,0},{64,32},{96,64},{1,97},{33,1},{65,33},{97,65},{2,98}... | collective-permute-start | bytes 1572872 | tf_op jit(solution)/shard_map/ppermute | solution.py:425
  152.0 8.4 %collective-permute-done.6.a_ref = bf16[128,2048]{1,0:T(8,128)(2,1)S(1)} collective-permute-done((bf16[128,2048]{1,0:T(8,128)(2,1)S(1)}, bf16[128,2048]{1,0:T(8,128)(2,1)S(1)}, u32[]{:S(2)}, u32[]{:S(2)}) %collective-permute-start.6) | collective-permute-done | bytes 524320 | tf_op jit(solution)/shard_map/ppermute | solution.py:424
  160.4 0.4 collective-permute-done.8.b_ref
  160.8 0.4 copy-done.7
  161.2 0.4 copy-done.8
  161.6 2.7 %join.1 = bf16[16,16,2048]{2,1,0:T(8,128)(2,1)} custom-call(bf16[128,2048]{1,0:T(8,128)(2,1)} %copy-done.7, bf16[128,2048]{1,0:T(8,128)(2,1)} %get-tuple-element.75.own_a_ref, bf16[128,2048]{1,0:T(8,128)(2,1)} %copy-done.8, bf16[128,2048]{1,0:T(8,128)(2,1)} %get-tuple-element.79.own_b_ref), custom_call_target="tpu_custom_call" | custom-call | tf_op jit(solution)/shard_map/join/pallas_call | solution.py:441
  164.3 6.7 %all-to-all-start.5 = ((bf16[16,16,2048]{2,1,0:T(8,128)(2,1)}), bf16[16,16,2048]{2,1,0:T(8,128)(2,1)S(1)}, u32[]{:S(2)}, u32[]{:S(2)}) async-start(bf16[16,16,2048]{2,1,0:T(8,128)(2,1)} %join.1), calls=%async_computation.5 | async-start | bytes 2097152 | tf_op jit(solution)/shard_map/all_to_all | solution.py:54
  171.0 2.2 %unpack.2 = bf16[256,2048]{1,0:T(8,128)(2,1)} custom-call(bf16[16,256,128]{2,1,0:T(8,128)(2,1)} %copy-done.2), custom_call_target="tpu_custom_call" | custom-call | bytes 2097152 | tf_op jit(solution)/shard_map/unpack/pallas_call | solution.py:95
  173.2 2.8 %unpack.3 = (bf16[256,2048]{1,0:T(8,128)(2,1)}, bf16[256,2048]{1,0:T(8,128)(2,1)}) custom-call(bf16[16,512,128]{2,1,0:T(8,128)(2,1)} %copy-done.1), custom_call_target="tpu_custom_call" | custom-call | bytes 4194304 | tf_op jit(solution)/shard_map/unpack/pallas_call | solution.py:95
  176.0 8.7 %all-to-all-done.5 = bf16[16,16,2048]{2,1,0:T(8,128)(2,1)S(1)} async-done(((bf16[16,16,2048]{2,1,0:T(8,128)(2,1)}), bf16[16,16,2048]{2,1,0:T(8,128)(2,1)S(1)}, u32[]{:S(2)}, u32[]{:S(2)}) %all-to-all-start.5) | async-done | bytes 1048608 | tf_op jit(solution)/shard_map/all_to_all | solution.py:54
  184.7 0.8 convert_reduce_fusion
  (22 shorter events, 0.1 us)
Async XLA Ops:
  3.9 51.0 %all-to-all-start = ((bf16[16,776,128]{2,1,0:T(8,128)(2,1)}), bf16[16,776,128]{2,1,0:T(8,128)(2,1)S(1)}, u32[]{:S(2)}, u32[]{:S(2)}) async-start(bf16[16,776,128]{2,1,0:T(8,128)(2,1)} %pack.1), calls=%async_computation | async-start | bytes 6356992 | tf_op jit(solution)/shard_map/all_to_all | solution.py:54
  12.1 8.9 %collective-permute-start = (bf16[256,2048]{1,0:T(8,128)(2,1)}, bf16[256,2048]{1,0:T(8,128)(2,1)}, u32[]{:S(2)}, u32[]{:S(2)}) collective-permute-start(bf16[256,2048]{1,0:T(8,128)(2,1)} %bitcast.11), channel_id=1, source_target_pairs={{0,1},{1,0},{2,3},{3,2},{4,5},{5,4},{6,7},{7,6},{8,9},{9,8},{10,11... | collective-permute-start | bytes 3145736 | tf_op jit(solution)/shard_map/ppermute | solution.py:464
  54.9 10.7 %copy-start = (bf16[16,776,128]{2,1,0:T(8,128)(2,1)}, bf16[16,776,128]{2,1,0:T(8,128)(2,1)S(1)}, u32[]{:S(2)}) copy-start(bf16[16,776,128]{2,1,0:T(8,128)(2,1)S(1)} %all-to-all-done.x_ref) | copy-start | bytes 9535492
  56.6 9.7 %collective-permute-start.1 = (bf16[16,512,128]{2,1,0:T(8,128)(2,1)}, bf16[16,512,128]{2,1,0:T(8,128)(2,1)}, u32[]{:S(2)}, u32[]{:S(2)}) collective-permute-start(bf16[16,512,128]{2,1,0:T(8,128)(2,1)} %slice.7), channel_id=1, source_target_pairs={{0,1},{1,0},{2,3},{3,2},{4,5},{5,4},{6,7},{7,6},{8,9},{9,8},{10,11... | collective-permute-start | bytes 6291464 | tf_op jit(solution)/shard_map/ppermute | solution.py:467
  56.7 26.7 %all-to-all-start.1 = ((bf16[16,256,128]{2,1,0:T(8,128)(2,1)}), bf16[16,256,128]{2,1,0:T(8,128)(2,1)}, u32[]{:S(2)}, u32[]{:S(2)}) async-start(bf16[16,256,128]{2,1,0:T(8,128)(2,1)} %grad_attn.1), calls=%async_computation.1 | async-start | bytes 2097152 | tf_op jit(solution)/shard_map/all_to_all | solution.py:54
  83.3 20.7 %all-to-all-start.2 = ((bf16[32,64,256]{2,1,0:T(8,128)(2,1)}), bf16[32,64,256]{2,1,0:T(8,128)(2,1)S(1)}, u32[]{:S(2)}, u32[]{:S(2)}) async-start(bf16[32,64,256]{2,1,0:T(8,128)(2,1)} %get-tuple-element.49), calls=%async_computation.2 | async-start | bytes 2097152 | tf_op jit(solution)/shard_map/all_to_all | solution.py:473
  104.0 1.0 copy-start.4
  105.0 4.4 %collective-permute-start.2 = (bf16[16,512,128]{2,1,0:T(8,128)(2,1)}, bf16[16,512,128]{2,1,0:T(8,128)(2,1)S(1)}, u32[]{:S(2)}, u32[]{:S(2)}) collective-permute-start(bf16[16,512,128]{2,1,0:T(8,128)(2,1)} %get-tuple-element.55), channel_id=1, source_target_pairs={{0,1},{1,0},{2,3},{3,2},{4,5},{5,4},{6,7},{7,6},{8,9},{9,8},{10,11... | collective-permute-start | bytes 6291464 | tf_op jit(solution)/shard_map/ppermute | solution.py:477
  105.4 22.0 %all-to-all-start.3 = ((bf16[16,256,128]{2,1,0:T(8,128)(2,1)}), bf16[16,256,128]{2,1,0:T(8,128)(2,1)S(1)}, u32[]{:S(2)}, u32[]{:S(2)}) async-start(bf16[16,256,128]{2,1,0:T(8,128)(2,1)} %get-tuple-element.66), calls=%async_computation.3 | async-start | bytes 2097152 | tf_op jit(solution)/shard_map/all_to_all | solution.py:54
  109.4 6.0 %copy-start.3 = (bf16[16,512,128]{2,1,0:T(8,128)(2,1)}, bf16[16,512,128]{2,1,0:T(8,128)(2,1)S(1)}, u32[]{:S(2)}) copy-start(bf16[16,512,128]{2,1,0:T(8,128)(2,1)S(1)} %collective-permute-done.2.got_ref) | copy-start | bytes 6291460
  115.4 16.7 %collective-permute-start.3 = (bf16[128,2048]{1,0:T(8,128)(2,1)}, bf16[128,2048]{1,0:T(8,128)(2,1)}, u32[]{:S(2)}, u32[]{:S(2)}) collective-permute-start(bf16[128,2048]{1,0:T(8,128)(2,1)} %get-tuple-element.64), channel_id=1, source_target_pairs={{0,32},{32,64},{64,96},{96,0},{1,33},{33,65},{65,97},{97,1},{2,34}... | collective-permute-start | bytes 1572872 | tf_op jit(solution)/shard_map/ppermute | solution.py:424
  117.0 15.2 %collective-permute-start.4 = (bf16[128,2048]{1,0:T(8,128)(2,1)}, bf16[128,2048]{1,0:T(8,128)(2,1)}, u32[]{:S(2)}, u32[]{:S(2)}) collective-permute-start(bf16[128,2048]{1,0:T(8,128)(2,1)} %get-tuple-element.65), channel_id=1, source_target_pairs={{0,96},{32,0},{64,32},{96,64},{1,97},{33,1},{65,33},{97,65},{2,98}... | collective-permute-start | bytes 1572872 | tf_op jit(solution)/shard_map/ppermute | solution.py:425
  127.4 1.0 copy-start.2
  128.4 36.0 %all-to-all-start.4 = ((bf16[16,512,128]{2,1,0:T(8,128)(2,1)}), bf16[16,512,128]{2,1,0:T(8,128)(2,1)S(1)}, u32[]{:S(2)}, u32[]{:S(2)}) async-start(bf16[16,512,128]{2,1,0:T(8,128)(2,1)} %combine.1), calls=%async_computation.4 | async-start | bytes 4194304 | tf_op jit(solution)/shard_map/all_to_all | solution.py:54
  132.1 15.4 %copy-start.6 = (bf16[128,2048]{1,0:T(8,128)(2,1)S(1)}, bf16[128,2048]{1,0:T(8,128)(2,1)}, u32[]{:S(2)}) copy-start(bf16[128,2048]{1,0:T(8,128)(2,1)} %get-tuple-element.74) | copy-start | bytes 1572868
  132.1 16.8 %copy-start.5 = (bf16[128,2048]{1,0:T(8,128)(2,1)S(1)}, bf16[128,2048]{1,0:T(8,128)(2,1)}, u32[]{:S(2)}) copy-start(bf16[128,2048]{1,0:T(8,128)(2,1)} %get-tuple-element.78) | copy-start | bytes 1572868
  133.5 13.9 %collective-permute-start.5 = (bf16[128,2048]{1,0:T(8,128)(2,1)S(1)}, bf16[128,2048]{1,0:T(8,128)(2,1)S(1)}, u32[]{:S(2)}, u32[]{:S(2)}) collective-permute-start(bf16[128,2048]{1,0:T(8,128)(2,1)S(1)} %add_convert_fusion.3), channel_id=1, source_target_pairs={{0,32},{32,64},{64,96},{96,0},{1,33},{33,65},{65,97},{97,1},{2,34}... | collective-permute-start | bytes 1572872 | tf_op jit(solution)/shard_map/ppermute | solution.py:424
  136.7 12.2 %collective-permute-start.7 = (bf16[128,2048]{1,0:T(8,128)(2,1)S(1)}, bf16[128,2048]{1,0:T(8,128)(2,1)S(1)}, u32[]{:S(2)}, u32[]{:S(2)}) collective-permute-start(bf16[128,2048]{1,0:T(8,128)(2,1)S(1)} %add_convert_fusion.1), channel_id=1, source_target_pairs={{0,96},{32,0},{64,32},{96,64},{1,97},{33,1},{65,33},{97,65},{2,98}... | collective-permute-start | bytes 1572872 | tf_op jit(solution)/shard_map/ppermute | solution.py:425
  147.6 12.8 %collective-permute-start.6 = (bf16[128,2048]{1,0:T(8,128)(2,1)S(1)}, bf16[128,2048]{1,0:T(8,128)(2,1)S(1)}, u32[]{:S(2)}, u32[]{:S(2)}) collective-permute-start(bf16[128,2048]{1,0:T(8,128)(2,1)S(1)} %add_convert_fusion.2), channel_id=1, source_target_pairs={{0,32},{32,64},{64,96},{96,0},{1,33},{33,65},{65,97},{97,1},{2,34}... | collective-permute-start | bytes 1572872 | tf_op jit(solution)/shard_map/ppermute | solution.py:424
  149.0 11.8 %collective-permute-start.8 = (bf16[128,2048]{1,0:T(8,128)(2,1)S(1)}, bf16[128,2048]{1,0:T(8,128)(2,1)S(1)}, u32[]{:S(2)}, u32[]{:S(2)}) collective-permute-start(bf16[128,2048]{1,0:T(8,128)(2,1)S(1)} %add_convert_fusion), channel_id=1, source_target_pairs={{0,96},{32,0},{64,32},{96,64},{1,97},{33,1},{65,33},{97,65},{2,98}... | collective-permute-start | bytes 1572872 | tf_op jit(solution)/shard_map/ppermute | solution.py:425
  160.4 0.8 copy-start.7
  160.8 0.8 copy-start.8
  164.3 8.9 %copy-start.1 = (bf16[16,512,128]{2,1,0:T(8,128)(2,1)}, bf16[16,512,128]{2,1,0:T(8,128)(2,1)S(1)}, u32[]{:S(2)}) copy-start(bf16[16,512,128]{2,1,0:T(8,128)(2,1)S(1)} %all-to-all-done.4.r_ref) | copy-start | bytes 6291460
  164.3 20.4 %all-to-all-start.5 = ((bf16[16,16,2048]{2,1,0:T(8,128)(2,1)}), bf16[16,16,2048]{2,1,0:T(8,128)(2,1)S(1)}, u32[]{:S(2)}, u32[]{:S(2)}) async-start(bf16[16,16,2048]{2,1,0:T(8,128)(2,1)} %join.1), calls=%async_computation.5 | async-start | bytes 2097152 | tf_op jit(solution)/shard_map/all_to_all | solution.py:54

commit v10 on v9

--- a/solution.py
+++ b/solution.py
@@ -136,7 +136,7 @@
                     x_ref.at[at, pl.ds(0, 2 * TOK), :], kv.at[at], sems.at[3 * j]
                 ),
                 pltpu.make_async_copy(
-                    y_ref.at[at],
+                    y_ref.at[at, pl.ds(0, 2 * TOK), :],
                     kv.at[pl.ds(CHIPS + j * GROUP, GROUP)],
                     sems.at[3 * j + 1],
                 ),
@@ -464,7 +464,7 @@
     cot_other = lax.ppermute(cot, "seq", CORE_SWAP)
     x = exchange(pack(block_offsets[0], key_states[0], value_states[0], queries[0]))
     x, g, cot_other = after(x, grad_attn_by_head(cot, out_weight), cot_other)
-    y = lax.ppermute(x[:, 0 : 2 * TOK], "seq", CORE_SWAP)
+    y = lax.ppermute(x, "seq", CORE_SWAP)
     g = exchange(g)
     table = block_table(x[:, RIDER, 0 : 2 * SLOTS], core)
     table, place = after(table, jnp.stack([core, lax.axis_index("dp")]))

time: 187 us -> 185 us (0.989)
  local copies, waits for them, and re-layouts: 4.68 us -> 1.96 us
where the time goes in v10:
time: 185 us; the launch traced here: 183 us
  waiting for transfers between devices  80 us (43%)
  Pallas kernels  51.3 us (28%)
  starting transfers between devices  43.5 us (24%)
  other arithmetic  5.2 us (3%)
  local copies, waits for them, and re-layouts  1.96 us (1%)
    all_to_all x5, waiting for transfers between devices, exchange(): lax.all_to_all(x, 'seq', 0, 0, axis_index_groups=SAME_CORE, tiled=True)  55.3 us
    all_to_all x5, starting transfers between devices, exchange(): lax.all_to_all(x, 'seq', 0, 0, axis_index_groups=SAME_CORE, tiled=True)  28.6 us
    ppermute x3, waiting for transfers between devices, sum_over_docs(): a = lax.ppermute(a, 'dp', route_up)  19.1 us
    pallas_call x1, Pallas kernels, attention_backward(): pl.pallas_call(backward_body, out_shape=(jax.ShapeDtypeStruct((CHIPS, 2 *...  12.6 us
    pallas_call x1, Pallas kernels, attention_forward(): pl.pallas_call(forward_body, out_shape=(jax.ShapeDtypeStruct((2 * CHIPS,...  9.6 us
    pallas_call x1, Pallas kernels, grad_attn_by_head(): pl.pallas_call(grad_attn_body, out_shape=jax.ShapeDtypeStruct((HEADS, TOK...  8.78 us
    ppermute x3, starting transfers between devices, sum_over_docs(): b = lax.ppermute(b, 'dp', route_down)  6.9 us
    pallas_call x1, Pallas kernels, weight_partial(): pl.pallas_call(weight_body, out_shape=(jax.ShapeDtypeStruct((CHUNK, D), b...  5.95 us
  transfers between devices with their start and end apart: 15, of which 10 were waited for; matrix products, arithmetic and copies ran while one was open for 2% of the time, Pallas kernels for 26%

profile of v10, /device:TPU:0, one launch (start us, length us, event | category | flops | bytes accessed | tf_op | source)
XLA Modules:
  0.0 182.8 jit_solution(11993324293315378780)
XLA Ops:
  0.6 3.3 %pack.1 = bf16[16,776,128]{2,1,0:T(8,128)(2,1)} custom-call(s32[2,4]{1,0:T(2,128)} %bitcast.20, bf16[256,2048]{1,0:T(8,128)(2,1)} %bitcast.17, bf16[256,2048]{1,0:T(8,128)(2,1)} %bitcast.18, bf16[256,2048]{1,0:T(8,128)(2,1)} %bitcast.19), custom_call_target="tpu_custom_call" | custom-call | tf_op jit(solution)/shard_map/pack/pallas_call | solution.py:75
  3.9 8.1 %all-to-all-start = ((bf16[16,776,128]{2,1,0:T(8,128)(2,1)}), bf16[16,776,128]{2,1,0:T(8,128)(2,1)S(1)}, u32[]{:S(2)}, u32[]{:S(2)}) async-start(bf16[16,776,128]{2,1,0:T(8,128)(2,1)} %pack.1), calls=%async_computation | async-start | bytes 6356992 | tf_op jit(solution)/shard_map/all_to_all | solution.py:54
  12.1 0.1 collective-permute-start
  12.2 8.8 %grad_attn.1 = bf16[16,256,128]{2,1,0:T(8,128)(2,1)} custom-call(bf16[256,2048]{1,0:T(8,128)(2,1)} %bitcast.12, bf16[2048,2048]{1,0:T(8,128)(2,1)} %w_ref.1), custom_call_target="tpu_custom_call" | custom-call | flops 2147483648 | bytes 10485760 | tf_op jit(solution)/shard_map/grad_attn/pallas_call | solution.py:114
  21.0 0.0 collective-permute-done.cb_ref
  21.0 33.9 %all-to-all-done.x_ref = bf16[16,776,128]{2,1,0:T(8,128)(2,1)S(1)} async-done(((bf16[16,776,128]{2,1,0:T(8,128)(2,1)}), bf16[16,776,128]{2,1,0:T(8,128)(2,1)S(1)}, u32[]{:S(2)}, u32[]{:S(2)}) %all-to-all-start) | async-done | bytes 3178528 | tf_op jit(solution)/shard_map/all_to_all | solution.py:54
  54.9 8.1 %all-to-all-start.1 = ((bf16[16,256,128]{2,1,0:T(8,128)(2,1)}), bf16[16,256,128]{2,1,0:T(8,128)(2,1)}, u32[]{:S(2)}, u32[]{:S(2)}) async-start(bf16[16,256,128]{2,1,0:T(8,128)(2,1)} %grad_attn.1), calls=%async_computation.1 | async-start | bytes 2097152 | tf_op jit(solution)/shard_map/all_to_all | solution.py:54
  63.1 0.1 iota_add_fusion
  63.1 0.1 add.62
  63.2 0.6 pad_add_fusion.place
  63.9 0.1 reshape.47
  63.9 0.7 add_select_fusion.table
  64.6 9.6 %attn_fwd.1 = (bf16[32,64,256]{2,1,0:T(8,128)(2,1)}, bf16[32,640,128]{2,1,0:T(8,128)(2,1)}) custom-call(s32[32,4]{1,0:T(8,128)} %add_select_fusion.table, bf16[16,776,128]{2,1,0:T(8,128)(2,1)} %copy-done, bf16[16,776,128]{2,1,0:T(8,128)(2,1)} %collective-permute-done.1.y_ref), custom_call_target="tpu_custom_call" | custom-call | flops 1342177280 | bytes 12582912 | tf_op jit(solution)/shard_map/attn_fwd/pallas_call | solution.py:220
  74.2 7.3 %all-to-all-done.1.g_ref = bf16[16,256,128]{2,1,0:T(8,128)(2,1)} async-done(((bf16[16,256,128]{2,1,0:T(8,128)(2,1)}), bf16[16,256,128]{2,1,0:T(8,128)(2,1)}, u32[]{:S(2)}, u32[]{:S(2)}) %all-to-all-start.1) | async-done | bytes 1048608 | tf_op jit(solution)/shard_map/all_to_all | solution.py:54
  81.6 4.1 %all-to-all-start.2 = ((bf16[32,64,256]{2,1,0:T(8,128)(2,1)}), bf16[32,64,256]{2,1,0:T(8,128)(2,1)S(1)}, u32[]{:S(2)}, u32[]{:S(2)}) async-start(bf16[32,64,256]{2,1,0:T(8,128)(2,1)} %get-tuple-element.49), calls=%async_computation.2 | async-start | bytes 2097152 | tf_op jit(solution)/shard_map/all_to_all | solution.py:473
  85.7 12.6 %attn_bwd.1 = (bf16[16,512,128]{2,1,0:T(8,128)(2,1)}, bf16[16,512,128]{2,1,0:T(8,128)(2,1)}, bf16[16,256,128]{2,1,0:T(8,128)(2,1)}) custom-call(s32[32,4]{1,0:T(8,128)} %add_select_fusion.table, bf16[16,776,128]{2,1,0:T(8,128)(2,1)} %copy-done, bf16[16,776,128]{2,1,0:T(8,128)(2,1)} %collective-permute-done.1.y_ref, ...), custom_call_target="tpu_custom_call" | custom-call | flops 2684354560 | bytes 17825792 | tf_op jit(solution)/shard_map/attn_bwd/pallas_call | solution.py:324
  98.3 4.0 %all-to-all-done.2 = bf16[32,64,256]{2,1,0:T(8,128)(2,1)S(1)} async-done(((bf16[32,64,256]{2,1,0:T(8,128)(2,1)}), bf16[32,64,256]{2,1,0:T(8,128)(2,1)S(1)}, u32[]{:S(2)}, u32[]{:S(2)}) %all-to-all-start.2) | async-done | bytes 1048608 | tf_op jit(solution)/shard_map/all_to_all | solution.py:473
  102.3 1.0 copy-done.4
  103.3 0.4 collective-permute-start.2
  103.6 3.7 %all-to-all-start.3 = ((bf16[16,256,128]{2,1,0:T(8,128)(2,1)}), bf16[16,256,128]{2,1,0:T(8,128)(2,1)S(1)}, u32[]{:S(2)}, u32[]{:S(2)}) async-start(bf16[16,256,128]{2,1,0:T(8,128)(2,1)} %get-tuple-element.66), calls=%async_computation.3 | async-start | bytes 2097152 | tf_op jit(solution)/shard_map/all_to_all | solution.py:54
  107.3 0.3 collective-permute-done.2.got_ref
  107.6 5.9 %weight_partial.1 = (bf16[128,2048]{1,0:T(8,128)(2,1)}, bf16[128,2048]{1,0:T(8,128)(2,1)}, bf16[128,2048]{1,0:T(8,128)(2,1)}, bf16[128,2048]{1,0:T(8,128)(2,1)},...) custom-call(s32[2]{0:T(128)} %pad_add_fusion.place, ...), custom_call_target="tpu_custom_call" | custom-call | flops 2147483648 | bytes 8388608 | tf_op jit(solution)/shard_map/weight_partial/pallas_call | solution.py:395
  113.6 1.6 collective-permute-start.3
  115.2 1.7 collective-permute-start.4
  116.9 3.4 %combine.1 = bf16[16,512,128]{2,1,0:T(8,128)(2,1)} custom-call(bf16[16,512,128]{2,1,0:T(8,128)(2,1)} %get-tuple-element.67.own_ref, bf16[16,512,128]{2,1,0:T(8,128)(2,1)} %copy-done.3), custom_call_target="tpu_custom_call" | custom-call | flops 1048576 | bytes 6291456 | tf_op jit(solution)/shard_map/combine/pallas_call | solution.py:359
  120.3 5.3 %all-to-all-done.3.r_ref = bf16[16,256,128]{2,1,0:T(8,128)(2,1)S(1)} async-done(((bf16[16,256,128]{2,1,0:T(8,128)(2,1)}), bf16[16,256,128]{2,1,0:T(8,128)(2,1)S(1)}, u32[]{:S(2)}, u32[]{:S(2)}) %all-to-all-start.3) | async-done | bytes 1048608 | tf_op jit(solution)/shard_map/all_to_all | solution.py:54
  125.6 3.7 %all-to-all-start.4 = ((bf16[16,512,128]{2,1,0:T(8,128)(2,1)}), bf16[16,512,128]{2,1,0:T(8,128)(2,1)S(1)}, u32[]{:S(2)}, u32[]{:S(2)}) async-start(bf16[16,512,128]{2,1,0:T(8,128)(2,1)} %combine.1), calls=%async_computation.4 | async-start | bytes 4194304 | tf_op jit(solution)/shard_map/all_to_all | solution.py:54
  129.4 0.0 collective-permute-done.3
  129.4 1.4 add_convert_fusion.3
  130.8 1.8 collective-permute-start.5
  132.6 1.3 add_convert_fusion.1
  133.9 1.8 collective-permute-start.7
  135.8 9.9 %collective-permute-done.5 = bf16[128,2048]{1,0:T(8,128)(2,1)S(1)} collective-permute-done((bf16[128,2048]{1,0:T(8,128)(2,1)S(1)}, bf16[128,2048]{1,0:T(8,128)(2,1)S(1)}, u32[]{:S(2)}, u32[]{:S(2)}) %collective-permute-start.5) | collective-permute-done | bytes 524320 | tf_op jit(solution)/shard_map/ppermute | solution.py:424
  145.6 0.1 add_convert_fusion.2
  145.8 0.1 collective-permute-start.6
  145.8 0.9 collective-permute-done.7
  146.7 0.1 add_convert_fusion
  146.8 3.3 %collective-permute-start.8 = (bf16[128,2048]{1,0:T(8,128)(2,1)S(1)}, bf16[128,2048]{1,0:T(8,128)(2,1)S(1)}, u32[]{:S(2)}, u32[]{:S(2)}) collective-permute-start(bf16[128,2048]{1,0:T(8,128)(2,1)S(1)} %add_convert_fusion), channel_id=1, source_target_pairs={{0,96},{32,0},{64,32},{96,64},{1,97},{33,1},{65,33},{97,65},{2,98}... | collective-permute-start | bytes 1572872 | tf_op jit(solution)/shard_map/ppermute | solution.py:425
  150.2 9.2 %collective-permute-done.6.a_ref = bf16[128,2048]{1,0:T(8,128)(2,1)S(1)} collective-permute-done((bf16[128,2048]{1,0:T(8,128)(2,1)S(1)}, bf16[128,2048]{1,0:T(8,128)(2,1)S(1)}, u32[]{:S(2)}, u32[]{:S(2)}) %collective-permute-start.6) | collective-permute-done | bytes 524320 | tf_op jit(solution)/shard_map/ppermute | solution.py:424
  159.4 0.4 collective-permute-done.8.b_ref
  159.8 0.4 copy-done.7
  160.2 0.4 copy-done.8
  160.6 2.7 %join.1 = bf16[16,16,2048]{2,1,0:T(8,128)(2,1)} custom-call(bf16[128,2048]{1,0:T(8,128)(2,1)} %copy-done.7, bf16[128,2048]{1,0:T(8,128)(2,1)} %get-tuple-element.75.own_a_ref, bf16[128,2048]{1,0:T(8,128)(2,1)} %copy-done.8, bf16[128,2048]{1,0:T(8,128)(2,1)} %get-tuple-element.79.own_b_ref), custom_call_target="tpu_custom_call" | custom-call | tf_op jit(solution)/shard_map/join/pallas_call | solution.py:441
  163.4 5.0 %all-to-all-start.5 = ((bf16[16,16,2048]{2,1,0:T(8,128)(2,1)}), bf16[16,16,2048]{2,1,0:T(8,128)(2,1)S(1)}, u32[]{:S(2)}, u32[]{:S(2)}) async-start(bf16[16,16,2048]{2,1,0:T(8,128)(2,1)} %join.1), calls=%async_computation.5 | async-start | bytes 2097152 | tf_op jit(solution)/shard_map/all_to_all | solution.py:54
  168.3 2.2 %unpack.2 = bf16[256,2048]{1,0:T(8,128)(2,1)} custom-call(bf16[16,256,128]{2,1,0:T(8,128)(2,1)} %copy-done.2), custom_call_target="tpu_custom_call" | custom-call | bytes 2097152 | tf_op jit(solution)/shard_map/unpack/pallas_call | solution.py:95
  170.5 2.8 %unpack.3 = (bf16[256,2048]{1,0:T(8,128)(2,1)}, bf16[256,2048]{1,0:T(8,128)(2,1)}) custom-call(bf16[16,512,128]{2,1,0:T(8,128)(2,1)} %copy-done.1), custom_call_target="tpu_custom_call" | custom-call | bytes 4194304 | tf_op jit(solution)/shard_map/unpack/pallas_call | solution.py:95
  173.3 8.7 %all-to-all-done.5 = bf16[16,16,2048]{2,1,0:T(8,128)(2,1)S(1)} async-done(((bf16[16,16,2048]{2,1,0:T(8,128)(2,1)}), bf16[16,16,2048]{2,1,0:T(8,128)(2,1)S(1)}, u32[]{:S(2)}, u32[]{:S(2)}) %all-to-all-start.5) | async-done | bytes 1048608 | tf_op jit(solution)/shard_map/all_to_all | solution.py:54
  182.0 0.8 convert_reduce_fusion
  (21 shorter events, 0.1 us)
Async XLA Ops:
  3.9 51.0 %all-to-all-start = ((bf16[16,776,128]{2,1,0:T(8,128)(2,1)}), bf16[16,776,128]{2,1,0:T(8,128)(2,1)S(1)}, u32[]{:S(2)}, u32[]{:S(2)}) async-start(bf16[16,776,128]{2,1,0:T(8,128)(2,1)} %pack.1), calls=%async_computation | async-start | bytes 6356992 | tf_op jit(solution)/shard_map/all_to_all | solution.py:54
  12.1 8.9 %collective-permute-start = (bf16[256,2048]{1,0:T(8,128)(2,1)}, bf16[256,2048]{1,0:T(8,128)(2,1)}, u32[]{:S(2)}, u32[]{:S(2)}) collective-permute-start(bf16[256,2048]{1,0:T(8,128)(2,1)} %bitcast.11), channel_id=1, source_target_pairs={{0,1},{1,0},{2,3},{3,2},{4,5},{5,4},{6,7},{7,6},{8,9},{9,8},{10,11... | collective-permute-start | bytes 3145736 | tf_op jit(solution)/shard_map/ppermute | solution.py:464
  54.9 9.7 %copy-start = (bf16[16,776,128]{2,1,0:T(8,128)(2,1)}, bf16[16,776,128]{2,1,0:T(8,128)(2,1)S(1)}, u32[]{:S(2)}) copy-start(bf16[16,776,128]{2,1,0:T(8,128)(2,1)S(1)} %all-to-all-done.x_ref) | copy-start | bytes 9535492
  54.9 9.7 %collective-permute-start.1 = (bf16[16,776,128]{2,1,0:T(8,128)(2,1)S(1)}, bf16[16,776,128]{2,1,0:T(8,128)(2,1)}, u32[]{:S(2)}, u32[]{:S(2)}) collective-permute-start(bf16[16,776,128]{2,1,0:T(8,128)(2,1)S(1)} %all-to-all-done.x_ref), channel_id=1, source_target_pairs={{0,1},{1,0},{2,3},{3,2},{4,5},{5,4},{6,7},{7,6},{8,9},{9,8},{10,11... | collective-permute-start | bytes 9535496 | tf_op jit(solution)/shard_map/ppermute | solution.py:467
  54.9 26.7 %all-to-all-start.1 = ((bf16[16,256,128]{2,1,0:T(8,128)(2,1)}), bf16[16,256,128]{2,1,0:T(8,128)(2,1)}, u32[]{:S(2)}, u32[]{:S(2)}) async-start(bf16[16,256,128]{2,1,0:T(8,128)(2,1)} %grad_attn.1), calls=%async_computation.1 | async-start | bytes 2097152 | tf_op jit(solution)/shard_map/all_to_all | solution.py:54
  81.6 20.7 %all-to-all-start.2 = ((bf16[32,64,256]{2,1,0:T(8,128)(2,1)}), bf16[32,64,256]{2,1,0:T(8,128)(2,1)S(1)}, u32[]{:S(2)}, u32[]{:S(2)}) async-start(bf16[32,64,256]{2,1,0:T(8,128)(2,1)} %get-tuple-element.49), calls=%async_computation.2 | async-start | bytes 2097152 | tf_op jit(solution)/shard_map/all_to_all | solution.py:473
  102.3 1.0 copy-start.4
  103.3 4.4 %collective-permute-start.2 = (bf16[16,512,128]{2,1,0:T(8,128)(2,1)}, bf16[16,512,128]{2,1,0:T(8,128)(2,1)S(1)}, u32[]{:S(2)}, u32[]{:S(2)}) collective-permute-start(bf16[16,512,128]{2,1,0:T(8,128)(2,1)} %get-tuple-element.55), channel_id=1, source_target_pairs={{0,1},{1,0},{2,3},{3,2},{4,5},{5,4},{6,7},{7,6},{8,9},{9,8},{10,11... | collective-permute-start | bytes 6291464 | tf_op jit(solution)/shard_map/ppermute | solution.py:477
  103.6 22.0 %all-to-all-start.3 = ((bf16[16,256,128]{2,1,0:T(8,128)(2,1)}), bf16[16,256,128]{2,1,0:T(8,128)(2,1)S(1)}, u32[]{:S(2)}, u32[]{:S(2)}) async-start(bf16[16,256,128]{2,1,0:T(8,128)(2,1)} %get-tuple-element.66), calls=%async_computation.3 | async-start | bytes 2097152 | tf_op jit(solution)/shard_map/all_to_all | solution.py:54
  107.6 6.0 %copy-start.3 = (bf16[16,512,128]{2,1,0:T(8,128)(2,1)}, bf16[16,512,128]{2,1,0:T(8,128)(2,1)S(1)}, u32[]{:S(2)}) copy-start(bf16[16,512,128]{2,1,0:T(8,128)(2,1)S(1)} %collective-permute-done.2.got_ref) | copy-start | bytes 6291460
  113.6 15.8 %collective-permute-start.3 = (bf16[128,2048]{1,0:T(8,128)(2,1)}, bf16[128,2048]{1,0:T(8,128)(2,1)}, u32[]{:S(2)}, u32[]{:S(2)}) collective-permute-start(bf16[128,2048]{1,0:T(8,128)(2,1)} %get-tuple-element.64), channel_id=1, source_target_pairs={{0,32},{32,64},{64,96},{96,0},{1,33},{33,65},{65,97},{97,1},{2,34}... | collective-permute-start | bytes 1572872 | tf_op jit(solution)/shard_map/ppermute | solution.py:424
  115.2 14.2 %collective-permute-start.4 = (bf16[128,2048]{1,0:T(8,128)(2,1)}, bf16[128,2048]{1,0:T(8,128)(2,1)}, u32[]{:S(2)}, u32[]{:S(2)}) collective-permute-start(bf16[128,2048]{1,0:T(8,128)(2,1)} %get-tuple-element.65), channel_id=1, source_target_pairs={{0,96},{32,0},{64,32},{96,64},{1,97},{33,1},{65,33},{97,65},{2,98}... | collective-permute-start | bytes 1572872 | tf_op jit(solution)/shard_map/ppermute | solution.py:425
  125.6 8.3 %copy-start.2 = (bf16[16,256,128]{2,1,0:T(8,128)(2,1)}, bf16[16,256,128]{2,1,0:T(8,128)(2,1)S(1)}, u32[]{:S(2)}) copy-start(bf16[16,256,128]{2,1,0:T(8,128)(2,1)S(1)} %all-to-all-done.3.r_ref) | copy-start | bytes 3145732
  125.6 37.7 %all-to-all-start.4 = ((bf16[16,512,128]{2,1,0:T(8,128)(2,1)}), bf16[16,512,128]{2,1,0:T(8,128)(2,1)S(1)}, u32[]{:S(2)}, u32[]{:S(2)}) async-start(bf16[16,512,128]{2,1,0:T(8,128)(2,1)} %combine.1), calls=%async_computation.4 | async-start | bytes 4194304 | tf_op jit(solution)/shard_map/all_to_all | solution.py:54
  129.4 16.2 %copy-start.6 = (bf16[128,2048]{1,0:T(8,128)(2,1)S(1)}, bf16[128,2048]{1,0:T(8,128)(2,1)}, u32[]{:S(2)}) copy-start(bf16[128,2048]{1,0:T(8,128)(2,1)} %get-tuple-element.74) | copy-start | bytes 1572868
  129.4 17.3 %copy-start.5 = (bf16[128,2048]{1,0:T(8,128)(2,1)S(1)}, bf16[128,2048]{1,0:T(8,128)(2,1)}, u32[]{:S(2)}) copy-start(bf16[128,2048]{1,0:T(8,128)(2,1)} %get-tuple-element.78) | copy-start | bytes 1572868
  130.8 14.8 %collective-permute-start.5 = (bf16[128,2048]{1,0:T(8,128)(2,1)S(1)}, bf16[128,2048]{1,0:T(8,128)(2,1)S(1)}, u32[]{:S(2)}, u32[]{:S(2)}) collective-permute-start(bf16[128,2048]{1,0:T(8,128)(2,1)S(1)} %add_convert_fusion.3), channel_id=1, source_target_pairs={{0,32},{32,64},{64,96},{96,0},{1,33},{33,65},{65,97},{97,1},{2,34}... | collective-permute-start | bytes 1572872 | tf_op jit(solution)/shard_map/ppermute | solution.py:424
  133.9 12.8 %collective-permute-start.7 = (bf16[128,2048]{1,0:T(8,128)(2,1)S(1)}, bf16[128,2048]{1,0:T(8,128)(2,1)S(1)}, u32[]{:S(2)}, u32[]{:S(2)}) collective-permute-start(bf16[128,2048]{1,0:T(8,128)(2,1)S(1)} %add_convert_fusion.1), channel_id=1, source_target_pairs={{0,96},{32,0},{64,32},{96,64},{1,97},{33,1},{65,33},{97,65},{2,98}... | collective-permute-start | bytes 1572872 | tf_op jit(solution)/shard_map/ppermute | solution.py:425
  145.8 13.6 %collective-permute-start.6 = (bf16[128,2048]{1,0:T(8,128)(2,1)S(1)}, bf16[128,2048]{1,0:T(8,128)(2,1)S(1)}, u32[]{:S(2)}, u32[]{:S(2)}) collective-permute-start(bf16[128,2048]{1,0:T(8,128)(2,1)S(1)} %add_convert_fusion.2), channel_id=1, source_target_pairs={{0,32},{32,64},{64,96},{96,0},{1,33},{33,65},{65,97},{97,1},{2,34}... | collective-permute-start | bytes 1572872 | tf_op jit(solution)/shard_map/ppermute | solution.py:424
  146.8 13.0 %collective-permute-start.8 = (bf16[128,2048]{1,0:T(8,128)(2,1)S(1)}, bf16[128,2048]{1,0:T(8,128)(2,1)S(1)}, u32[]{:S(2)}, u32[]{:S(2)}) collective-permute-start(bf16[128,2048]{1,0:T(8,128)(2,1)S(1)} %add_convert_fusion), channel_id=1, source_target_pairs={{0,96},{32,0},{64,32},{96,64},{1,97},{33,1},{65,33},{97,65},{2,98}... | collective-permute-start | bytes 1572872 | tf_op jit(solution)/shard_map/ppermute | solution.py:425
  159.4 0.8 copy-start.7
  159.8 0.8 copy-start.8
  163.4 7.1 %copy-start.1 = (bf16[16,512,128]{2,1,0:T(8,128)(2,1)}, bf16[16,512,128]{2,1,0:T(8,128)(2,1)S(1)}, u32[]{:S(2)}) copy-start(bf16[16,512,128]{2,1,0:T(8,128)(2,1)S(1)} %all-to-all-done.4.r_ref) | copy-start | bytes 6291460
  163.4 18.7 %all-to-all-start.5 = ((bf16[16,16,2048]{2,1,0:T(8,128)(2,1)}), bf16[16,16,2048]{2,1,0:T(8,128)(2,1)S(1)}, u32[]{:S(2)}, u32[]{:S(2)}) async-start(bf16[16,16,2048]{2,1,0:T(8,128)(2,1)} %join.1), calls=%async_computation.5 | async-start | bytes 2097152 | tf_op jit(solution)/shard_map/all_to_all | solution.py:54

commit v11 on v10

--- a/solution.py
+++ b/solution.py
@@ -31,7 +31,7 @@
 
 UNROLL = 4
 GROUP = 4
-PACK = 8
+PACK = 16
 VMEM_LIMIT = 56 * 1024 * 1024
 
 

time: 185 us -> 185 us (level)
  transfers between devices with their start and end apart: 15 -> 15, of which waited for: 10 -> 10; matrix products, arithmetic and copies ran while one was open for 2% -> 2% of each run, Pallas kernels for 26% -> 27%
where the time goes in v11:
time: 185 us; the launch traced here: 184 us
  waiting for transfers between devices  79 us (43%)
  Pallas kernels  53.1 us (29%)
  starting transfers between devices  43.5 us (24%)
  other arithmetic  5.2 us (3%)
  local copies, waits for them, and re-layouts  1.96 us (1%)
    all_to_all x5, waiting for transfers between devices, exchange(): lax.all_to_all(x, 'seq', 0, 0, axis_index_groups=SAME_CORE, tiled=True)  54.3 us
    all_to_all x5, starting transfers between devices, exchange(): lax.all_to_all(x, 'seq', 0, 0, axis_index_groups=SAME_CORE, tiled=True)  28.6 us
    ppermute x3, waiting for transfers between devices, sum_over_docs(): a = lax.ppermute(a, 'dp', route_up)  19.1 us
    pallas_call x1, Pallas kernels, attention_backward(): pl.pallas_call(backward_body, out_shape=(jax.ShapeDtypeStruct((CHIPS, 2 *...  12.6 us
    pallas_call x1, Pallas kernels, attention_forward(): pl.pallas_call(forward_body, out_shape=(jax.ShapeDtypeStruct((2 * CHIPS,...  9.6 us
    pallas_call x1, Pallas kernels, grad_attn_by_head(): pl.pallas_call(grad_attn_body, out_shape=jax.ShapeDtypeStruct((HEADS, TOK...  8.78 us
    ppermute x3, starting transfers between devices, sum_over_docs(): b = lax.ppermute(b, 'dp', route_down)  6.91 us
    pallas_call x2, Pallas kernels, unpack(): pl.pallas_call(unpack_body, out_shape=(out,) * n, grid=(HEADS // PACK,),...  5.99 us
  transfers between devices with their start and end apart: 15, of which 10 were waited for; matrix products, arithmetic and copies ran while one was open for 2% of the time, Pallas kernels for 27%

profile of v11, /device:TPU:0, one launch (start us, length us, event | category | flops | bytes accessed | tf_op | source)
XLA Modules:
  0.0 183.6 jit_solution(1447785716423135662)
XLA Ops:
  0.6 4.1 %pack.1 = bf16[16,776,128]{2,1,0:T(8,128)(2,1)} custom-call(s32[2,4]{1,0:T(2,128)} %bitcast.20, bf16[256,2048]{1,0:T(8,128)(2,1)} %bitcast.17, bf16[256,2048]{1,0:T(8,128)(2,1)} %bitcast.18, bf16[256,2048]{1,0:T(8,128)(2,1)} %bitcast.19), custom_call_target="tpu_custom_call" | custom-call | tf_op jit(solution)/shard_map/pack/pallas_call | solution.py:75
  4.7 8.1 %all-to-all-start = ((bf16[16,776,128]{2,1,0:T(8,128)(2,1)}), bf16[16,776,128]{2,1,0:T(8,128)(2,1)S(1)}, u32[]{:S(2)}, u32[]{:S(2)}) async-start(bf16[16,776,128]{2,1,0:T(8,128)(2,1)} %pack.1), calls=%async_computation | async-start | bytes 6356992 | tf_op jit(solution)/shard_map/all_to_all | solution.py:54
  12.9 0.1 collective-permute-start
  12.9 8.8 %grad_attn.1 = bf16[16,256,128]{2,1,0:T(8,128)(2,1)} custom-call(bf16[256,2048]{1,0:T(8,128)(2,1)} %bitcast.12, bf16[2048,2048]{1,0:T(8,128)(2,1)} %w_ref.1), custom_call_target="tpu_custom_call" | custom-call | flops 2147483648 | bytes 10485760 | tf_op jit(solution)/shard_map/grad_attn/pallas_call | solution.py:114
  21.7 33.9 %all-to-all-done.x_ref = bf16[16,776,128]{2,1,0:T(8,128)(2,1)S(1)} async-done(((bf16[16,776,128]{2,1,0:T(8,128)(2,1)}), bf16[16,776,128]{2,1,0:T(8,128)(2,1)S(1)}, u32[]{:S(2)}, u32[]{:S(2)}) %all-to-all-start) | async-done | bytes 3178528 | tf_op jit(solution)/shard_map/all_to_all | solution.py:54
  55.7 0.0 collective-permute-start.1
  55.7 8.1 %all-to-all-start.1 = ((bf16[16,256,128]{2,1,0:T(8,128)(2,1)}), bf16[16,256,128]{2,1,0:T(8,128)(2,1)}, u32[]{:S(2)}, u32[]{:S(2)}) async-start(bf16[16,256,128]{2,1,0:T(8,128)(2,1)} %grad_attn.1), calls=%async_computation.1 | async-start | bytes 2097152 | tf_op jit(solution)/shard_map/all_to_all | solution.py:54
  63.8 0.1 iota_add_fusion
  63.9 0.1 add.62
  64.0 0.6 pad_add_fusion.place
  64.7 0.1 reshape.47
  64.7 0.7 add_select_fusion.table
  65.4 9.6 %attn_fwd.1 = (bf16[32,64,256]{2,1,0:T(8,128)(2,1)}, bf16[32,640,128]{2,1,0:T(8,128)(2,1)}) custom-call(s32[32,4]{1,0:T(8,128)} %add_select_fusion.table, bf16[16,776,128]{2,1,0:T(8,128)(2,1)} %copy-done, bf16[16,776,128]{2,1,0:T(8,128)(2,1)} %collective-permute-done.1.y_ref), custom_call_target="tpu_custom_call" | custom-call | flops 1342177280 | bytes 12582912 | tf_op jit(solution)/shard_map/attn_fwd/pallas_call | solution.py:220
  75.0 7.3 %all-to-all-done.1.g_ref = bf16[16,256,128]{2,1,0:T(8,128)(2,1)} async-done(((bf16[16,256,128]{2,1,0:T(8,128)(2,1)}), bf16[16,256,128]{2,1,0:T(8,128)(2,1)}, u32[]{:S(2)}, u32[]{:S(2)}) %all-to-all-start.1) | async-done | bytes 1048608 | tf_op jit(solution)/shard_map/all_to_all | solution.py:54
  82.3 4.1 %all-to-all-start.2 = ((bf16[32,64,256]{2,1,0:T(8,128)(2,1)}), bf16[32,64,256]{2,1,0:T(8,128)(2,1)S(1)}, u32[]{:S(2)}, u32[]{:S(2)}) async-start(bf16[32,64,256]{2,1,0:T(8,128)(2,1)} %get-tuple-element.49), calls=%async_computation.2 | async-start | bytes 2097152 | tf_op jit(solution)/shard_map/all_to_all | solution.py:473
  86.5 12.6 %attn_bwd.1 = (bf16[16,512,128]{2,1,0:T(8,128)(2,1)}, bf16[16,512,128]{2,1,0:T(8,128)(2,1)}, bf16[16,256,128]{2,1,0:T(8,128)(2,1)}) custom-call(s32[32,4]{1,0:T(8,128)} %add_select_fusion.table, bf16[16,776,128]{2,1,0:T(8,128)(2,1)} %copy-done, bf16[16,776,128]{2,1,0:T(8,128)(2,1)} %collective-permute-done.1.y_ref, ...), custom_call_target="tpu_custom_call" | custom-call | flops 2684354560 | bytes 17825792 | tf_op jit(solution)/shard_map/attn_bwd/pallas_call | solution.py:324
  99.1 4.0 %all-to-all-done.2 = bf16[32,64,256]{2,1,0:T(8,128)(2,1)S(1)} async-done(((bf16[32,64,256]{2,1,0:T(8,128)(2,1)}), bf16[32,64,256]{2,1,0:T(8,128)(2,1)S(1)}, u32[]{:S(2)}, u32[]{:S(2)}) %all-to-all-start.2) | async-done | bytes 1048608 | tf_op jit(solution)/shard_map/all_to_all | solution.py:473
  103.1 1.0 copy-done.4
  104.0 0.4 collective-permute-start.2
  104.4 3.7 %all-to-all-start.3 = ((bf16[16,256,128]{2,1,0:T(8,128)(2,1)}), bf16[16,256,128]{2,1,0:T(8,128)(2,1)S(1)}, u32[]{:S(2)}, u32[]{:S(2)}) async-start(bf16[16,256,128]{2,1,0:T(8,128)(2,1)} %get-tuple-element.66), calls=%async_computation.3 | async-start | bytes 2097152 | tf_op jit(solution)/shard_map/all_to_all | solution.py:54
  108.1 0.3 collective-permute-done.2.got_ref
  108.4 5.9 %weight_partial.1 = (bf16[128,2048]{1,0:T(8,128)(2,1)}, bf16[128,2048]{1,0:T(8,128)(2,1)}, bf16[128,2048]{1,0:T(8,128)(2,1)}, bf16[128,2048]{1,0:T(8,128)(2,1)},...) custom-call(s32[2]{0:T(128)} %pad_add_fusion.place, ...), custom_call_target="tpu_custom_call" | custom-call | flops 2147483648 | bytes 8388608 | tf_op jit(solution)/shard_map/weight_partial/pallas_call | solution.py:395
  114.4 1.6 collective-permute-start.3
  116.0 1.7 collective-permute-start.4
  117.7 3.4 %combine.1 = bf16[16,512,128]{2,1,0:T(8,128)(2,1)} custom-call(bf16[16,512,128]{2,1,0:T(8,128)(2,1)} %get-tuple-element.67.own_ref, bf16[16,512,128]{2,1,0:T(8,128)(2,1)} %copy-done.3), custom_call_target="tpu_custom_call" | custom-call | flops 1048576 | bytes 6291456 | tf_op jit(solution)/shard_map/combine/pallas_call | solution.py:359
  121.1 5.3 %all-to-all-done.3.r_ref = bf16[16,256,128]{2,1,0:T(8,128)(2,1)S(1)} async-done(((bf16[16,256,128]{2,1,0:T(8,128)(2,1)}), bf16[16,256,128]{2,1,0:T(8,128)(2,1)S(1)}, u32[]{:S(2)}, u32[]{:S(2)}) %all-to-all-start.3) | async-done | bytes 1048608 | tf_op jit(solution)/shard_map/all_to_all | solution.py:54
  126.4 3.7 %all-to-all-start.4 = ((bf16[16,512,128]{2,1,0:T(8,128)(2,1)}), bf16[16,512,128]{2,1,0:T(8,128)(2,1)S(1)}, u32[]{:S(2)}, u32[]{:S(2)}) async-start(bf16[16,512,128]{2,1,0:T(8,128)(2,1)} %combine.1), calls=%async_computation.4 | async-start | bytes 4194304 | tf_op jit(solution)/shard_map/all_to_all | solution.py:54
  130.2 0.0 collective-permute-done.3
  130.2 1.4 add_convert_fusion.3
  131.6 1.8 collective-permute-start.5
  133.4 1.3 add_convert_fusion.1
  134.7 1.8 collective-permute-start.7
  136.5 9.9 %collective-permute-done.5 = bf16[128,2048]{1,0:T(8,128)(2,1)S(1)} collective-permute-done((bf16[128,2048]{1,0:T(8,128)(2,1)S(1)}, bf16[128,2048]{1,0:T(8,128)(2,1)S(1)}, u32[]{:S(2)}, u32[]{:S(2)}) %collective-permute-start.5) | collective-permute-done | bytes 524320 | tf_op jit(solution)/shard_map/ppermute | solution.py:424
  146.4 0.1 add_convert_fusion.2
  146.5 0.1 collective-permute-start.6
  146.6 0.9 collective-permute-done.7
  147.5 0.1 add_convert_fusion
  147.6 3.3 %collective-permute-start.8 = (bf16[128,2048]{1,0:T(8,128)(2,1)S(1)}, bf16[128,2048]{1,0:T(8,128)(2,1)S(1)}, u32[]{:S(2)}, u32[]{:S(2)}) collective-permute-start(bf16[128,2048]{1,0:T(8,128)(2,1)S(1)} %add_convert_fusion), channel_id=1, source_target_pairs={{0,96},{32,0},{64,32},{96,64},{1,97},{33,1},{65,33},{97,65},{2,98}... | collective-permute-start | bytes 1572872 | tf_op jit(solution)/shard_map/ppermute | solution.py:425
  151.0 9.2 %collective-permute-done.6.a_ref = bf16[128,2048]{1,0:T(8,128)(2,1)S(1)} collective-permute-done((bf16[128,2048]{1,0:T(8,128)(2,1)S(1)}, bf16[128,2048]{1,0:T(8,128)(2,1)S(1)}, u32[]{:S(2)}, u32[]{:S(2)}) %collective-permute-start.6) | collective-permute-done | bytes 524320 | tf_op jit(solution)/shard_map/ppermute | solution.py:424
  160.2 0.4 collective-permute-done.8.b_ref
  160.6 0.4 copy-done.7
  161.0 0.4 copy-done.8
  161.4 2.7 %join.1 = bf16[16,16,2048]{2,1,0:T(8,128)(2,1)} custom-call(bf16[128,2048]{1,0:T(8,128)(2,1)} %copy-done.7, bf16[128,2048]{1,0:T(8,128)(2,1)} %get-tuple-element.75.own_a_ref, bf16[128,2048]{1,0:T(8,128)(2,1)} %copy-done.8, bf16[128,2048]{1,0:T(8,128)(2,1)} %get-tuple-element.79.own_b_ref), custom_call_target="tpu_custom_call" | custom-call | tf_op jit(solution)/shard_map/join/pallas_call | solution.py:441
  164.1 5.0 %all-to-all-start.5 = ((bf16[16,16,2048]{2,1,0:T(8,128)(2,1)}), bf16[16,16,2048]{2,1,0:T(8,128)(2,1)S(1)}, u32[]{:S(2)}, u32[]{:S(2)}) async-start(bf16[16,16,2048]{2,1,0:T(8,128)(2,1)} %join.1), calls=%async_computation.5 | async-start | bytes 2097152 | tf_op jit(solution)/shard_map/all_to_all | solution.py:54
  169.1 2.5 %unpack.2 = bf16[256,2048]{1,0:T(8,128)(2,1)} custom-call(bf16[16,256,128]{2,1,0:T(8,128)(2,1)} %copy-done.2), custom_call_target="tpu_custom_call" | custom-call | bytes 2097152 | tf_op jit(solution)/shard_map/unpack/pallas_call | solution.py:95
  171.6 3.5 %unpack.3 = (bf16[256,2048]{1,0:T(8,128)(2,1)}, bf16[256,2048]{1,0:T(8,128)(2,1)}) custom-call(bf16[16,512,128]{2,1,0:T(8,128)(2,1)} %copy-done.1), custom_call_target="tpu_custom_call" | custom-call | bytes 4194304 | tf_op jit(solution)/shard_map/unpack/pallas_call | solution.py:95
  175.1 7.7 %all-to-all-done.5 = bf16[16,16,2048]{2,1,0:T(8,128)(2,1)S(1)} async-done(((bf16[16,16,2048]{2,1,0:T(8,128)(2,1)}), bf16[16,16,2048]{2,1,0:T(8,128)(2,1)S(1)}, u32[]{:S(2)}, u32[]{:S(2)}) %all-to-all-start.5) | async-done | bytes 1048608 | tf_op jit(solution)/shard_map/all_to_all | solution.py:54
  182.8 0.8 convert_reduce_fusion
  (21 shorter events, 0.1 us)
Async XLA Ops:
  4.7 51.0 %all-to-all-start = ((bf16[16,776,128]{2,1,0:T(8,128)(2,1)}), bf16[16,776,128]{2,1,0:T(8,128)(2,1)S(1)}, u32[]{:S(2)}, u32[]{:S(2)}) async-start(bf16[16,776,128]{2,1,0:T(8,128)(2,1)} %pack.1), calls=%async_computation | async-start | bytes 6356992 | tf_op jit(solution)/shard_map/all_to_all | solution.py:54
  12.9 8.9 %collective-permute-start = (bf16[256,2048]{1,0:T(8,128)(2,1)}, bf16[256,2048]{1,0:T(8,128)(2,1)}, u32[]{:S(2)}, u32[]{:S(2)}) collective-permute-start(bf16[256,2048]{1,0:T(8,128)(2,1)} %bitcast.11), channel_id=1, source_target_pairs={{0,1},{1,0},{2,3},{3,2},{4,5},{5,4},{6,7},{7,6},{8,9},{9,8},{10,11... | collective-permute-start | bytes 3145736 | tf_op jit(solution)/shard_map/ppermute | solution.py:464
  55.7 9.7 %copy-start = (bf16[16,776,128]{2,1,0:T(8,128)(2,1)}, bf16[16,776,128]{2,1,0:T(8,128)(2,1)S(1)}, u32[]{:S(2)}) copy-start(bf16[16,776,128]{2,1,0:T(8,128)(2,1)S(1)} %all-to-all-done.x_ref) | copy-start | bytes 9535492
  55.7 9.7 %collective-permute-start.1 = (bf16[16,776,128]{2,1,0:T(8,128)(2,1)S(1)}, bf16[16,776,128]{2,1,0:T(8,128)(2,1)}, u32[]{:S(2)}, u32[]{:S(2)}) collective-permute-start(bf16[16,776,128]{2,1,0:T(8,128)(2,1)S(1)} %all-to-all-done.x_ref), channel_id=1, source_target_pairs={{0,1},{1,0},{2,3},{3,2},{4,5},{5,4},{6,7},{7,6},{8,9},{9,8},{10,11... | collective-permute-start | bytes 9535496 | tf_op jit(solution)/shard_map/ppermute | solution.py:467
  55.7 26.7 %all-to-all-start.1 = ((bf16[16,256,128]{2,1,0:T(8,128)(2,1)}), bf16[16,256,128]{2,1,0:T(8,128)(2,1)}, u32[]{:S(2)}, u32[]{:S(2)}) async-start(bf16[16,256,128]{2,1,0:T(8,128)(2,1)} %grad_attn.1), calls=%async_computation.1 | async-start | bytes 2097152 | tf_op jit(solution)/shard_map/all_to_all | solution.py:54
  82.3 20.7 %all-to-all-start.2 = ((bf16[32,64,256]{2,1,0:T(8,128)(2,1)}), bf16[32,64,256]{2,1,0:T(8,128)(2,1)S(1)}, u32[]{:S(2)}, u32[]{:S(2)}) async-start(bf16[32,64,256]{2,1,0:T(8,128)(2,1)} %get-tuple-element.49), calls=%async_computation.2 | async-start | bytes 2097152 | tf_op jit(solution)/shard_map/all_to_all | solution.py:473
  103.1 1.0 copy-start.4
  104.0 4.4 %collective-permute-start.2 = (bf16[16,512,128]{2,1,0:T(8,128)(2,1)}, bf16[16,512,128]{2,1,0:T(8,128)(2,1)S(1)}, u32[]{:S(2)}, u32[]{:S(2)}) collective-permute-start(bf16[16,512,128]{2,1,0:T(8,128)(2,1)} %get-tuple-element.55), channel_id=1, source_target_pairs={{0,1},{1,0},{2,3},{3,2},{4,5},{5,4},{6,7},{7,6},{8,9},{9,8},{10,11... | collective-permute-start | bytes 6291464 | tf_op jit(solution)/shard_map/ppermute | solution.py:477
  104.4 22.0 %all-to-all-start.3 = ((bf16[16,256,128]{2,1,0:T(8,128)(2,1)}), bf16[16,256,128]{2,1,0:T(8,128)(2,1)S(1)}, u32[]{:S(2)}, u32[]{:S(2)}) async-start(bf16[16,256,128]{2,1,0:T(8,128)(2,1)} %get-tuple-element.66), calls=%async_computation.3 | async-start | bytes 2097152 | tf_op jit(solution)/shard_map/all_to_all | solution.py:54
  108.4 6.0 %copy-start.3 = (bf16[16,512,128]{2,1,0:T(8,128)(2,1)}, bf16[16,512,128]{2,1,0:T(8,128)(2,1)S(1)}, u32[]{:S(2)}) copy-start(bf16[16,512,128]{2,1,0:T(8,128)(2,1)S(1)} %collective-permute-done.2.got_ref) | copy-start | bytes 6291460
  114.4 15.8 %collective-permute-start.3 = (bf16[128,2048]{1,0:T(8,128)(2,1)}, bf16[128,2048]{1,0:T(8,128)(2,1)}, u32[]{:S(2)}, u32[]{:S(2)}) collective-permute-start(bf16[128,2048]{1,0:T(8,128)(2,1)} %get-tuple-element.64), channel_id=1, source_target_pairs={{0,32},{32,64},{64,96},{96,0},{1,33},{33,65},{65,97},{97,1},{2,34}... | collective-permute-start | bytes 1572872 | tf_op jit(solution)/shard_map/ppermute | solution.py:424
  116.0 14.2 %collective-permute-start.4 = (bf16[128,2048]{1,0:T(8,128)(2,1)}, bf16[128,2048]{1,0:T(8,128)(2,1)}, u32[]{:S(2)}, u32[]{:S(2)}) collective-permute-start(bf16[128,2048]{1,0:T(8,128)(2,1)} %get-tuple-element.65), channel_id=1, source_target_pairs={{0,96},{32,0},{64,32},{96,64},{1,97},{33,1},{65,33},{97,65},{2,98}... | collective-permute-start | bytes 1572872 | tf_op jit(solution)/shard_map/ppermute | solution.py:425
  126.4 8.3 %copy-start.2 = (bf16[16,256,128]{2,1,0:T(8,128)(2,1)}, bf16[16,256,128]{2,1,0:T(8,128)(2,1)S(1)}, u32[]{:S(2)}) copy-start(bf16[16,256,128]{2,1,0:T(8,128)(2,1)S(1)} %all-to-all-done.3.r_ref) | copy-start | bytes 3145732
  126.4 37.7 %all-to-all-start.4 = ((bf16[16,512,128]{2,1,0:T(8,128)(2,1)}), bf16[16,512,128]{2,1,0:T(8,128)(2,1)S(1)}, u32[]{:S(2)}, u32[]{:S(2)}) async-start(bf16[16,512,128]{2,1,0:T(8,128)(2,1)} %combine.1), calls=%async_computation.4 | async-start | bytes 4194304 | tf_op jit(solution)/shard_map/all_to_all | solution.py:54
  130.1 16.2 %copy-start.6 = (bf16[128,2048]{1,0:T(8,128)(2,1)S(1)}, bf16[128,2048]{1,0:T(8,128)(2,1)}, u32[]{:S(2)}) copy-start(bf16[128,2048]{1,0:T(8,128)(2,1)} %get-tuple-element.74) | copy-start | bytes 1572868
  130.2 17.3 %copy-start.5 = (bf16[128,2048]{1,0:T(8,128)(2,1)S(1)}, bf16[128,2048]{1,0:T(8,128)(2,1)}, u32[]{:S(2)}) copy-start(bf16[128,2048]{1,0:T(8,128)(2,1)} %get-tuple-element.78) | copy-start | bytes 1572868
  131.6 14.8 %collective-permute-start.5 = (bf16[128,2048]{1,0:T(8,128)(2,1)S(1)}, bf16[128,2048]{1,0:T(8,128)(2,1)S(1)}, u32[]{:S(2)}, u32[]{:S(2)}) collective-permute-start(bf16[128,2048]{1,0:T(8,128)(2,1)S(1)} %add_convert_fusion.3), channel_id=1, source_target_pairs={{0,32},{32,64},{64,96},{96,0},{1,33},{33,65},{65,97},{97,1},{2,34}... | collective-permute-start | bytes 1572872 | tf_op jit(solution)/shard_map/ppermute | solution.py:424
  134.7 12.8 %collective-permute-start.7 = (bf16[128,2048]{1,0:T(8,128)(2,1)S(1)}, bf16[128,2048]{1,0:T(8,128)(2,1)S(1)}, u32[]{:S(2)}, u32[]{:S(2)}) collective-permute-start(bf16[128,2048]{1,0:T(8,128)(2,1)S(1)} %add_convert_fusion.1), channel_id=1, source_target_pairs={{0,96},{32,0},{64,32},{96,64},{1,97},{33,1},{65,33},{97,65},{2,98}... | collective-permute-start | bytes 1572872 | tf_op jit(solution)/shard_map/ppermute | solution.py:425
  146.5 13.6 %collective-permute-start.6 = (bf16[128,2048]{1,0:T(8,128)(2,1)S(1)}, bf16[128,2048]{1,0:T(8,128)(2,1)S(1)}, u32[]{:S(2)}, u32[]{:S(2)}) collective-permute-start(bf16[128,2048]{1,0:T(8,128)(2,1)S(1)} %add_convert_fusion.2), channel_id=1, source_target_pairs={{0,32},{32,64},{64,96},{96,0},{1,33},{33,65},{65,97},{97,1},{2,34}... | collective-permute-start | bytes 1572872 | tf_op jit(solution)/shard_map/ppermute | solution.py:424
  147.6 13.0 %collective-permute-start.8 = (bf16[128,2048]{1,0:T(8,128)(2,1)S(1)}, bf16[128,2048]{1,0:T(8,128)(2,1)S(1)}, u32[]{:S(2)}, u32[]{:S(2)}) collective-permute-start(bf16[128,2048]{1,0:T(8,128)(2,1)S(1)} %add_convert_fusion), channel_id=1, source_target_pairs={{0,96},{32,0},{64,32},{96,64},{1,97},{33,1},{65,33},{97,65},{2,98}... | collective-permute-start | bytes 1572872 | tf_op jit(solution)/shard_map/ppermute | solution.py:425
  160.2 0.8 copy-start.7
  160.6 0.8 copy-start.8
  164.1 7.5 %copy-start.1 = (bf16[16,512,128]{2,1,0:T(8,128)(2,1)}, bf16[16,512,128]{2,1,0:T(8,128)(2,1)S(1)}, u32[]{:S(2)}) copy-start(bf16[16,512,128]{2,1,0:T(8,128)(2,1)S(1)} %all-to-all-done.4.r_ref) | copy-start | bytes 6291460
  164.1 18.7 %all-to-all-start.5 = ((bf16[16,16,2048]{2,1,0:T(8,128)(2,1)}), bf16[16,16,2048]{2,1,0:T(8,128)(2,1)S(1)}, u32[]{:S(2)}, u32[]{:S(2)}) async-start(bf16[16,16,2048]{2,1,0:T(8,128)(2,1)} %join.1), calls=%async_computation.5 | async-start | bytes 2097152 | tf_op jit(solution)/shard_map/all_to_all | solution.py:54
